TPU v7x, 128 devices: a whole 4x4x4 slice. The times are simulated.
128 devices in a mesh: sub: 8 (over x, core), beam: 8 (over y_hi, z), comp: 2 (over y_lo).
Axes of the slice: x: 4, y: 4 (y_hi: 2, y_lo: 2; y = y_hi * 2 + y_lo), z: 4, core: 2. Of those that a mesh axis runs over, the one named last changes fastest.
Arguments:
- raw_pulses: bfloat16 [16384, 2, 16384], P(('sub', 'beam', 'comp')), may hold values from -6 to 6
- range_filter: float32 [2, 16384], replicated, may hold values from -4 to 4
- steer_angle: float32 [128, 16384], P(None, ('sub', 'beam', 'comp')), may hold values from -3.140625 to 3.140625
- band_offsets: int32 [2, 1792], P(None, ('beam', 'comp')), may hold values from -4 to 28, as said below
- band_weights: float32 [2, 1792, 8], P(None, ('beam', 'comp')), may hold values from -1.5 to 1.5
- beam_delay: float32 [2, 1792], P(None, ('beam', 'comp')), may hold values from -3 to 3
Outputs:
- scene_beams: float32 [1024, 2, 16384], P(('beam', 'comp'), None, 'sub')
Inputs may be any that keep to these rules, and one draw needn't show every extreme that they name: `band_offsets`: for new beam u of a merge level l and a block (0 <= u < 2 * 8 2^l), each side's offset is u // 2 - 8 // 2 + 1 or one less; the first beam of every level and block takes the lesser value, the last the greater.
All inputs are finite; a program needn't handle non-finite values.
Results may differ from a plain program's by a relative error of at most 0.0059.
Values may be sent and summed in bfloat16 or wider, within the bound.
No kernel may reach another device: no remote copies, remote signals or barrier semaphores. Data moves between devices by JAX's collectives and lax.ppermute only.
A program may use at most 128 MiB of HBM per device.

v0:
```python
import functools
import math

import jax
import jax.numpy as jnp
import ml_dtypes
import numpy as np
from jax import lax
from jax.experimental import pallas as pl
from jax.experimental.pallas import tpu as pltpu
from jax.sharding import Mesh
from jax.sharding import PartitionSpec as P

NR = 16384
RADIX = 128
NB0 = 8
BAND = 8
PSUB = 2048
RING = 4
HALF = NR // 2
TILE = 2048
SLAB = NR // 8
COLS = 512
SIDE = 208
BEAM_COMP = ("y_hi", "z", "y_lo")
SUB_BEAM_COMP = ("sub", "y_hi", "z", "y_lo")
Y = ("y_hi", "y_lo")
Z = "z"
BF = jnp.bfloat16
F4 = jnp.float32
ORDER = (
    (2, 0), (2, 1), (1, 2), (1, 3),
    (2, 2), (2, 3), (3, 0), (3, 1),
    (1, 0), (1, 1),
    (3, 2), (3, 3),
    (0, 0), (0, 1), (0, 2), (0, 3),
)
PARTS = (64, 64, 32, 32, 64)


def params(mebibytes):
    return pltpu.CompilerParams(vmem_limit_bytes=mebibytes << 20)


def real_form_transposed():
    index = np.arange(RADIX)
    angle = (index[:, None] * index[None, :] % RADIX) * (2.0 * math.pi / RADIX)
    cos_part, sin_part = np.cos(angle), -np.sin(angle)
    upper = np.concatenate([cos_part, sin_part], 1)
    lower = np.concatenate([-sin_part, cos_part], 1)
    return np.concatenate([upper, lower], 0).T.astype(ml_dtypes.bfloat16)


def twiddle():
    index = np.arange(RADIX)
    angle = (index[:, None] * index[None, :] % NR) * (2.0 * math.pi / NR)
    return np.stack([np.cos(angle), -np.sin(angle)]).astype(np.float32)


def ring_send(x, axis, step):
    return lax.ppermute(x, axis, [(k, (k + step) % RING) for k in range(RING)])


def beam_kernel(order_ref, angle_ref, raw_ref, *rest):
    outs, weights = rest[:-1], rest[-1]

    @pl.when(pl.program_id(0) == 0)
    def _():
        rows = lax.broadcasted_iota(jnp.int32, (128, 256), 0)
        cols = lax.broadcasted_iota(jnp.int32, (128, 256), 1)
        spread = jnp.where(cols // 2 == rows, 1.0, 0.0).astype(F4)
        angle = jnp.dot(
            angle_ref[...], spread, precision=lax.Precision.HIGHEST, preferred_element_type=F4
        )
        factor = float(PSUB) ** -0.5
        cosine = jnp.cos(angle) * factor
        sine = jnp.sin(angle) * factor
        even = cols % 2 == 0
        weights[0] = jnp.where(even, cosine, -sine)
        weights[1] = jnp.where(even, sine, cosine)

    picked = []
    for k in range(16):
        first = pl.multiple_of(order_ref[k] * NB0, NB0)
        picked.append(weights[0, pl.ds(first, NB0), :])
        picked.append(weights[1, pl.ds(first, NB0), :])
    matrix = jnp.concatenate(picked, 0).astype(BF)
    raw = raw_ref[...].reshape(256, raw_ref.shape[2])
    total = jnp.dot(matrix, raw, preferred_element_type=F4).astype(BF)
    start = 0
    for out in outs:
        size = out.shape[0]
        out[...] = total[start : start + size]
        start += size


def beam_sums(order, angles, raw, half):
    steps = HALF // TILE
    return pl.pallas_call(
        beam_kernel,
        grid_spec=pltpu.PrefetchScalarGridSpec(
            num_scalar_prefetch=1,
            grid=(steps,),
            in_specs=[
                pl.BlockSpec((128, 128), lambda i, o: (0, 0)),
                pl.BlockSpec((128, 2, TILE), lambda i, o: (0, 0, i + half * steps)),
            ],
            out_specs=[pl.BlockSpec((n, TILE), lambda i, o: (0, i)) for n in PARTS],
            scratch_shapes=[pltpu.VMEM((2, 128, 256), F4)],
        ),
        out_shape=[jax.ShapeDtypeStruct((n, HALF), BF) for n in PARTS],
        compiler_params=params(40),
        name="beam_sums",
    )(order, angles, raw)


def relay_kernel(q1, q3, p1, m1, s, t):
    s[...] = (q1[...].astype(F4) + p1[...].astype(F4)).astype(BF)
    t[...] = (q3[...].astype(F4) + m1[...].astype(F4)).astype(BF)


def relay_sums(q1, q3, p1, m1, tile):
    rows, cols = q1.shape
    spec = pl.BlockSpec((rows, tile), lambda i: (0, i))
    return pl.pallas_call(
        relay_kernel,
        grid=(cols // tile,),
        in_specs=[spec] * 4,
        out_specs=[spec] * 2,
        out_shape=[jax.ShapeDtypeStruct((rows, cols), BF)] * 2,
        name="relay_sums",
    )(q1, q3, p1, m1)


def middle_kernel(own, p1, m1, p2, m2, plus, minus, q1, q3, keep):
    low = own[:32].astype(F4) + m1[...].astype(F4) + p2[...].astype(F4)
    high = own[32:].astype(F4) + p1[...].astype(F4) + m2[...].astype(F4)
    keep[...] = low[:16]
    q1[...] = low[16:24].astype(BF)
    plus[...] = jnp.concatenate([high[:8], low[24:]], 0).astype(BF)
    minus[...] = jnp.concatenate([high[8:16], high[16:24]], 0).astype(BF)
    q3[...] = high[24:].astype(BF)


def middle_sums(own, p1, m1, p2, m2):
    tile = 2048
    outs = ((16, BF), (16, BF), (8, BF), (8, BF), (16, F4))
    received = pl.BlockSpec((32, tile), lambda i: (1, i))
    return pl.pallas_call(
        middle_kernel,
        grid=(HALF // tile,),
        in_specs=[pl.BlockSpec((64, tile), lambda i: (0, i)), received, received]
        + [pl.BlockSpec((32, tile), lambda i: (0, i))] * 2,
        out_specs=[pl.BlockSpec((n, tile), lambda i: (0, i)) for n, _ in outs],
        out_shape=[jax.ShapeDtypeStruct((n, HALF), d) for n, d in outs],
        name="middle_sums",
    )(own, p1, m1, p2, m2)


def compress_kernel(*refs):
    ins, (form_ref, turn_ref, filter_ref, out, lines, bins) = refs[:10], refs[10:]
    for half in range(2):
        keep, p3, m3, p4, m4 = ins[5 * half : 5 * half + 5]
        sums = (
            keep[:8] + m3[...].astype(F4)[8:] + p4[...].astype(F4),
            keep[8:] + p3[...].astype(F4)[8:] + m4[...].astype(F4),
        )
        for part in range(2):
            for k in range(64):
                row = (half * 64 + k) * 8
                lines[part, row : row + 8, :] = sums[part][:, k * 128 : (k + 1) * 128]
    form = form_ref[...]
    cos_part, sin_part = turn_ref[0], turn_ref[1]
    scale = NR ** (-0.5)
    real_filter, imag_filter = filter_ref[0] * scale, filter_ref[1] * scale
    for beam in range(NB0):
        picked = pl.ds(beam, 128, stride=8)
        data = jnp.concatenate([lines[0, picked, :], lines[1, picked, :]], 0)
        upper = data.astype(BF)
        lower = (data - upper.astype(F4)).astype(BF)
        one = jnp.dot(form, jnp.concatenate([upper, lower], 1), preferred_element_type=F4)
        one = one[:, :128] + one[:, 128:]
        real_in, imag_in = one[:128], one[128:]
        turned = jnp.concatenate(
            [real_in * cos_part - imag_in * sin_part, real_in * sin_part + imag_in * cos_part], 1
        )
        upper = turned.astype(BF)
        lower = (turned - upper.astype(F4)).astype(BF)
        two = lax.dot_general(
            form,
            jnp.concatenate([upper, lower], 0),
            (((1,), (1,)), ((), ())),
            preferred_element_type=F4,
        )
        two = two[:, :128] + two[:, 128:]
        real_in, imag_in = two[:128], two[128:]
        bins[0, picked, :] = real_in * real_filter - imag_in * imag_filter
        bins[1, picked, :] = real_in * imag_filter + imag_in * real_filter
    for slab in range(8):
        for k in range(16):
            row = (slab * 16 + k) * 8
            both = jnp.concatenate([bins[0, row : row + 8, :], bins[1, row : row + 8, :]], 0)
            out[slab, :, k * 128 : (k + 1) * 128] = both.astype(BF)


def compressed_beams(pieces, range_filter):
    return pl.pallas_call(
        compress_kernel,
        out_shape=jax.ShapeDtypeStruct((8, 16, SLAB), BF),
        scratch_shapes=[pltpu.VMEM((2, 1024, 128), F4), pltpu.VMEM((2, 1024, 128), F4)],
        compiler_params=params(40),
        name="compressed_beams",
    )(
        *pieces,
        jnp.asarray(real_form_transposed()),
        jnp.asarray(twiddle()),
        range_filter.reshape(2, 128, 128),
    )


def table_kernel(start_ref, table_ref, matrix, near_a, near_b, far_cos, far_sin):
    rows = table_ref.shape[0]
    lane = lax.broadcasted_iota(jnp.int32, (rows, 128), 1)
    row = lax.broadcasted_iota(jnp.int32, (rows, 128), 0) % SIDE
    lane_f = lane.astype(F4)
    table = table_ref[...]
    offset = table[:, 0:1]
    total = jnp.zeros((rows, 128), F4)
    for tap in range(BAND):
        total = total + jnp.where(lane_f == offset + float(tap), table[:, tap + 1 : tap + 2], 0.0)
    matrix[...] = total
    delay = table[:, 9:10]
    step = delay * (lane_f * (1.0 / NR))
    far_cos[...] = jnp.cos(step)
    far_sin[...] = jnp.sin(step)
    first = start_ref[0].astype(F4)
    base = delay * (1.0 + (first + lane_f * 128.0) * (1.0 / NR))
    cosine, sine = jnp.cos(base), jnp.sin(base)
    odd = (row >= 80) & (row % 2 == 1)
    value_a = jnp.where(odd, sine, cosine)
    value_b = jnp.where(odd, cosine, -sine)
    for tile in range(SLAB // COLS):
        lanes = slice(tile * 4, tile * 4 + 4)
        near_a[tile, :, 0:4] = value_a[:, lanes]
        near_b[tile, :, 0:4] = value_b[:, lanes]


def merge_tables(start, table):
    rows = table.shape[0]
    tiles = SLAB // COLS
    one = jax.ShapeDtypeStruct((rows, 128), F4)
    many = jax.ShapeDtypeStruct((tiles, rows, 128), F4)
    vmem = pl.BlockSpec(memory_space=pltpu.VMEM)
    return pl.pallas_call(
        table_kernel,
        in_specs=[pl.BlockSpec(memory_space=pltpu.SMEM), vmem],
        out_specs=[vmem] * 5,
        out_shape=[one, many, many, one, one],
        compiler_params=params(40),
        name="merge_tables",
    )(start, table)


def split_rows(matrix):
    upper = matrix.astype(BF)
    return upper, (matrix - upper.astype(F4)).astype(BF)


def merge_kernel(left, own, right, matrix, near_a, near_b, far_cos, far_sin, out):
    dot = functools.partial(jnp.dot, preferred_element_type=F4)

    def phases(first, count):
        rows = slice(first, first + count)
        cosine, sine = far_cos[rows, :], far_sin[rows, :]
        real_parts, imag_parts = [], []
        for k in range(COLS // 128):
            a, b = near_a[0, rows, k : k + 1], near_b[0, rows, k : k + 1]
            real_parts.append(a * cosine + b * sine)
            imag_parts.append(b * cosine - a * sine)
        return jnp.concatenate(real_parts, 1), jnp.concatenate(imag_parts, 1)

    def blend(matrices, image, exact):
        upper, lower = matrices
        rows = upper.shape[0]
        if exact:
            both = dot(jnp.concatenate([upper, lower], 0), image.astype(BF))
            return both[:rows] + both[rows:]
        high = image.astype(BF)
        low = (image - high.astype(F4)).astype(BF)
        both = dot(jnp.concatenate([upper, lower], 0), high)
        return both[:rows] + both[rows:] + dot(upper, low)

    zeros = jnp.zeros((8, COLS), F4)
    images = []
    for side in range(8):
        parts = [ref[side].astype(F4) for ref in (left, own, right)]
        images.append(
            tuple(jnp.concatenate([p[8 * q : 8 * q + 8] for p in parts] + [zeros], 0) for q in (0, 1))
        )
    for first, count, depth in ((0, 32, 32), (32, 48, 32)):
        sides = [
            (
                split_rows(matrix[c * SIDE + first : c * SIDE + first + count, :depth]),
                phases(c * SIDE + first, count),
            )
            for c in range(2)
        ]
        merged = []
        for group in range(len(images) // 2):
            real_sum, imag_sum = None, None
            for c, (matrices, (a, b)) in enumerate(sides):
                real_in, imag_in = (
                    blend(matrices, images[2 * group + c][q], first == 0) for q in (0, 1)
                )
                real_out = a * real_in + b * imag_in
                imag_out = a * imag_in - b * real_in
                real_sum = real_out if c == 0 else real_sum + real_out
                imag_sum = imag_out if c == 0 else imag_sum + imag_out
            merged.append((real_sum, imag_sum))
        images = merged
    total = None
    for c in range(2):
        rows = slice(c * SIDE + 80, c * SIDE + SIDE)
        matrices = split_rows(matrix[rows, :48])
        a, b = phases(c * SIDE + 80, 128)
        value = a * blend(matrices, images[c][0], False) + b * blend(matrices, images[c][1], False)
        total = value if c == 0 else total + value
    out[...] = total.reshape(64, 2, COLS)


def merge(left, own, right, tables):
    matrix, near_a, near_b, far_cos, far_sin = tables
    rows = matrix.shape[0]
    image = pl.BlockSpec((8, 16, COLS), lambda i: (0, 0, i))
    whole = pl.BlockSpec((rows, 128), lambda i: (0, 0))
    tiled = pl.BlockSpec((1, rows, 128), lambda i: (i, 0, 0))
    return pl.pallas_call(
        merge_kernel,
        grid=(SLAB // COLS,),
        in_specs=[image] * 3 + [whole, tiled, tiled, whole, whole],
        out_specs=pl.BlockSpec((64, 2, COLS), lambda i: (0, 0, i)),
        out_shape=jax.ShapeDtypeStruct((64, 2, SLAB), F4),
        compiler_params=params(48),
        name="merge",
    )(left, own, right, matrix, near_a, near_b, far_cos, far_sin)


def from_neighbours(array):
    blocks = lax.axis_size(BEAM_COMP)
    left = lax.ppermute(array, BEAM_COMP, [(k, k + 1) for k in range(blocks - 1)])
    right = lax.ppermute(array, BEAM_COMP, [(k + 1, k) for k in range(blocks - 1)])
    return left, right


def band_table(band_offsets, band_weights, beam_delay):
    own = jnp.concatenate(
        [band_offsets.astype(F4)[:, :, None], band_weights, beam_delay[:, :, None]], 2
    )
    left, right = from_neighbours(own)
    pieces = [left[:, 8:16], own[:, 0:16], right[:, 0:8]]
    pieces += [left[:, 40:48], own[:, 16:48], right[:, 16:24]]
    pieces += [jnp.repeat(own[:, 48:112], 2, axis=1)]
    base = np.zeros((1, SIDE, 10), np.float32)
    spans = ((8, 0), (16, 8), (8, 16), (8, -8), (32, 8), (8, 24), (128, 8))
    base[0, :, 0] = np.concatenate([np.full(n, v) for n, v in spans])
    return (jnp.concatenate(pieces, 1) + base).reshape(2 * SIDE, 10)


def ring_half(order, angles, raw, half, first, second):
    plus, minus, q1, q3, own = beam_sums(order, angles, raw, half)
    p1 = ring_send(plus, first, 1)
    m1 = ring_send(minus, first, -1)
    s, t = relay_sums(q1, q3, p1, m1, 2048)
    p2 = ring_send(s, first, 1)
    m2 = ring_send(t, first, -1)
    plus, minus, q1, q3, keep = middle_sums(own, p1, m1, p2, m2)
    p3 = ring_send(plus, second, 1)
    m3 = ring_send(minus, second, -1)
    s, t = relay_sums(q1, q3, p3, m3, 8192)
    p4 = ring_send(s, second, 1)
    m4 = ring_send(t, second, -1)
    return keep, p3, m3, p4, m4


def body(raw_pulses, range_filter, steer_angle, band_offsets, band_weights, beam_delay):
    y_index = lax.axis_index(Y)
    z_index = lax.axis_index(Z)
    near = np.array(ORDER, np.int32)

    def block_of(y, z):
        y, z = y % RING, z % RING
        return (y // 2) * 8 + z * 2 + y % 2

    order_z = block_of(y_index + near[:, 1], z_index + near[:, 0]).astype(jnp.int32)
    order_y = block_of(y_index + near[:, 0], z_index + near[:, 1]).astype(jnp.int32)
    pieces = ring_half(order_z, steer_angle, raw_pulses, 0, Z, Y)
    pieces += ring_half(order_y, steer_angle, raw_pulses, 1, Y, Z)
    table = band_table(band_offsets, band_weights, beam_delay)
    start = (lax.axis_index("sub") * SLAB).astype(jnp.int32).reshape(1)
    tables = merge_tables(start, table)
    beams = compressed_beams(pieces, range_filter)
    image = lax.all_to_all(beams, "sub", 0, 0, tiled=True)
    left, right = from_neighbours(image)
    return merge(left, image, right, tables)


def solution(mesh):
    split = Mesh(
        mesh.devices.reshape(mesh.shape["sub"], 2, RING, mesh.shape["comp"]), SUB_BEAM_COMP
    )
    return jax.shard_map(
        body,
        mesh=split,
        in_specs=(
            P(SUB_BEAM_COMP, None, None),
            P(),
            P(None, SUB_BEAM_COMP),
            P(None, BEAM_COMP),
            P(None, BEAM_COMP, None),
            P(None, BEAM_COMP),
        ),
        out_specs=P(BEAM_COMP, None, "sub"),
        check_vma=False,
    )
```

profile of v0, /device:TPU:16, one launch (start us, length us, event | category | flops | bytes accessed | tf_op | source)
XLA Modules:
  0.0 145.7 jit_solution(16903672367707468964)
XLA Ops:
  0.7 3.4 %copy-done = bf16[128,2,16384]{2,1,0:T(2,128)(2,1)S(1)} copy-done((bf16[128,2,16384]{2,1,0:T(2,128)(2,1)S(1)}, bf16[128,2,16384]{2,1,0:T(2,128)(2,1)}, u32[]{:S(2)}) %copy-start) | copy-done | bytes 8388632
  4.9 3.7 %beam_sums.3 = (bf16[64,8192]{1,0:T(8,128)(2,1)S(1)}, bf16[64,8192]{1,0:T(8,128)(2,1)S(1)}, bf16[32,8192]{1,0:T(8,128)(2,1)S(1)}, bf16[32,8192]{1,0:T(8,128)(2,1)S(1)}, bf16[64,8192]{1,0:T(8,128)(2,1)S(1)}) custom-call(s32[16]{0:T(128)S(1)} %get-tuple-element.75.order_ref, f32[128,128]{1,0:T(8,128)S(1)} %copy-done.18, bf16[128,2,16384]{2,1,0:T(2,128)(2,1)S(1)} %copy-done), custom_call_target="tpu_custom_call" | custom-call | tf_op jit(solution)/shard_map/beam_sums/pallas_call | solution.py:99
  13.3 3.7 %beam_sums.2 = (bf16[64,8192]{1,0:T(8,128)(2,1)S(1)}, bf16[64,8192]{1,0:T(8,128)(2,1)S(1)}, bf16[32,8192]{1,0:T(8,128)(2,1)S(1)}, bf16[32,8192]{1,0:T(8,128)(2,1)S(1)}, bf16[64,8192]{1,0:T(8,128)(2,1)S(1)}) custom-call(s32[16]{0:T(128)S(1)} %get-tuple-element.76.order_ref, f32[128,128]{1,0:T(8,128)S(1)} %copy-done.19, bf16[128,2,16384]{2,1,0:T(2,128)(2,1)S(1)} %copy-done.1), custom_call_target="tpu_custom_call" | custom-call | tf_op jit(solution)/shard_map/beam_sums/pallas_call | solution.py:99
  19.6 1.9 %collective-permute-start = (bf16[64,8192]{1,0:T(8,128)(2,1)S(1)}, bf16[64,8192]{1,0:T(8,128)(2,1)S(1)}, u32[]{:S(2)}, u32[]{:S(2)}) collective-permute-start(bf16[64,8192]{1,0:T(8,128)(2,1)S(1)} %get-tuple-element.39), channel_id=1, source_target_pairs={{0,2},{2,4},{4,6},{6,0},{1,3},{3,5},{5,7},{7,1},{8,10},{10,12},{12... | collective-permute-start | bytes 3145736 | tf_op jit(solution)/shard_map/ppermute | solution.py:61
  21.5 2.2 %collective-permute-start.1 = (bf16[64,8192]{1,0:T(8,128)(2,1)S(1)}, bf16[64,8192]{1,0:T(8,128)(2,1)}, u32[]{:S(2)}, u32[]{:S(2)}) collective-permute-start(bf16[64,8192]{1,0:T(8,128)(2,1)S(1)} %get-tuple-element.40), channel_id=1, source_target_pairs={{0,6},{2,0},{4,2},{6,4},{1,7},{3,1},{5,3},{7,5},{8,14},{10,8},{12,... | collective-permute-start | bytes 3145736 | tf_op jit(solution)/shard_map/ppermute | solution.py:61
  23.7 12.4 %collective-permute-done.8.p1 = bf16[64,8192]{1,0:T(8,128)(2,1)S(1)} collective-permute-done((bf16[64,8192]{1,0:T(8,128)(2,1)S(1)}, bf16[64,8192]{1,0:T(8,128)(2,1)S(1)}, u32[]{:S(2)}, u32[]{:S(2)}) %collective-permute-start.8) | collective-permute-done | bytes 1048608 | tf_op jit(solution)/shard_map/ppermute | solution.py:61
  38.1 3.6 %relay_sums.6 = (bf16[32,8192]{1,0:T(8,128)(2,1)}, bf16[32,8192]{1,0:T(8,128)(2,1)}) custom-call(bf16[32,8192]{1,0:T(8,128)(2,1)} %copy-done.16, bf16[32,8192]{1,0:T(8,128)(2,1)} %copy-done.17, bf16[64,8192]{1,0:T(8,128)(2,1)} %copy-done.23, bf16[64,8192]{1,0:T(8,128)(2,1)} %copy-done.24), custom_call_target="tpu_custom_call" | custom-call | tf_op jit(solution)/shard_map/relay_sums/pallas_call | solution.py:125
  43.8 2.4 %collective-permute-done.p1 = bf16[64,8192]{1,0:T(8,128)(2,1)S(1)} collective-permute-done((bf16[64,8192]{1,0:T(8,128)(2,1)S(1)}, bf16[64,8192]{1,0:T(8,128)(2,1)S(1)}, u32[]{:S(2)}, u32[]{:S(2)}) %collective-permute-start) | collective-permute-done | bytes 1048608 | tf_op jit(solution)/shard_map/ppermute | solution.py:61
  47.2 3.7 %relay_sums.4 = (bf16[32,8192]{1,0:T(8,128)(2,1)}, bf16[32,8192]{1,0:T(8,128)(2,1)}) custom-call(bf16[32,8192]{1,0:T(8,128)(2,1)} %copy-done.14, bf16[32,8192]{1,0:T(8,128)(2,1)} %copy-done.15, bf16[64,8192]{1,0:T(8,128)(2,1)} %copy-done.22, bf16[64,8192]{1,0:T(8,128)(2,1)} %collective-permute-done.1.m1), custom_call_target="tpu_custom_call" | custom-call | tf_op jit(solution)/shard_map/relay_sums/pallas_call | solution.py:125
  51.3 2.9 %collective-permute-start.3 = (bf16[32,8192]{1,0:T(8,128)(2,1)}, bf16[32,8192]{1,0:T(8,128)(2,1)S(1)}, u32[]{:S(2)}, u32[]{:S(2)}) collective-permute-start(bf16[32,8192]{1,0:T(8,128)(2,1)} %get-tuple-element.44), channel_id=1, source_target_pairs={{0,6},{2,0},{4,2},{6,4},{1,7},{3,1},{5,3},{7,5},{8,14},{10,8},{12,... | collective-permute-start | bytes 1572872 | tf_op jit(solution)/shard_map/ppermute | solution.py:61
  55.9 3.8 %middle_sums.3 = (bf16[16,8192]{1,0:T(8,128)(2,1)}, bf16[16,8192]{1,0:T(8,128)(2,1)}, bf16[8,8192]{1,0:T(8,128)(2,1)}, bf16[8,8192]{1,0:T(8,128)(2,1)}, f32[16,8192]{1,0:T(8,128)}) custom-call(bf16[64,8192]{1,0:T(8,128)(2,1)} %copy-done.11, bf16[64,8192]{1,0:T(8,128)(2,1)} %copy-done.23, bf16[64,8192]{1,0:T(8,128)(2,1)} %copy-done.24, ...), custom_call_target="tpu_custom_call" | custom-call | tf_op jit(solution)/shard_map/middle_sums/pallas_call | solution.py:149
  59.8 2.0 %collective-permute-start.12 = (bf16[16,8192]{1,0:T(8,128)(2,1)}, bf16[16,8192]{1,0:T(8,128)(2,1)S(1)}, u32[]{:S(2)}, u32[]{:S(2)}) collective-permute-start(bf16[16,8192]{1,0:T(8,128)(2,1)} %get-tuple-element.60), channel_id=1, source_target_pairs={{0,2},{2,4},{4,6},{6,0},{1,3},{3,5},{5,7},{7,1},{8,10},{10,12},{12... | collective-permute-start | bytes 786440 | tf_op jit(solution)/shard_map/ppermute | solution.py:61
  61.8 2.2 %collective-permute-start.13 = (bf16[16,8192]{1,0:T(8,128)(2,1)}, bf16[16,8192]{1,0:T(8,128)(2,1)S(1)}, u32[]{:S(2)}, u32[]{:S(2)}) collective-permute-start(bf16[16,8192]{1,0:T(8,128)(2,1)} %get-tuple-element.61), channel_id=1, source_target_pairs={{0,6},{2,0},{4,2},{6,4},{1,7},{3,1},{5,3},{7,5},{8,14},{10,8},{12,... | collective-permute-start | bytes 786440 | tf_op jit(solution)/shard_map/ppermute | solution.py:61
  64.0 3.1 %collective-permute-done.2.p2 = bf16[32,8192]{1,0:T(8,128)(2,1)S(1)} collective-permute-done((bf16[32,8192]{1,0:T(8,128)(2,1)}, bf16[32,8192]{1,0:T(8,128)(2,1)S(1)}, u32[]{:S(2)}, u32[]{:S(2)}) %collective-permute-start.2) | collective-permute-done | bytes 524320 | tf_op jit(solution)/shard_map/ppermute | solution.py:61
  68.0 3.9 %middle_sums.2 = (bf16[16,8192]{1,0:T(8,128)(2,1)}, bf16[16,8192]{1,0:T(8,128)(2,1)}, bf16[8,8192]{1,0:T(8,128)(2,1)}, bf16[8,8192]{1,0:T(8,128)(2,1)}, f32[16,8192]{1,0:T(8,128)}) custom-call(bf16[64,8192]{1,0:T(8,128)(2,1)} %copy-done.10, bf16[64,8192]{1,0:T(8,128)(2,1)} %copy-done.22, bf16[64,8192]{1,0:T(8,128)(2,1)} %collective-permute-done.1.m1, ...), custom_call_target="tpu_custom_call" | custom-call | tf_op jit(solution)/shard_map/middle_sums/pallas_call | solution.py:149
  71.9 2.0 %collective-permute-start.5 = (bf16[16,8192]{1,0:T(8,128)(2,1)}, bf16[16,8192]{1,0:T(8,128)(2,1)S(1)}, u32[]{:S(2)}, u32[]{:S(2)}) collective-permute-start(bf16[16,8192]{1,0:T(8,128)(2,1)} %get-tuple-element.47), channel_id=1, source_target_pairs={{0,9},{1,0},{8,1},{9,8},{2,11},{3,2},{10,3},{11,10},{4,13},{5,4},{... | collective-permute-start | bytes 786440 | tf_op jit(solution)/shard_map/ppermute | solution.py:61
  74.8 1.8 %relay_sums.7 = (bf16[8,8192]{1,0:T(8,128)(2,1)}, bf16[8,8192]{1,0:T(8,128)(2,1)}) custom-call(bf16[8,8192]{1,0:T(8,128)(2,1)} %get-tuple-element.62.q1, bf16[8,8192]{1,0:T(8,128)(2,1)} %get-tuple-element.63.q3, bf16[16,8192]{1,0:T(8,128)(2,1)} %copy-done.2, bf16[16,8192]{1,0:T(8,128)(2,1)} %copy-done.4), custom_call_target="tpu_custom_call" | custom-call | tf_op jit(solution)/shard_map/relay_sums/pallas_call | solution.py:125
  76.6 3.2 %collective-permute-start.15 = (bf16[8,8192]{1,0:T(8,128)(2,1)}, bf16[8,8192]{1,0:T(8,128)(2,1)S(1)}, u32[]{:S(2)}, u32[]{:S(2)}) collective-permute-start(bf16[8,8192]{1,0:T(8,128)(2,1)} %get-tuple-element.65), channel_id=1, source_target_pairs={{0,6},{2,0},{4,2},{6,4},{1,7},{3,1},{5,3},{7,5},{8,14},{10,8},{12,... | collective-permute-start | bytes 393224 | tf_op jit(solution)/shard_map/ppermute | solution.py:61
  80.7 1.9 %relay_sums.5 = (bf16[8,8192]{1,0:T(8,128)(2,1)}, bf16[8,8192]{1,0:T(8,128)(2,1)}) custom-call(bf16[8,8192]{1,0:T(8,128)(2,1)} %get-tuple-element.48.q1, bf16[8,8192]{1,0:T(8,128)(2,1)} %get-tuple-element.49.q3, bf16[16,8192]{1,0:T(8,128)(2,1)} %copy-done.6, bf16[16,8192]{1,0:T(8,128)(2,1)} %copy-done.8), custom_call_target="tpu_custom_call" | custom-call | tf_op jit(solution)/shard_map/relay_sums/pallas_call | solution.py:125
  82.5 1.8 %collective-permute-start.6 = (bf16[8,8192]{1,0:T(8,128)(2,1)}, bf16[8,8192]{1,0:T(8,128)(2,1)S(1)}, u32[]{:S(2)}, u32[]{:S(2)}) collective-permute-start(bf16[8,8192]{1,0:T(8,128)(2,1)} %get-tuple-element.50), channel_id=1, source_target_pairs={{0,1},{1,8},{8,9},{9,0},{2,3},{3,10},{10,11},{11,2},{4,5},{5,12},{... | collective-permute-start | bytes 393224 | tf_op jit(solution)/shard_map/ppermute | solution.py:61
  84.6 3.1 %collective-permute-done.6.refs_3_ = bf16[8,8192]{1,0:T(8,128)(2,1)S(1)} collective-permute-done((bf16[8,8192]{1,0:T(8,128)(2,1)}, bf16[8,8192]{1,0:T(8,128)(2,1)S(1)}, u32[]{:S(2)}, u32[]{:S(2)}) %collective-permute-start.6) | collective-permute-done | bytes 131104 | tf_op jit(solution)/shard_map/ppermute | solution.py:61
  95.4 2.1 %compressed_beams.1 = bf16[8,16,2048]{2,1,0:T(8,128)(2,1)} custom-call(f32[16,8192]{1,0:T(8,128)S(1)} %copy-done.13, bf16[16,8192]{1,0:T(8,128)(2,1)S(1)} %copy-done.7, bf16[16,8192]{1,0:T(8,128)(2,1)S(1)} %copy-done.9, bf16[8,8192]{1,0:T(8,128)(2,1)S(1)} %collective-permute-done.6.refs_3_, bf16[8,8192]{1,0:T(8,128)(2,1)S(1)} %collective-permute-done.7.refs_4_, ...), custom_call_target="tpu_custom_call" | custom-call | tf_op jit(solution)/shard_map/compressed_beams/pallas_call | solution.py:207
  97.5 4.3 %all-to-all-start = ((bf16[8,16,2048]{2,1,0:T(8,128)(2,1)}), bf16[8,16,2048]{2,1,0:T(8,128)(2,1)S(1)}, u32[]{:S(2)}, u32[]{:S(2)}) async-start(bf16[8,16,2048]{2,1,0:T(8,128)(2,1)} %compressed_beams.1), calls=%async_computation | async-start | bytes 1048576 | tf_op jit(solution)/shard_map/all_to_all | solution.py:402
  101.8 4.1 %collective-permute-start.19 = (f32[2,112,10]{1,0,2:T(2,128)S(1)}, f32[2,112,10]{1,0,2:T(2,128)S(1)}, u32[]{:S(2)}, u32[]{:S(2)}) collective-permute-start(f32[2,112,10]{1,0,2:T(2,128)S(1)} %pad_maximum_fusion), channel_id=1, source_target_pairs={{1,0},{2,1},{3,2},{4,3},{5,4},{6,5},{7,6},{8,7},{9,8},{10,9},{11,1... | collective-permute-start | bytes 26888 | tf_op jit(solution)/shard_map/ppermute | solution.py:351
  105.9 2.4 %collective-permute-start.18 = (f32[2,112,10]{1,0,2:T(2,128)S(1)}, f32[2,112,10]{1,0,2:T(2,128)S(1)}, u32[]{:S(2)}, u32[]{:S(2)}) collective-permute-start(f32[2,112,10]{1,0,2:T(2,128)S(1)} %pad_maximum_fusion), channel_id=1, source_target_pairs={{0,1},{1,2},{2,3},{3,4},{4,5},{5,6},{6,7},{7,8},{8,9},{9,10},{10,1... | collective-permute-start | bytes 26888 | tf_op jit(solution)/shard_map/ppermute | solution.py:350
  108.7 3.4 %all-to-all-done.own = bf16[8,16,2048]{2,1,0:T(8,128)(2,1)S(1)} async-done(((bf16[8,16,2048]{2,1,0:T(8,128)(2,1)}), bf16[8,16,2048]{2,1,0:T(8,128)(2,1)S(1)}, u32[]{:S(2)}, u32[]{:S(2)}) %all-to-all-start) | async-done | bytes 524320 | tf_op jit(solution)/shard_map/all_to_all | solution.py:402
  112.1 4.5 %collective-permute-start.16 = (bf16[8,16,2048]{2,1,0:T(8,128)(2,1)S(1)}, bf16[8,16,2048]{2,1,0:T(8,128)(2,1)S(1)}, u32[]{:S(2)}, u32[]{:S(2)}) collective-permute-start(bf16[8,16,2048]{2,1,0:T(8,128)(2,1)S(1)} %all-to-all-done.own), channel_id=1, source_target_pairs={{0,1},{1,2},{2,3},{3,4},{4,5},{5,6},{6,7},{7,8},{8,9},{9,10},{10,1... | collective-permute-start | bytes 1572872 | tf_op jit(solution)/shard_map/ppermute | solution.py:350
  116.7 3.6 %collective-permute-start.17 = (bf16[8,16,2048]{2,1,0:T(8,128)(2,1)S(1)}, bf16[8,16,2048]{2,1,0:T(8,128)(2,1)S(1)}, u32[]{:S(2)}, u32[]{:S(2)}) collective-permute-start(bf16[8,16,2048]{2,1,0:T(8,128)(2,1)S(1)} %all-to-all-done.own), channel_id=1, source_target_pairs={{1,0},{2,1},{3,2},{4,3},{5,4},{6,5},{7,6},{8,7},{9,8},{10,9},{11,1... | collective-permute-start | bytes 1572872 | tf_op jit(solution)/shard_map/ppermute | solution.py:351
  120.8 3.0 %merge_tables.1 = (f32[416,128]{1,0:T(8,128)S(1)}, f32[4,416,128]{2,1,0:T(8,128)S(1)}, f32[4,416,128]{2,1,0:T(8,128)S(1)}, f32[416,128]{1,0:T(8,128)S(1)}, f32[416,128]{1,0:T(8,128)S(1)}) custom-call(s32[1]{0:T(128)} %bitcast.start_ref, f32[416,10]{1,0:T(8,128)S(1)} %bitcast.11), custom_call_target="tpu_custom_call" | custom-call | tf_op jit(solution)/shard_map/merge_tables/pallas_call | solution.py:254
  123.8 5.8 %collective-permute-done.16.left = bf16[8,16,2048]{2,1,0:T(8,128)(2,1)S(1)} collective-permute-done((bf16[8,16,2048]{2,1,0:T(8,128)(2,1)S(1)}, bf16[8,16,2048]{2,1,0:T(8,128)(2,1)S(1)}, u32[]{:S(2)}, u32[]{:S(2)}) %collective-permute-start.16) | collective-permute-done | bytes 524320 | tf_op jit(solution)/shard_map/ppermute | solution.py:350
  129.6 10.0 %collective-permute-done.17.right = bf16[8,16,2048]{2,1,0:T(8,128)(2,1)S(1)} collective-permute-done((bf16[8,16,2048]{2,1,0:T(8,128)(2,1)S(1)}, bf16[8,16,2048]{2,1,0:T(8,128)(2,1)S(1)}, u32[]{:S(2)}, u32[]{:S(2)}) %collective-permute-start.17) | collective-permute-done | bytes 524320 | tf_op jit(solution)/shard_map/ppermute | solution.py:351
  139.6 6.1 %merge.1 = f32[64,2,2048]{2,1,0:T(2,128)} custom-call(bf16[8,16,2048]{2,1,0:T(8,128)(2,1)S(1)} %collective-permute-done.16.left, bf16[8,16,2048]{2,1,0:T(8,128)(2,1)S(1)} %all-to-all-done.own, bf16[8,16,2048]{2,1,0:T(8,128)(2,1)S(1)} %collective-permute-done.17.right, f32[416,128]{1,0:T(8,128)S(1)} %get-tuple-element.66.matrix, ...), custom_call_target="tpu_custom_call" | custom-call | tf_op jit(solution)/shard_map/merge/pallas_call | solution.py:337
  (100 shorter events, 27.4 us)
Async XLA Ops:
  0.7 3.4 %copy-start = (bf16[128,2,16384]{2,1,0:T(2,128)(2,1)S(1)}, bf16[128,2,16384]{2,1,0:T(2,128)(2,1)}, u32[]{:S(2)}) copy-start(bf16[128,2,16384]{2,1,0:T(2,128)(2,1)} %raw_ref.3) | copy-start | bytes 25165828
  4.9 8.3 %copy-start.1 = (bf16[128,2,16384]{2,1,0:T(2,128)(2,1)S(1)}, bf16[128,2,16384]{2,1,0:T(2,128)(2,1)}, u32[]{:S(2)}) copy-start(bf16[128,2,16384]{2,1,0:T(2,128)(2,1)} %raw_ref.3) | copy-start | bytes 25165828
  4.9 8.3 %copy-start.19 = (f32[128,128]{1,0:T(8,128)S(1)}, f32[128,128]{1,0:T(8,128)}, u32[]{:S(2)}) copy-start(f32[128,128]{1,0:T(8,128)} %angle_ref.3) | copy-start | bytes 196612
  11.2 24.9 %collective-permute-start.8 = (bf16[64,8192]{1,0:T(8,128)(2,1)S(1)}, bf16[64,8192]{1,0:T(8,128)(2,1)S(1)}, u32[]{:S(2)}, u32[]{:S(2)}) collective-permute-start(bf16[64,8192]{1,0:T(8,128)(2,1)S(1)} %get-tuple-element.53), channel_id=1, source_target_pairs={{0,1},{1,8},{8,9},{9,0},{2,3},{3,10},{10,11},{11,2},{4,5},{5,12},{... | collective-permute-start | bytes 3145736 | tf_op jit(solution)/shard_map/ppermute | solution.py:61
  12.5 24.6 %collective-permute-start.9 = (bf16[64,8192]{1,0:T(8,128)(2,1)S(1)}, bf16[64,8192]{1,0:T(8,128)(2,1)S(1)}, u32[]{:S(2)}, u32[]{:S(2)}) collective-permute-start(bf16[64,8192]{1,0:T(8,128)(2,1)S(1)} %get-tuple-element.54), channel_id=1, source_target_pairs={{0,9},{1,0},{8,1},{9,8},{2,11},{3,2},{10,3},{11,10},{4,13},{5,4},{... | collective-permute-start | bytes 3145736 | tf_op jit(solution)/shard_map/ppermute | solution.py:61
  19.6 64.9 %copy-start.27 = (f32[2,16384]{1,0:T(2,128)S(1)}, f32[2,16384]{1,0:T(2,128)}, u32[]{:S(2)}) copy-start(f32[2,16384]{1,0:T(2,128)} %param.14) | copy-start | bytes 393220
  19.6 69.9 %copy-start.20 = (bf16[256,256]{1,0:T(8,128)(2,1)S(1)}, bf16[256,256]{1,0:T(8,128)(2,1)}, u32[]{:S(2)}) copy-start(bf16[256,256]{1,0:T(8,128)(2,1)} %constant.98.clone.refs_10_) | copy-start | bytes 393220
  19.6 69.9 %copy-start.21 = (f32[2,128,128]{2,1,0:T(8,128)S(1)}, f32[2,128,128]{2,1,0:T(8,128)}, u32[]{:S(2)}) copy-start(f32[2,128,128]{2,1,0:T(8,128)} %constant.99.clone.refs_11_) | copy-start | bytes 393220
  19.6 26.6 %collective-permute-start = (bf16[64,8192]{1,0:T(8,128)(2,1)S(1)}, bf16[64,8192]{1,0:T(8,128)(2,1)S(1)}, u32[]{:S(2)}, u32[]{:S(2)}) collective-permute-start(bf16[64,8192]{1,0:T(8,128)(2,1)S(1)} %get-tuple-element.39), channel_id=1, source_target_pairs={{0,2},{2,4},{4,6},{6,0},{1,3},{3,5},{5,7},{7,1},{8,10},{10,12},{12... | collective-permute-start | bytes 3145736 | tf_op jit(solution)/shard_map/ppermute | solution.py:61
  21.5 24.7 %collective-permute-start.1 = (bf16[64,8192]{1,0:T(8,128)(2,1)S(1)}, bf16[64,8192]{1,0:T(8,128)(2,1)}, u32[]{:S(2)}, u32[]{:S(2)}) collective-permute-start(bf16[64,8192]{1,0:T(8,128)(2,1)S(1)} %get-tuple-element.40), channel_id=1, source_target_pairs={{0,6},{2,0},{4,2},{6,4},{1,7},{3,1},{5,3},{7,5},{8,14},{10,8},{12,... | collective-permute-start | bytes 3145736 | tf_op jit(solution)/shard_map/ppermute | solution.py:61
  41.8 13.2 %collective-permute-start.10 = (bf16[32,8192]{1,0:T(8,128)(2,1)}, bf16[32,8192]{1,0:T(8,128)(2,1)}, u32[]{:S(2)}, u32[]{:S(2)}) collective-permute-start(bf16[32,8192]{1,0:T(8,128)(2,1)} %get-tuple-element.57), channel_id=1, source_target_pairs={{0,1},{1,8},{8,9},{9,0},{2,3},{3,10},{10,11},{11,2},{4,5},{5,12},{... | collective-permute-start | bytes 1572872 | tf_op jit(solution)/shard_map/ppermute | solution.py:61
  43.3 12.7 %collective-permute-start.11 = (bf16[32,8192]{1,0:T(8,128)(2,1)}, bf16[32,8192]{1,0:T(8,128)(2,1)}, u32[]{:S(2)}, u32[]{:S(2)}) collective-permute-start(bf16[32,8192]{1,0:T(8,128)(2,1)} %get-tuple-element.58), channel_id=1, source_target_pairs={{0,9},{1,0},{8,1},{9,8},{2,11},{3,2},{10,3},{11,10},{4,13},{5,4},{... | collective-permute-start | bytes 1572872 | tf_op jit(solution)/shard_map/ppermute | solution.py:61
  47.2 54.6 %copy-start.29 = (f32[2,112,8]{1,2,0:T(8,128)S(1)}, f32[2,112,8]{1,2,0:T(8,128)}, u32[]{:S(2)}) copy-start(f32[2,112,8]{1,2,0:T(8,128)} %param.17) | copy-start | bytes 21508
  47.2 54.6 %copy-start.31 = (s32[2,112]{1,0:T(2,128)S(1)}, s32[2,112]{1,0:T(2,128)}, u32[]{:S(2)}) copy-start(s32[2,112]{1,0:T(2,128)} %param.16) | copy-start | bytes 2692
  47.2 54.6 %copy-start.30 = (f32[2,112]{1,0:T(2,128)S(1)}, f32[2,112]{1,0:T(2,128)}, u32[]{:S(2)}) copy-start(f32[2,112]{1,0:T(2,128)} %param.18) | copy-start | bytes 2692
  50.9 69.7 %copy-start.28 = (f32[208,10]{0,1:T(8,128)S(1)}, f32[208,10]{0,1:T(8,128)}, u32[]{:S(2)}) copy-start(f32[208,10]{0,1:T(8,128)} %constant.100) | copy-start | bytes 24964
  50.9 16.1 %collective-permute-start.2 = (bf16[32,8192]{1,0:T(8,128)(2,1)}, bf16[32,8192]{1,0:T(8,128)(2,1)S(1)}, u32[]{:S(2)}, u32[]{:S(2)}) collective-permute-start(bf16[32,8192]{1,0:T(8,128)(2,1)} %get-tuple-element.43), channel_id=1, source_target_pairs={{0,2},{2,4},{4,6},{6,0},{1,3},{3,5},{5,7},{7,1},{8,10},{10,12},{12... | collective-permute-start | bytes 1572872 | tf_op jit(solution)/shard_map/ppermute | solution.py:61
  51.3 15.7 %collective-permute-start.3 = (bf16[32,8192]{1,0:T(8,128)(2,1)}, bf16[32,8192]{1,0:T(8,128)(2,1)S(1)}, u32[]{:S(2)}, u32[]{:S(2)}) collective-permute-start(bf16[32,8192]{1,0:T(8,128)(2,1)} %get-tuple-element.44), channel_id=1, source_target_pairs={{0,6},{2,0},{4,2},{6,4},{1,7},{3,1},{5,3},{7,5},{8,14},{10,8},{12,... | collective-permute-start | bytes 1572872 | tf_op jit(solution)/shard_map/ppermute | solution.py:61
  59.8 14.2 %collective-permute-start.12 = (bf16[16,8192]{1,0:T(8,128)(2,1)}, bf16[16,8192]{1,0:T(8,128)(2,1)S(1)}, u32[]{:S(2)}, u32[]{:S(2)}) collective-permute-start(bf16[16,8192]{1,0:T(8,128)(2,1)} %get-tuple-element.60), channel_id=1, source_target_pairs={{0,2},{2,4},{4,6},{6,0},{1,3},{3,5},{5,7},{7,1},{8,10},{10,12},{12... | collective-permute-start | bytes 786440 | tf_op jit(solution)/shard_map/ppermute | solution.py:61
  61.8 12.2 %collective-permute-start.13 = (bf16[16,8192]{1,0:T(8,128)(2,1)}, bf16[16,8192]{1,0:T(8,128)(2,1)S(1)}, u32[]{:S(2)}, u32[]{:S(2)}) collective-permute-start(bf16[16,8192]{1,0:T(8,128)(2,1)} %get-tuple-element.61), channel_id=1, source_target_pairs={{0,6},{2,0},{4,2},{6,4},{1,7},{3,1},{5,3},{7,5},{8,14},{10,8},{12,... | collective-permute-start | bytes 786440 | tf_op jit(solution)/shard_map/ppermute | solution.py:61
  71.9 8.0 %collective-permute-start.4 = (bf16[16,8192]{1,0:T(8,128)(2,1)}, bf16[16,8192]{1,0:T(8,128)(2,1)S(1)}, u32[]{:S(2)}, u32[]{:S(2)}) collective-permute-start(bf16[16,8192]{1,0:T(8,128)(2,1)} %get-tuple-element.46), channel_id=1, source_target_pairs={{0,1},{1,8},{8,9},{9,0},{2,3},{3,10},{10,11},{11,2},{4,5},{5,12},{... | collective-permute-start | bytes 786440 | tf_op jit(solution)/shard_map/ppermute | solution.py:61
  71.9 7.9 %collective-permute-start.5 = (bf16[16,8192]{1,0:T(8,128)(2,1)}, bf16[16,8192]{1,0:T(8,128)(2,1)S(1)}, u32[]{:S(2)}, u32[]{:S(2)}) collective-permute-start(bf16[16,8192]{1,0:T(8,128)(2,1)} %get-tuple-element.47), channel_id=1, source_target_pairs={{0,9},{1,0},{8,1},{9,8},{2,11},{3,2},{10,3},{11,10},{4,13},{5,4},{... | collective-permute-start | bytes 786440 | tf_op jit(solution)/shard_map/ppermute | solution.py:61
  76.6 7.9 %collective-permute-start.14 = (bf16[8,8192]{1,0:T(8,128)(2,1)}, bf16[8,8192]{1,0:T(8,128)(2,1)S(1)}, u32[]{:S(2)}, u32[]{:S(2)}) collective-permute-start(bf16[8,8192]{1,0:T(8,128)(2,1)} %get-tuple-element.64), channel_id=1, source_target_pairs={{0,2},{2,4},{4,6},{6,0},{1,3},{3,5},{5,7},{7,1},{8,10},{10,12},{12... | collective-permute-start | bytes 393224 | tf_op jit(solution)/shard_map/ppermute | solution.py:61
  76.6 7.9 %collective-permute-start.15 = (bf16[8,8192]{1,0:T(8,128)(2,1)}, bf16[8,8192]{1,0:T(8,128)(2,1)S(1)}, u32[]{:S(2)}, u32[]{:S(2)}) collective-permute-start(bf16[8,8192]{1,0:T(8,128)(2,1)} %get-tuple-element.65), channel_id=1, source_target_pairs={{0,6},{2,0},{4,2},{6,4},{1,7},{3,1},{5,3},{7,5},{8,14},{10,8},{12,... | collective-permute-start | bytes 393224 | tf_op jit(solution)/shard_map/ppermute | solution.py:61
  82.5 5.2 %collective-permute-start.6 = (bf16[8,8192]{1,0:T(8,128)(2,1)}, bf16[8,8192]{1,0:T(8,128)(2,1)S(1)}, u32[]{:S(2)}, u32[]{:S(2)}) collective-permute-start(bf16[8,8192]{1,0:T(8,128)(2,1)} %get-tuple-element.50), channel_id=1, source_target_pairs={{0,1},{1,8},{8,9},{9,0},{2,3},{3,10},{10,11},{11,2},{4,5},{5,12},{... | collective-permute-start | bytes 393224 | tf_op jit(solution)/shard_map/ppermute | solution.py:61
  84.3 5.2 %collective-permute-start.7 = (bf16[8,8192]{1,0:T(8,128)(2,1)}, bf16[8,8192]{1,0:T(8,128)(2,1)S(1)}, u32[]{:S(2)}, u32[]{:S(2)}) collective-permute-start(bf16[8,8192]{1,0:T(8,128)(2,1)} %get-tuple-element.51), channel_id=1, source_target_pairs={{0,9},{1,0},{8,1},{9,8},{2,11},{3,2},{10,3},{11,10},{4,13},{5,4},{... | collective-permute-start | bytes 393224 | tf_op jit(solution)/shard_map/ppermute | solution.py:61
  93.3 1.0 copy-start.12
  97.5 14.7 %all-to-all-start = ((bf16[8,16,2048]{2,1,0:T(8,128)(2,1)}), bf16[8,16,2048]{2,1,0:T(8,128)(2,1)S(1)}, u32[]{:S(2)}, u32[]{:S(2)}) async-start(bf16[8,16,2048]{2,1,0:T(8,128)(2,1)} %compressed_beams.1), calls=%async_computation | async-start | bytes 1048576 | tf_op jit(solution)/shard_map/all_to_all | solution.py:402
  101.8 18.4 %collective-permute-start.19 = (f32[2,112,10]{1,0,2:T(2,128)S(1)}, f32[2,112,10]{1,0,2:T(2,128)S(1)}, u32[]{:S(2)}, u32[]{:S(2)}) collective-permute-start(f32[2,112,10]{1,0,2:T(2,128)S(1)} %pad_maximum_fusion), channel_id=1, source_target_pairs={{1,0},{2,1},{3,2},{4,3},{5,4},{6,5},{7,6},{8,7},{9,8},{10,9},{11,1... | collective-permute-start | bytes 26888 | tf_op jit(solution)/shard_map/ppermute | solution.py:351
  105.9 14.4 %collective-permute-start.18 = (f32[2,112,10]{1,0,2:T(2,128)S(1)}, f32[2,112,10]{1,0,2:T(2,128)S(1)}, u32[]{:S(2)}, u32[]{:S(2)}) collective-permute-start(f32[2,112,10]{1,0,2:T(2,128)S(1)} %pad_maximum_fusion), channel_id=1, source_target_pairs={{0,1},{1,2},{2,3},{3,4},{4,5},{5,6},{6,7},{7,8},{8,9},{9,10},{10,1... | collective-permute-start | bytes 26888 | tf_op jit(solution)/shard_map/ppermute | solution.py:350
  112.1 17.5 %collective-permute-start.16 = (bf16[8,16,2048]{2,1,0:T(8,128)(2,1)S(1)}, bf16[8,16,2048]{2,1,0:T(8,128)(2,1)S(1)}, u32[]{:S(2)}, u32[]{:S(2)}) collective-permute-start(bf16[8,16,2048]{2,1,0:T(8,128)(2,1)S(1)} %all-to-all-done.own), channel_id=1, source_target_pairs={{0,1},{1,2},{2,3},{3,4},{4,5},{5,6},{6,7},{7,8},{8,9},{9,10},{10,1... | collective-permute-start | bytes 1572872 | tf_op jit(solution)/shard_map/ppermute | solution.py:350
  116.7 22.9 %collective-permute-start.17 = (bf16[8,16,2048]{2,1,0:T(8,128)(2,1)S(1)}, bf16[8,16,2048]{2,1,0:T(8,128)(2,1)S(1)}, u32[]{:S(2)}, u32[]{:S(2)}) collective-permute-start(bf16[8,16,2048]{2,1,0:T(8,128)(2,1)S(1)} %all-to-all-done.own), channel_id=1, source_target_pairs={{1,0},{2,1},{3,2},{4,3},{5,4},{6,5},{7,6},{8,7},{9,8},{10,9},{11,1... | collective-permute-start | bytes 1572872 | tf_op jit(solution)/shard_map/ppermute | solution.py:351
  (21 other events, 18.7 us)
where the time goes:
time: 147 us; the launch traced here: 146 us
  waiting for transfers between devices  44.9 us (31%)
  starting transfers between devices  41.9 us (29%)
  Pallas kernels  37.3 us (25%)
  local copies, waits for them, and re-layouts  20.7 us (14%)
    ppermute x16, waiting for transfers between devices, ring_send(): return lax.ppermute(x, axis, [(k, (k + step) % RING) for k in range(RING)])  25.6 us
    ppermute x16, starting transfers between devices, ring_send(): return lax.ppermute(x, axis, [(k, (k + step) % RING) for k in range(RING)])  23 us
    unnamed x66, local copies, waits for them, and re-layouts  19.9 us
    pallas_call x4, Pallas kernels, relay_sums(): pl.pallas_call(relay_kernel, grid=(cols // tile,), in_specs=[spec] * 4, o...  11 us
    ppermute x2, waiting for transfers between devices, from_neighbours(): lax.ppermute(array, BEAM_COMP, [(k + 1, k) for k in range(blocks - 1)])  10 us
    pallas_call x2, Pallas kernels, middle_sums(): pl.pallas_call(middle_kernel, grid=(HALF // tile,), in_specs=[pl.BlockSpe...  7.69 us
    ppermute x2, starting transfers between devices, from_neighbours(): lax.ppermute(array, BEAM_COMP, [(k + 1, k) for k in range(blocks - 1)])  7.64 us
    pallas_call x2, Pallas kernels, beam_sums(): pl.pallas_call(beam_kernel, grid_spec=pltpu.PrefetchScalarGridSpec(num_sc...  7.43 us
  transfers between devices with their start and end apart: 21, of which 11 were waited for; matrix products, arithmetic and copies ran while one was open for 1% of the time, Pallas kernels for 17%

commit v1 on v0

--- a/solution.py
+++ b/solution.py
@@ -28,14 +28,10 @@
 Z = "z"
 BF = jnp.bfloat16
 F4 = jnp.float32
-ORDER = (
-    (2, 0), (2, 1), (1, 2), (1, 3),
-    (2, 2), (2, 3), (3, 0), (3, 1),
-    (1, 0), (1, 1),
-    (3, 2), (3, 3),
-    (0, 0), (0, 1), (0, 2), (0, 3),
-)
-PARTS = (64, 64, 32, 32, 64)
+SENT = ((2, 0), (2, 1), (1, 2), (1, 3), (2, 2), (2, 3), (3, 0), (3, 1))
+KEPT = ((1, 0), (1, 1), (3, 2), (3, 3), (0, 0), (0, 1), (0, 2), (0, 3))
+SENT_ROWS = (64, 64)
+KEPT_ROWS = (32, 32, 64)
 
 
 def params(mebibytes):
@@ -61,29 +57,32 @@
     return lax.ppermute(x, axis, [(k, (k + step) % RING) for k in range(RING)])
 
 
-def beam_kernel(order_ref, angle_ref, raw_ref, *rest):
-    outs, weights = rest[:-1], rest[-1]
-
-    @pl.when(pl.program_id(0) == 0)
-    def _():
-        rows = lax.broadcasted_iota(jnp.int32, (128, 256), 0)
-        cols = lax.broadcasted_iota(jnp.int32, (128, 256), 1)
-        spread = jnp.where(cols // 2 == rows, 1.0, 0.0).astype(F4)
-        angle = jnp.dot(
-            angle_ref[...], spread, precision=lax.Precision.HIGHEST, preferred_element_type=F4
-        )
-        factor = float(PSUB) ** -0.5
-        cosine = jnp.cos(angle) * factor
-        sine = jnp.sin(angle) * factor
-        even = cols % 2 == 0
-        weights[0] = jnp.where(even, cosine, -sine)
-        weights[1] = jnp.where(even, sine, cosine)
-
+def steering_rows(angle_ref, weights):
+    factor = float(PSUB) ** -0.5
+    rows = lax.broadcasted_iota(jnp.int32, (128, 256), 0)
+    cols = lax.broadcasted_iota(jnp.int32, (128, 256), 1)
+    spread = jnp.where(cols // 2 == rows, 1.0, 0.0).astype(BF)
+    angle = angle_ref[...]
+    cosine = (jnp.cos(angle) * factor).astype(BF)
+    sine = (jnp.sin(angle) * factor).astype(BF)
+    cosine = jnp.dot(cosine, spread, preferred_element_type=F4)
+    sine = jnp.dot(sine, spread, preferred_element_type=F4)
+    even = cols % 2 == 0
+    weights[0] = jnp.where(even, cosine, -sine)
+    weights[1] = jnp.where(even, sine, cosine)
+
+
+def beam_products(weights, raw_ref, owners, z_first, outs):
+    y = lax.axis_index("y_hi") * 2 + lax.axis_index("y_lo")
+    z = lax.axis_index("z")
     picked = []
-    for k in range(16):
-        first = pl.multiple_of(order_ref[k] * NB0, NB0)
-        picked.append(weights[0, pl.ds(first, NB0), :])
-        picked.append(weights[1, pl.ds(first, NB0), :])
+    for first, second in owners:
+        y_step, z_step = (second, first) if z_first else (first, second)
+        y_of, z_of = lax.rem(y + y_step, RING), lax.rem(z + z_step, RING)
+        block = lax.div(y_of, 2) * 8 + z_of * 2 + lax.rem(y_of, 2)
+        start = pl.multiple_of(block * NB0, NB0)
+        picked.append(weights[0, pl.ds(start, NB0), :])
+        picked.append(weights[1, pl.ds(start, NB0), :])
     matrix = jnp.concatenate(picked, 0).astype(BF)
     raw = raw_ref[...].reshape(256, raw_ref.shape[2])
     total = jnp.dot(matrix, raw, preferred_element_type=F4).astype(BF)
@@ -94,65 +93,72 @@
         start += size
 
 
-def beam_sums(order, angles, raw, half):
+def opening_kernel(angle_ref, raw_ref, plus, minus, weights):
+    @pl.when(pl.program_id(0) == 0)
+    def _():
+        steering_rows(angle_ref, weights)
+
+    beam_products(weights, raw_ref, SENT, True, (plus, minus))
+
+
+def later_kernel(owners, z_first, weights, raw_ref, *outs):
+    beam_products(weights, raw_ref, owners, z_first, outs)
+
+
+def beam_sums(kernel, small, raw, half, sizes, with_weights):
     steps = HALF // TILE
+    weights = (2, 128, 256)
+
+    def fixed(shape):
+        return pl.BlockSpec(shape, lambda i: (0,) * len(shape))
+
     return pl.pallas_call(
-        beam_kernel,
-        grid_spec=pltpu.PrefetchScalarGridSpec(
-            num_scalar_prefetch=1,
-            grid=(steps,),
-            in_specs=[
-                pl.BlockSpec((128, 128), lambda i, o: (0, 0)),
-                pl.BlockSpec((128, 2, TILE), lambda i, o: (0, 0, i + half * steps)),
-            ],
-            out_specs=[pl.BlockSpec((n, TILE), lambda i, o: (0, i)) for n in PARTS],
-            scratch_shapes=[pltpu.VMEM((2, 128, 256), F4)],
-        ),
-        out_shape=[jax.ShapeDtypeStruct((n, HALF), BF) for n in PARTS],
-        compiler_params=params(40),
+        kernel,
+        grid=(steps,),
+        in_specs=[
+            fixed(small.shape),
+            pl.BlockSpec((128, 2, TILE), lambda i: (0, 0, i + half * steps)),
+        ],
+        out_specs=[pl.BlockSpec((n, TILE), lambda i: (0, i)) for n in sizes]
+        + [fixed(weights)] * with_weights,
+        out_shape=[pltpu.HBM((n, HALF), BF) for n in sizes]
+        + [jax.ShapeDtypeStruct(weights, F4)] * with_weights,
+        compiler_params=params(16),
         name="beam_sums",
-    )(order, angles, raw)
-
-
-def relay_kernel(q1, q3, p1, m1, s, t):
-    s[...] = (q1[...].astype(F4) + p1[...].astype(F4)).astype(BF)
-    t[...] = (q3[...].astype(F4) + m1[...].astype(F4)).astype(BF)
-
-
-def relay_sums(q1, q3, p1, m1, tile):
-    rows, cols = q1.shape
-    spec = pl.BlockSpec((rows, tile), lambda i: (0, i))
-    return pl.pallas_call(
-        relay_kernel,
-        grid=(cols // tile,),
-        in_specs=[spec] * 4,
-        out_specs=[spec] * 2,
-        out_shape=[jax.ShapeDtypeStruct((rows, cols), BF)] * 2,
-        name="relay_sums",
-    )(q1, q3, p1, m1)
+    )(small, pltpu.with_memory_space_constraint(raw, pltpu.HBM))
+
+
+def relay(q, received):
+    rows = q.shape[0]
+    return (q.astype(F4) + received[:rows].astype(F4)).astype(BF)
 
 
 def middle_kernel(own, p1, m1, p2, m2, plus, minus, q1, q3, keep):
-    low = own[:32].astype(F4) + m1[...].astype(F4) + p2[...].astype(F4)
-    high = own[32:].astype(F4) + p1[...].astype(F4) + m2[...].astype(F4)
-    keep[...] = low[:16]
-    q1[...] = low[16:24].astype(BF)
-    plus[...] = jnp.concatenate([high[:8], low[24:]], 0).astype(BF)
-    minus[...] = jnp.concatenate([high[8:16], high[16:24]], 0).astype(BF)
-    q3[...] = high[24:].astype(BF)
+    tile = 512
+
+    def step(k, carry):
+        cols = pl.ds(pl.multiple_of(k * tile, tile), tile)
+        low = own[:32, cols].astype(F4) + m1[32:, cols].astype(F4) + p2[:, cols].astype(F4)
+        high = own[32:, cols].astype(F4) + p1[32:, cols].astype(F4) + m2[:, cols].astype(F4)
+        keep[:, cols] = low[:16]
+        q1[:, cols] = low[16:24].astype(BF)
+        plus[:, cols] = jnp.concatenate([high[:8], low[24:]], 0).astype(BF)
+        minus[:, cols] = jnp.concatenate([high[8:16], high[16:24]], 0).astype(BF)
+        q3[:, cols] = high[24:].astype(BF)
+        return carry
+
+    lax.fori_loop(0, HALF // tile, step, 0)
 
 
 def middle_sums(own, p1, m1, p2, m2):
-    tile = 2048
     outs = ((16, BF), (16, BF), (8, BF), (8, BF), (16, F4))
-    received = pl.BlockSpec((32, tile), lambda i: (1, i))
+    vmem = pl.BlockSpec(memory_space=pltpu.VMEM)
     return pl.pallas_call(
         middle_kernel,
-        grid=(HALF // tile,),
-        in_specs=[pl.BlockSpec((64, tile), lambda i: (0, i)), received, received]
-        + [pl.BlockSpec((32, tile), lambda i: (0, i))] * 2,
-        out_specs=[pl.BlockSpec((n, tile), lambda i: (0, i)) for n, _ in outs],
+        in_specs=[vmem] * 5,
+        out_specs=[vmem] * 5,
         out_shape=[jax.ShapeDtypeStruct((n, HALF), d) for n, d in outs],
+        compiler_params=params(4),
         name="middle_sums",
     )(own, p1, m1, p2, m2)
 
@@ -208,7 +214,7 @@
         compress_kernel,
         out_shape=jax.ShapeDtypeStruct((8, 16, SLAB), BF),
         scratch_shapes=[pltpu.VMEM((2, 1024, 128), F4), pltpu.VMEM((2, 1024, 128), F4)],
-        compiler_params=params(40),
+        compiler_params=params(12),
         name="compressed_beams",
     )(
         *pieces,
@@ -256,7 +262,7 @@
         in_specs=[pl.BlockSpec(memory_space=pltpu.SMEM), vmem],
         out_specs=[vmem] * 5,
         out_shape=[one, many, many, one, one],
-        compiler_params=params(40),
+        compiler_params=params(12),
         name="merge_tables",
     )(start, table)
 
@@ -340,7 +346,7 @@
         in_specs=[image] * 3 + [whole, tiled, tiled, whole, whole],
         out_specs=pl.BlockSpec((64, 2, COLS), lambda i: (0, 0, i)),
         out_shape=jax.ShapeDtypeStruct((64, 2, SLAB), F4),
-        compiler_params=params(48),
+        compiler_params=params(24),
         name="merge",
     )(left, own, right, matrix, near_a, near_b, far_cos, far_sin)
 
@@ -352,10 +358,13 @@
     return left, right
 
 
-def band_table(band_offsets, band_weights, beam_delay):
-    own = jnp.concatenate(
+def own_table(band_offsets, band_weights, beam_delay):
+    return jnp.concatenate(
         [band_offsets.astype(F4)[:, :, None], band_weights, beam_delay[:, :, None]], 2
     )
+
+
+def band_table(own):
     left, right = from_neighbours(own)
     pieces = [left[:, 8:16], own[:, 0:16], right[:, 0:8]]
     pieces += [left[:, 40:48], own[:, 16:48], right[:, 16:24]]
@@ -366,38 +375,36 @@
     return (jnp.concatenate(pieces, 1) + base).reshape(2 * SIDE, 10)
 
 
-def ring_half(order, angles, raw, half, first, second):
-    plus, minus, q1, q3, own = beam_sums(order, angles, raw, half)
-    p1 = ring_send(plus, first, 1)
-    m1 = ring_send(minus, first, -1)
-    s, t = relay_sums(q1, q3, p1, m1, 2048)
-    p2 = ring_send(s, first, 1)
-    m2 = ring_send(t, first, -1)
+def ring_start(parts, first):
+    return ring_send(parts[0], first, 1), ring_send(parts[1], first, -1)
+
+
+def ring_rest(kept, received, first, second):
+    q1, q3, own = kept
+    p1, m1 = received
+    p2 = ring_send(relay(q1, p1), first, 1)
+    m2 = ring_send(relay(q3, m1), first, -1)
     plus, minus, q1, q3, keep = middle_sums(own, p1, m1, p2, m2)
     p3 = ring_send(plus, second, 1)
     m3 = ring_send(minus, second, -1)
-    s, t = relay_sums(q1, q3, p3, m3, 8192)
-    p4 = ring_send(s, second, 1)
-    m4 = ring_send(t, second, -1)
+    p4 = ring_send(relay(q1, p3), second, 1)
+    m4 = ring_send(relay(q3, m3), second, -1)
     return keep, p3, m3, p4, m4
 
 
 def body(raw_pulses, range_filter, steer_angle, band_offsets, band_weights, beam_delay):
-    y_index = lax.axis_index(Y)
-    z_index = lax.axis_index(Z)
-    near = np.array(ORDER, np.int32)
-
-    def block_of(y, z):
-        y, z = y % RING, z % RING
-        return (y // 2) * 8 + z * 2 + y % 2
-
-    order_z = block_of(y_index + near[:, 1], z_index + near[:, 0]).astype(jnp.int32)
-    order_y = block_of(y_index + near[:, 0], z_index + near[:, 1]).astype(jnp.int32)
-    pieces = ring_half(order_z, steer_angle, raw_pulses, 0, Z, Y)
-    pieces += ring_half(order_y, steer_angle, raw_pulses, 1, Y, Z)
-    table = band_table(band_offsets, band_weights, beam_delay)
+    later = functools.partial
+    angles = pltpu.with_memory_space_constraint(steer_angle, pltpu.HBM)
+    *sent_z, weights = beam_sums(opening_kernel, angles, raw_pulses, 0, SENT_ROWS, True)
+    received_z = ring_start(sent_z, Z)
+    sent_y = beam_sums(later(later_kernel, SENT, False), weights, raw_pulses, 1, SENT_ROWS, False)
+    received_y = ring_start(sent_y, Y)
+    kept_z = beam_sums(later(later_kernel, KEPT, True), weights, raw_pulses, 0, KEPT_ROWS, False)
+    kept_y = beam_sums(later(later_kernel, KEPT, False), weights, raw_pulses, 1, KEPT_ROWS, False)
     start = (lax.axis_index("sub") * SLAB).astype(jnp.int32).reshape(1)
-    tables = merge_tables(start, table)
+    tables = merge_tables(start, band_table(own_table(band_offsets, band_weights, beam_delay)))
+    pieces = ring_rest(kept_z, received_z, Z, Y)
+    pieces += ring_rest(kept_y, received_y, Y, Z)
     beams = compressed_beams(pieces, range_filter)
     image = lax.all_to_all(beams, "sub", 0, 0, tiled=True)
     left, right = from_neighbours(image)

time: 147 us -> 125 us (0.85)
  local copies, waits for them, and re-layouts: 20.7 us -> 0.9 us
  Pallas kernels: 37.3 us -> 31.6 us
  other arithmetic: 0.72 us -> 2.75 us
  starting transfers between devices: 41.9 us -> 43.5 us
    unnamed x66 -> x24, local copies, waits for them, and re-layouts: 19.9 us -> 0.07 us
    pallas_call x8 -> x6, Pallas kernels: 26.1 us -> 20.4 us  [the longest x4 19.5 us: beam_sums(): pl.pallas_call(kernel, grid=(steps,), in_specs=[fixed(small.shape), pl.Bl...]
    convert_element_type x0 -> x8, other arithmetic: none -> 2.72 us  [relay(): return (q.astype(F4) + received[:rows].astype(F4)).astype(BF)]
    ppermute x2, starting transfers between devices: 6.95 us -> 9.21 us  [from_neighbours(): lax.ppermute(array, BEAM_COMP, [(k, k + 1) for k in range(blocks - 1)])]
    all_to_all x1, waiting for transfers between devices: 3.41 us -> 1.92 us  [body(): image = lax.all_to_all(beams, 'sub', 0, 0, tiled=True)]
  transfers between devices with their start and end apart: 21 -> 21, of which waited for: 11 -> 10; matrix products, arithmetic and copies ran while one was open for 1% -> 3% of each run, Pallas kernels for 17% -> 15%
where the time goes in v1:
time: 125 us; the launch traced here: 124 us
  waiting for transfers between devices  44.5 us (36%)
  starting transfers between devices  43.5 us (35%)
  Pallas kernels  31.6 us (25%)
  other arithmetic  2.75 us (2%)
    ppermute x16, waiting for transfers between devices, ring_send(): return lax.ppermute(x, axis, [(k, (k + step) % RING) for k in range(RING)])  26.7 us
    ppermute x16, starting transfers between devices, ring_send(): return lax.ppermute(x, axis, [(k, (k + step) % RING) for k in range(RING)])  23.2 us
    pallas_call x4, Pallas kernels, beam_sums(): pl.pallas_call(kernel, grid=(steps,), in_specs=[fixed(small.shape), pl.Bl...  19.5 us
    ppermute x2, waiting for transfers between devices, from_neighbours(): lax.ppermute(array, BEAM_COMP, [(k + 1, k) for k in range(blocks - 1)])  10.1 us
    ppermute x2, starting transfers between devices, from_neighbours(): lax.ppermute(array, BEAM_COMP, [(k, k + 1) for k in range(blocks - 1)])  9.21 us
    ppermute x2, starting transfers between devices, from_neighbours(): lax.ppermute(array, BEAM_COMP, [(k + 1, k) for k in range(blocks - 1)])  6.86 us
    pallas_call x1, Pallas kernels, merge(): pl.pallas_call(merge_kernel, grid=(SLAB // COLS,), in_specs=[image] * 3 +...  6.09 us
    ppermute x2, waiting for transfers between devices, from_neighbours(): lax.ppermute(array, BEAM_COMP, [(k, k + 1) for k in range(blocks - 1)])  5.77 us
  transfers between devices with their start and end apart: 21, of which 10 were waited for; matrix products, arithmetic and copies ran while one was open for 3% of the time, Pallas kernels for 15%

profile of v1, /device:TPU:16, one launch (start us, length us, event | category | flops | bytes accessed | tf_op | source)
XLA Modules:
  0.0 123.6 jit_solution(11880386550543624503)
XLA Ops:
  0.0 5.1 %beam_sums.4 = (bf16[64,8192]{1,0:T(8,128)(2,1)}, bf16[64,8192]{1,0:T(8,128)(2,1)}, f32[2,128,256]{2,1,0:T(8,128)S(1)}) custom-call(f32[128,128]{1,0:T(8,128)} %angle_ref.1, bf16[128,2,16384]{2,1,0:T(2,128)(2,1)} %raw_ref.7), custom_call_target="tpu_custom_call" | custom-call | tf_op jit(solution)/shard_map/beam_sums/pallas_call | solution.py:115
  5.1 1.9 %collective-permute-start = (bf16[64,8192]{1,0:T(8,128)(2,1)}, bf16[64,8192]{1,0:T(8,128)(2,1)S(1)}, u32[]{:S(2)}, u32[]{:S(2)}) collective-permute-start(bf16[64,8192]{1,0:T(8,128)(2,1)} %get-tuple-element.33), channel_id=1, source_target_pairs={{0,2},{2,4},{4,6},{6,0},{1,3},{3,5},{5,7},{7,1},{8,10},{10,12},{12... | collective-permute-start | bytes 3145736 | tf_op jit(solution)/shard_map/ppermute | solution.py:57
  7.1 2.1 %collective-permute-start.1 = (bf16[64,8192]{1,0:T(8,128)(2,1)}, bf16[64,8192]{1,0:T(8,128)(2,1)S(1)}, u32[]{:S(2)}, u32[]{:S(2)}) collective-permute-start(bf16[64,8192]{1,0:T(8,128)(2,1)} %get-tuple-element.34), channel_id=1, source_target_pairs={{0,6},{2,0},{4,2},{6,4},{1,7},{3,1},{5,3},{7,5},{8,14},{10,8},{12,... | collective-permute-start | bytes 3145736 | tf_op jit(solution)/shard_map/ppermute | solution.py:57
  9.2 4.8 %beam_sums.7 = (bf16[64,8192]{1,0:T(8,128)(2,1)}, bf16[64,8192]{1,0:T(8,128)(2,1)}) custom-call(f32[2,128,256]{2,1,0:T(8,128)S(1)} %get-tuple-element.31.weights, bf16[128,2,16384]{2,1,0:T(2,128)(2,1)} %raw_ref.7), custom_call_target="tpu_custom_call" | custom-call | tf_op jit(solution)/shard_map/beam_sums/pallas_call | solution.py:115
  13.9 1.3 %collective-permute-start.8 = (bf16[64,8192]{1,0:T(8,128)(2,1)}, bf16[64,8192]{1,0:T(8,128)(2,1)S(1)}, u32[]{:S(2)}, u32[]{:S(2)}) collective-permute-start(bf16[64,8192]{1,0:T(8,128)(2,1)} %get-tuple-element.43), channel_id=1, source_target_pairs={{0,1},{1,8},{8,9},{9,0},{2,3},{3,10},{10,11},{11,2},{4,5},{5,12},{... | collective-permute-start | bytes 3145736 | tf_op jit(solution)/shard_map/ppermute | solution.py:57
  16.0 4.7 %beam_sums.5 = (bf16[32,8192]{1,0:T(8,128)(2,1)}, bf16[32,8192]{1,0:T(8,128)(2,1)}, bf16[64,8192]{1,0:T(8,128)(2,1)}) custom-call(f32[2,128,256]{2,1,0:T(8,128)S(1)} %get-tuple-element.31.weights, bf16[128,2,16384]{2,1,0:T(2,128)(2,1)} %raw_ref.7), custom_call_target="tpu_custom_call" | custom-call | tf_op jit(solution)/shard_map/beam_sums/pallas_call | solution.py:115
  20.7 4.9 %beam_sums.6 = (bf16[32,8192]{1,0:T(8,128)(2,1)}, bf16[32,8192]{1,0:T(8,128)(2,1)}, bf16[64,8192]{1,0:T(8,128)(2,1)}) custom-call(f32[2,128,256]{2,1,0:T(8,128)S(1)} %get-tuple-element.31.weights, bf16[128,2,16384]{2,1,0:T(2,128)(2,1)} %raw_ref.7), custom_call_target="tpu_custom_call" | custom-call | tf_op jit(solution)/shard_map/beam_sums/pallas_call | solution.py:115
  25.6 6.9 %collective-permute-done.p1 = bf16[64,8192]{1,0:T(8,128)(2,1)S(1)} collective-permute-done((bf16[64,8192]{1,0:T(8,128)(2,1)}, bf16[64,8192]{1,0:T(8,128)(2,1)S(1)}, u32[]{:S(2)}, u32[]{:S(2)}) %collective-permute-start) | collective-permute-done | bytes 1048608 | tf_op jit(solution)/shard_map/ppermute | solution.py:57
  32.9 3.3 %collective-permute-start.3 = (bf16[32,8192]{1,0:T(8,128)(2,1)S(1)}, bf16[32,8192]{1,0:T(8,128)(2,1)S(1)}, u32[]{:S(2)}, u32[]{:S(2)}) collective-permute-start(bf16[32,8192]{1,0:T(8,128)(2,1)S(1)} %add_convert_fusion.2), channel_id=1, source_target_pairs={{0,6},{2,0},{4,2},{6,4},{1,7},{3,1},{5,3},{7,5},{8,14},{10,8},{12,... | collective-permute-start | bytes 1572872 | tf_op jit(solution)/shard_map/ppermute | solution.py:57
  36.2 2.6 %collective-permute-done.8.p1 = bf16[64,8192]{1,0:T(8,128)(2,1)S(1)} collective-permute-done((bf16[64,8192]{1,0:T(8,128)(2,1)}, bf16[64,8192]{1,0:T(8,128)(2,1)S(1)}, u32[]{:S(2)}, u32[]{:S(2)}) %collective-permute-start.8) | collective-permute-done | bytes 1048608 | tf_op jit(solution)/shard_map/ppermute | solution.py:57
  40.0 1.4 %collective-permute-start.10 = (bf16[32,8192]{1,0:T(8,128)(2,1)S(1)}, bf16[32,8192]{1,0:T(8,128)(2,1)S(1)}, u32[]{:S(2)}, u32[]{:S(2)}) collective-permute-start(bf16[32,8192]{1,0:T(8,128)(2,1)S(1)} %add_convert_fusion.1), channel_id=1, source_target_pairs={{0,1},{1,8},{8,9},{9,0},{2,3},{3,10},{10,11},{11,2},{4,5},{5,12},{... | collective-permute-start | bytes 1572872 | tf_op jit(solution)/shard_map/ppermute | solution.py:57
  41.3 1.2 add_convert_fusion
  43.3 3.7 %collective-permute-done.2.p2 = bf16[32,8192]{1,0:T(8,128)(2,1)S(1)} collective-permute-done((bf16[32,8192]{1,0:T(8,128)(2,1)S(1)}, bf16[32,8192]{1,0:T(8,128)(2,1)S(1)}, u32[]{:S(2)}, u32[]{:S(2)}) %collective-permute-start.2) | collective-permute-done | bytes 524320 | tf_op jit(solution)/shard_map/ppermute | solution.py:57
  47.5 1.4 %collective-permute-start.4 = (bf16[16,8192]{1,0:T(8,128)(2,1)S(1)}, bf16[16,8192]{1,0:T(8,128)(2,1)S(1)}, u32[]{:S(2)}, u32[]{:S(2)}) collective-permute-start(bf16[16,8192]{1,0:T(8,128)(2,1)S(1)} %get-tuple-element.38), channel_id=1, source_target_pairs={{0,1},{1,8},{8,9},{9,0},{2,3},{3,10},{10,11},{11,2},{4,5},{5,12},{... | collective-permute-start | bytes 786440 | tf_op jit(solution)/shard_map/ppermute | solution.py:57
  49.6 5.3 %collective-permute-done.10.p2 = bf16[32,8192]{1,0:T(8,128)(2,1)S(1)} collective-permute-done((bf16[32,8192]{1,0:T(8,128)(2,1)S(1)}, bf16[32,8192]{1,0:T(8,128)(2,1)S(1)}, u32[]{:S(2)}, u32[]{:S(2)}) %collective-permute-start.10) | collective-permute-done | bytes 524320 | tf_op jit(solution)/shard_map/ppermute | solution.py:57
  54.9 2.5 %collective-permute-done.11.m2 = bf16[32,8192]{1,0:T(8,128)(2,1)S(1)} collective-permute-done((bf16[32,8192]{1,0:T(8,128)(2,1)S(1)}, bf16[32,8192]{1,0:T(8,128)(2,1)S(1)}, u32[]{:S(2)}, u32[]{:S(2)}) %collective-permute-start.11) | collective-permute-done | bytes 524320 | tf_op jit(solution)/shard_map/ppermute | solution.py:57
  58.0 3.2 %collective-permute-start.13 = (bf16[16,8192]{1,0:T(8,128)(2,1)S(1)}, bf16[16,8192]{1,0:T(8,128)(2,1)S(1)}, u32[]{:S(2)}, u32[]{:S(2)}) collective-permute-start(bf16[16,8192]{1,0:T(8,128)(2,1)S(1)} %get-tuple-element.49), channel_id=1, source_target_pairs={{0,6},{2,0},{4,2},{6,4},{1,7},{3,1},{5,3},{7,5},{8,14},{10,8},{12,... | collective-permute-start | bytes 786440 | tf_op jit(solution)/shard_map/ppermute | solution.py:57
  61.2 2.8 %collective-permute-start.6 = (bf16[8,8192]{1,0:T(8,128)(2,1)S(1)}, bf16[8,8192]{1,0:T(8,128)(2,1)S(1)}, u32[]{:S(2)}, u32[]{:S(2)}) collective-permute-start(bf16[8,8192]{1,0:T(8,128)(2,1)S(1)} %add_convert_fusion.7), channel_id=1, source_target_pairs={{0,1},{1,8},{8,9},{9,0},{2,3},{3,10},{10,11},{11,2},{4,5},{5,12},{... | collective-permute-start | bytes 393224 | tf_op jit(solution)/shard_map/ppermute | solution.py:57
  64.1 2.8 %collective-permute-done.12.refs_6_ = bf16[16,8192]{1,0:T(8,128)(2,1)S(1)} collective-permute-done((bf16[16,8192]{1,0:T(8,128)(2,1)S(1)}, bf16[16,8192]{1,0:T(8,128)(2,1)S(1)}, u32[]{:S(2)}, u32[]{:S(2)}) %collective-permute-start.12) | collective-permute-done | bytes 262176 | tf_op jit(solution)/shard_map/ppermute | solution.py:57
  67.1 3.3 %collective-permute-start.15 = (bf16[8,8192]{1,0:T(8,128)(2,1)S(1)}, bf16[8,8192]{1,0:T(8,128)(2,1)S(1)}, u32[]{:S(2)}, u32[]{:S(2)}) collective-permute-start(bf16[8,8192]{1,0:T(8,128)(2,1)S(1)} %add_convert_fusion.4), channel_id=1, source_target_pairs={{0,6},{2,0},{4,2},{6,4},{1,7},{3,1},{5,3},{7,5},{8,14},{10,8},{12,... | collective-permute-start | bytes 393224 | tf_op jit(solution)/shard_map/ppermute | solution.py:57
  70.4 2.8 %collective-permute-done.14.refs_8_ = bf16[8,8192]{1,0:T(8,128)(2,1)S(1)} collective-permute-done((bf16[8,8192]{1,0:T(8,128)(2,1)S(1)}, bf16[8,8192]{1,0:T(8,128)(2,1)S(1)}, u32[]{:S(2)}, u32[]{:S(2)}) %collective-permute-start.14) | collective-permute-done | bytes 131104 | tf_op jit(solution)/shard_map/ppermute | solution.py:57
  73.3 2.1 %compressed_beams.1 = bf16[8,16,2048]{2,1,0:T(8,128)(2,1)} custom-call(f32[16,8192]{1,0:T(8,128)S(1)} %get-tuple-element.37.refs_0_, bf16[16,8192]{1,0:T(8,128)(2,1)S(1)} %collective-permute-done.4.refs_1_, bf16[16,8192]{1,0:T(8,128)(2,1)S(1)} %collective-permute-done.5.refs_2_, bf16[8,8192]{1,0:T(8,128)(2,1)S(1)} %collective-permute-done.6.refs_3_, ...), custom_call_target="tpu_custom_call" | custom-call | tf_op jit(solution)/shard_map/compressed_beams/pallas_call | solution.py:213
  75.3 4.3 %all-to-all-start = ((bf16[8,16,2048]{2,1,0:T(8,128)(2,1)}), bf16[8,16,2048]{2,1,0:T(8,128)(2,1)S(1)}, u32[]{:S(2)}, u32[]{:S(2)}) async-start(bf16[8,16,2048]{2,1,0:T(8,128)(2,1)} %compressed_beams.1), calls=%async_computation | async-start | bytes 1048576 | tf_op jit(solution)/shard_map/all_to_all | solution.py:409
  79.7 4.6 %collective-permute-start.18 = (f32[2,112,10]{1,0,2:T(2,128)S(1)}, f32[2,112,10]{1,0,2:T(2,128)S(1)}, u32[]{:S(2)}, u32[]{:S(2)}) collective-permute-start(f32[2,112,10]{1,0,2:T(2,128)S(1)} %pad_maximum_fusion), channel_id=1, source_target_pairs={{0,1},{1,2},{2,3},{3,4},{4,5},{5,6},{6,7},{7,8},{8,9},{9,10},{10,1... | collective-permute-start | bytes 26888 | tf_op jit(solution)/shard_map/ppermute | solution.py:356
  84.3 3.3 %collective-permute-start.19 = (f32[2,112,10]{1,0,2:T(2,128)S(1)}, f32[2,112,10]{1,0,2:T(2,128)S(1)}, u32[]{:S(2)}, u32[]{:S(2)}) collective-permute-start(f32[2,112,10]{1,0,2:T(2,128)S(1)} %pad_maximum_fusion), channel_id=1, source_target_pairs={{1,0},{2,1},{3,2},{4,3},{5,4},{6,5},{7,6},{8,7},{9,8},{10,9},{11,1... | collective-permute-start | bytes 26888 | tf_op jit(solution)/shard_map/ppermute | solution.py:357
  88.1 1.9 %all-to-all-done.own = bf16[8,16,2048]{2,1,0:T(8,128)(2,1)S(1)} async-done(((bf16[8,16,2048]{2,1,0:T(8,128)(2,1)}), bf16[8,16,2048]{2,1,0:T(8,128)(2,1)S(1)}, u32[]{:S(2)}, u32[]{:S(2)}) %all-to-all-start) | async-done | bytes 524320 | tf_op jit(solution)/shard_map/all_to_all | solution.py:409
  90.0 4.6 %collective-permute-start.16 = (bf16[8,16,2048]{2,1,0:T(8,128)(2,1)S(1)}, bf16[8,16,2048]{2,1,0:T(8,128)(2,1)S(1)}, u32[]{:S(2)}, u32[]{:S(2)}) collective-permute-start(bf16[8,16,2048]{2,1,0:T(8,128)(2,1)S(1)} %all-to-all-done.own), channel_id=1, source_target_pairs={{0,1},{1,2},{2,3},{3,4},{4,5},{5,6},{6,7},{7,8},{8,9},{9,10},{10,1... | collective-permute-start | bytes 1572872 | tf_op jit(solution)/shard_map/ppermute | solution.py:356
  94.6 3.5 %collective-permute-start.17 = (bf16[8,16,2048]{2,1,0:T(8,128)(2,1)S(1)}, bf16[8,16,2048]{2,1,0:T(8,128)(2,1)S(1)}, u32[]{:S(2)}, u32[]{:S(2)}) collective-permute-start(bf16[8,16,2048]{2,1,0:T(8,128)(2,1)S(1)} %all-to-all-done.own), channel_id=1, source_target_pairs={{1,0},{2,1},{3,2},{4,3},{5,4},{6,5},{7,6},{8,7},{9,8},{10,9},{11,1... | collective-permute-start | bytes 1572872 | tf_op jit(solution)/shard_map/ppermute | solution.py:357
  98.6 3.0 %merge_tables.1 = (f32[416,128]{1,0:T(8,128)S(1)}, f32[4,416,128]{2,1,0:T(8,128)S(1)}, f32[4,416,128]{2,1,0:T(8,128)S(1)}, f32[416,128]{1,0:T(8,128)S(1)}, f32[416,128]{1,0:T(8,128)S(1)}) custom-call(s32[1]{0:T(128)} %bitcast.start_ref, f32[416,10]{1,0:T(8,128)S(1)} %bitcast.11), custom_call_target="tpu_custom_call" | custom-call | tf_op jit(solution)/shard_map/merge_tables/pallas_call | solution.py:260
  101.7 5.8 %collective-permute-done.16.left = bf16[8,16,2048]{2,1,0:T(8,128)(2,1)S(1)} collective-permute-done((bf16[8,16,2048]{2,1,0:T(8,128)(2,1)S(1)}, bf16[8,16,2048]{2,1,0:T(8,128)(2,1)S(1)}, u32[]{:S(2)}, u32[]{:S(2)}) %collective-permute-start.16) | collective-permute-done | bytes 524320 | tf_op jit(solution)/shard_map/ppermute | solution.py:356
  107.4 10.1 %collective-permute-done.17.right = bf16[8,16,2048]{2,1,0:T(8,128)(2,1)S(1)} collective-permute-done((bf16[8,16,2048]{2,1,0:T(8,128)(2,1)S(1)}, bf16[8,16,2048]{2,1,0:T(8,128)(2,1)S(1)}, u32[]{:S(2)}, u32[]{:S(2)}) %collective-permute-start.17) | collective-permute-done | bytes 524320 | tf_op jit(solution)/shard_map/ppermute | solution.py:357
  117.5 6.1 %merge.1 = f32[64,2,2048]{2,1,0:T(2,128)} custom-call(bf16[8,16,2048]{2,1,0:T(8,128)(2,1)S(1)} %collective-permute-done.16.left, bf16[8,16,2048]{2,1,0:T(8,128)(2,1)S(1)} %all-to-all-done.own, bf16[8,16,2048]{2,1,0:T(8,128)(2,1)S(1)} %collective-permute-done.17.right, f32[416,128]{1,0:T(8,128)S(1)} %get-tuple-element.52.matrix, ...), custom_call_target="tpu_custom_call" | custom-call | tf_op jit(solution)/shard_map/merge/pallas_call | solution.py:343
  (63 shorter events, 6.0 us)
Async XLA Ops:
  5.1 27.4 %collective-permute-start = (bf16[64,8192]{1,0:T(8,128)(2,1)}, bf16[64,8192]{1,0:T(8,128)(2,1)S(1)}, u32[]{:S(2)}, u32[]{:S(2)}) collective-permute-start(bf16[64,8192]{1,0:T(8,128)(2,1)} %get-tuple-element.33), channel_id=1, source_target_pairs={{0,2},{2,4},{4,6},{6,0},{1,3},{3,5},{5,7},{7,1},{8,10},{10,12},{12... | collective-permute-start | bytes 3145736 | tf_op jit(solution)/shard_map/ppermute | solution.py:57
  7.1 25.7 %collective-permute-start.1 = (bf16[64,8192]{1,0:T(8,128)(2,1)}, bf16[64,8192]{1,0:T(8,128)(2,1)S(1)}, u32[]{:S(2)}, u32[]{:S(2)}) collective-permute-start(bf16[64,8192]{1,0:T(8,128)(2,1)} %get-tuple-element.34), channel_id=1, source_target_pairs={{0,6},{2,0},{4,2},{6,4},{1,7},{3,1},{5,3},{7,5},{8,14},{10,8},{12,... | collective-permute-start | bytes 3145736 | tf_op jit(solution)/shard_map/ppermute | solution.py:57
  13.9 24.8 %collective-permute-start.8 = (bf16[64,8192]{1,0:T(8,128)(2,1)}, bf16[64,8192]{1,0:T(8,128)(2,1)S(1)}, u32[]{:S(2)}, u32[]{:S(2)}) collective-permute-start(bf16[64,8192]{1,0:T(8,128)(2,1)} %get-tuple-element.43), channel_id=1, source_target_pairs={{0,1},{1,8},{8,9},{9,0},{2,3},{3,10},{10,11},{11,2},{4,5},{5,12},{... | collective-permute-start | bytes 3145736 | tf_op jit(solution)/shard_map/ppermute | solution.py:57
  15.2 26.1 %collective-permute-start.9 = (bf16[64,8192]{1,0:T(8,128)(2,1)}, bf16[64,8192]{1,0:T(8,128)(2,1)S(1)}, u32[]{:S(2)}, u32[]{:S(2)}) collective-permute-start(bf16[64,8192]{1,0:T(8,128)(2,1)} %get-tuple-element.44), channel_id=1, source_target_pairs={{0,9},{1,0},{8,1},{9,8},{2,11},{3,2},{10,3},{11,10},{4,13},{5,4},{... | collective-permute-start | bytes 3145736 | tf_op jit(solution)/shard_map/ppermute | solution.py:57
  20.7 11.9 %copy-start.5 = (bf16[32,8192]{1,0:T(8,128)(2,1)S(1)}, bf16[32,8192]{1,0:T(8,128)(2,1)}, u32[]{:S(2)}) copy-start(bf16[32,8192]{1,0:T(8,128)(2,1)} %get-tuple-element.35) | copy-start | bytes 1572868
  20.7 12.1 %copy-start.4 = (bf16[32,8192]{1,0:T(8,128)(2,1)S(1)}, bf16[32,8192]{1,0:T(8,128)(2,1)}, u32[]{:S(2)}) copy-start(bf16[32,8192]{1,0:T(8,128)(2,1)} %get-tuple-element.36) | copy-start | bytes 1572868
  20.7 26.4 %copy-start.1 = (bf16[64,8192]{1,0:T(8,128)(2,1)S(1)}, bf16[64,8192]{1,0:T(8,128)(2,1)}, u32[]{:S(2)}) copy-start(bf16[64,8192]{1,0:T(8,128)(2,1)} %get-tuple-element.32.own) | copy-start | bytes 3145732
  25.6 31.8 %copy-start = (bf16[64,8192]{1,0:T(8,128)(2,1)S(1)}, bf16[64,8192]{1,0:T(8,128)(2,1)}, u32[]{:S(2)}) copy-start(bf16[64,8192]{1,0:T(8,128)(2,1)} %get-tuple-element.42.own) | copy-start | bytes 3145732
  25.6 44.8 %copy-start.6 = (f32[2,16384]{1,0:T(2,128)S(1)}, f32[2,16384]{1,0:T(2,128)}, u32[]{:S(2)}) copy-start(f32[2,16384]{1,0:T(2,128)} %param.10) | copy-start | bytes 393220
  25.6 47.6 %copy-start.2 = (bf16[256,256]{1,0:T(8,128)(2,1)S(1)}, bf16[256,256]{1,0:T(8,128)(2,1)}, u32[]{:S(2)}) copy-start(bf16[256,256]{1,0:T(8,128)(2,1)} %constant.15.clone.refs_10_) | copy-start | bytes 393220
  25.6 47.6 %copy-start.3 = (f32[2,128,128]{2,1,0:T(8,128)S(1)}, f32[2,128,128]{2,1,0:T(8,128)}, u32[]{:S(2)}) copy-start(f32[2,128,128]{2,1,0:T(8,128)} %constant.16.clone.refs_11_) | copy-start | bytes 393220
  32.7 14.4 %collective-permute-start.2 = (bf16[32,8192]{1,0:T(8,128)(2,1)S(1)}, bf16[32,8192]{1,0:T(8,128)(2,1)S(1)}, u32[]{:S(2)}, u32[]{:S(2)}) collective-permute-start(bf16[32,8192]{1,0:T(8,128)(2,1)S(1)} %add_convert_fusion.3), channel_id=1, source_target_pairs={{0,2},{2,4},{4,6},{6,0},{1,3},{3,5},{5,7},{7,1},{8,10},{10,12},{12... | collective-permute-start | bytes 1572872 | tf_op jit(solution)/shard_map/ppermute | solution.py:57
  32.9 14.2 %collective-permute-start.3 = (bf16[32,8192]{1,0:T(8,128)(2,1)S(1)}, bf16[32,8192]{1,0:T(8,128)(2,1)S(1)}, u32[]{:S(2)}, u32[]{:S(2)}) collective-permute-start(bf16[32,8192]{1,0:T(8,128)(2,1)S(1)} %add_convert_fusion.2), channel_id=1, source_target_pairs={{0,6},{2,0},{4,2},{6,4},{1,7},{3,1},{5,3},{7,5},{8,14},{10,8},{12,... | collective-permute-start | bytes 1572872 | tf_op jit(solution)/shard_map/ppermute | solution.py:57
  39.9 39.7 %copy-start.8 = (f32[2,112,8]{1,2,0:T(8,128)S(1)}, f32[2,112,8]{1,2,0:T(8,128)}, u32[]{:S(2)}) copy-start(f32[2,112,8]{1,2,0:T(8,128)} %param.13) | copy-start | bytes 21508
  40.0 39.7 %copy-start.10 = (s32[2,112]{1,0:T(2,128)S(1)}, s32[2,112]{1,0:T(2,128)}, u32[]{:S(2)}) copy-start(s32[2,112]{1,0:T(2,128)} %param.12) | copy-start | bytes 2692
  40.0 39.7 %copy-start.9 = (f32[2,112]{1,0:T(2,128)S(1)}, f32[2,112]{1,0:T(2,128)}, u32[]{:S(2)}) copy-start(f32[2,112]{1,0:T(2,128)} %param.14) | copy-start | bytes 2692
  40.0 14.9 %collective-permute-start.10 = (bf16[32,8192]{1,0:T(8,128)(2,1)S(1)}, bf16[32,8192]{1,0:T(8,128)(2,1)S(1)}, u32[]{:S(2)}, u32[]{:S(2)}) collective-permute-start(bf16[32,8192]{1,0:T(8,128)(2,1)S(1)} %add_convert_fusion.1), channel_id=1, source_target_pairs={{0,1},{1,8},{8,9},{9,0},{2,3},{3,10},{10,11},{11,2},{4,5},{5,12},{... | collective-permute-start | bytes 1572872 | tf_op jit(solution)/shard_map/ppermute | solution.py:57
  41.3 57.1 %copy-start.7 = (f32[208,10]{0,1:T(8,128)S(1)}, f32[208,10]{0,1:T(8,128)}, u32[]{:S(2)}) copy-start(f32[208,10]{0,1:T(8,128)} %constant.17) | copy-start | bytes 24964
  42.5 14.9 %collective-permute-start.11 = (bf16[32,8192]{1,0:T(8,128)(2,1)S(1)}, bf16[32,8192]{1,0:T(8,128)(2,1)S(1)}, u32[]{:S(2)}, u32[]{:S(2)}) collective-permute-start(bf16[32,8192]{1,0:T(8,128)(2,1)S(1)} %add_convert_fusion), channel_id=1, source_target_pairs={{0,9},{1,0},{8,1},{9,8},{2,11},{3,2},{10,3},{11,10},{4,13},{5,4},{... | collective-permute-start | bytes 1572872 | tf_op jit(solution)/shard_map/ppermute | solution.py:57
  47.5 13.7 %collective-permute-start.4 = (bf16[16,8192]{1,0:T(8,128)(2,1)S(1)}, bf16[16,8192]{1,0:T(8,128)(2,1)S(1)}, u32[]{:S(2)}, u32[]{:S(2)}) collective-permute-start(bf16[16,8192]{1,0:T(8,128)(2,1)S(1)} %get-tuple-element.38), channel_id=1, source_target_pairs={{0,1},{1,8},{8,9},{9,0},{2,3},{3,10},{10,11},{11,2},{4,5},{5,12},{... | collective-permute-start | bytes 786440 | tf_op jit(solution)/shard_map/ppermute | solution.py:57
  48.9 15.1 %collective-permute-start.5 = (bf16[16,8192]{1,0:T(8,128)(2,1)S(1)}, bf16[16,8192]{1,0:T(8,128)(2,1)S(1)}, u32[]{:S(2)}, u32[]{:S(2)}) collective-permute-start(bf16[16,8192]{1,0:T(8,128)(2,1)S(1)} %get-tuple-element.39), channel_id=1, source_target_pairs={{0,9},{1,0},{8,1},{9,8},{2,11},{3,2},{10,3},{11,10},{4,13},{5,4},{... | collective-permute-start | bytes 786440 | tf_op jit(solution)/shard_map/ppermute | solution.py:57
  57.9 9.1 %collective-permute-start.12 = (bf16[16,8192]{1,0:T(8,128)(2,1)S(1)}, bf16[16,8192]{1,0:T(8,128)(2,1)S(1)}, u32[]{:S(2)}, u32[]{:S(2)}) collective-permute-start(bf16[16,8192]{1,0:T(8,128)(2,1)S(1)} %get-tuple-element.48), channel_id=1, source_target_pairs={{0,2},{2,4},{4,6},{6,0},{1,3},{3,5},{5,7},{7,1},{8,10},{10,12},{12... | collective-permute-start | bytes 786440 | tf_op jit(solution)/shard_map/ppermute | solution.py:57
  58.0 9.1 %collective-permute-start.13 = (bf16[16,8192]{1,0:T(8,128)(2,1)S(1)}, bf16[16,8192]{1,0:T(8,128)(2,1)S(1)}, u32[]{:S(2)}, u32[]{:S(2)}) collective-permute-start(bf16[16,8192]{1,0:T(8,128)(2,1)S(1)} %get-tuple-element.49), channel_id=1, source_target_pairs={{0,6},{2,0},{4,2},{6,4},{1,7},{3,1},{5,3},{7,5},{8,14},{10,8},{12,... | collective-permute-start | bytes 786440 | tf_op jit(solution)/shard_map/ppermute | solution.py:57
  61.2 9.2 %collective-permute-start.6 = (bf16[8,8192]{1,0:T(8,128)(2,1)S(1)}, bf16[8,8192]{1,0:T(8,128)(2,1)S(1)}, u32[]{:S(2)}, u32[]{:S(2)}) collective-permute-start(bf16[8,8192]{1,0:T(8,128)(2,1)S(1)} %add_convert_fusion.7), channel_id=1, source_target_pairs={{0,1},{1,8},{8,9},{9,0},{2,3},{3,10},{10,11},{11,2},{4,5},{5,12},{... | collective-permute-start | bytes 393224 | tf_op jit(solution)/shard_map/ppermute | solution.py:57
  64.1 6.4 %collective-permute-start.7 = (bf16[8,8192]{1,0:T(8,128)(2,1)S(1)}, bf16[8,8192]{1,0:T(8,128)(2,1)S(1)}, u32[]{:S(2)}, u32[]{:S(2)}) collective-permute-start(bf16[8,8192]{1,0:T(8,128)(2,1)S(1)} %add_convert_fusion.6), channel_id=1, source_target_pairs={{0,9},{1,0},{8,1},{9,8},{2,11},{3,2},{10,3},{11,10},{4,13},{5,4},{... | collective-permute-start | bytes 393224 | tf_op jit(solution)/shard_map/ppermute | solution.py:57
  67.0 6.2 %collective-permute-start.14 = (bf16[8,8192]{1,0:T(8,128)(2,1)S(1)}, bf16[8,8192]{1,0:T(8,128)(2,1)S(1)}, u32[]{:S(2)}, u32[]{:S(2)}) collective-permute-start(bf16[8,8192]{1,0:T(8,128)(2,1)S(1)} %add_convert_fusion.5), channel_id=1, source_target_pairs={{0,2},{2,4},{4,6},{6,0},{1,3},{3,5},{5,7},{7,1},{8,10},{10,12},{12... | collective-permute-start | bytes 393224 | tf_op jit(solution)/shard_map/ppermute | solution.py:57
  67.1 6.1 %collective-permute-start.15 = (bf16[8,8192]{1,0:T(8,128)(2,1)S(1)}, bf16[8,8192]{1,0:T(8,128)(2,1)S(1)}, u32[]{:S(2)}, u32[]{:S(2)}) collective-permute-start(bf16[8,8192]{1,0:T(8,128)(2,1)S(1)} %add_convert_fusion.4), channel_id=1, source_target_pairs={{0,6},{2,0},{4,2},{6,4},{1,7},{3,1},{5,3},{7,5},{8,14},{10,8},{12,... | collective-permute-start | bytes 393224 | tf_op jit(solution)/shard_map/ppermute | solution.py:57
  75.3 14.7 %all-to-all-start = ((bf16[8,16,2048]{2,1,0:T(8,128)(2,1)}), bf16[8,16,2048]{2,1,0:T(8,128)(2,1)S(1)}, u32[]{:S(2)}, u32[]{:S(2)}) async-start(bf16[8,16,2048]{2,1,0:T(8,128)(2,1)} %compressed_beams.1), calls=%async_computation | async-start | bytes 1048576 | tf_op jit(solution)/shard_map/all_to_all | solution.py:409
  79.7 18.4 %collective-permute-start.18 = (f32[2,112,10]{1,0,2:T(2,128)S(1)}, f32[2,112,10]{1,0,2:T(2,128)S(1)}, u32[]{:S(2)}, u32[]{:S(2)}) collective-permute-start(f32[2,112,10]{1,0,2:T(2,128)S(1)} %pad_maximum_fusion), channel_id=1, source_target_pairs={{0,1},{1,2},{2,3},{3,4},{4,5},{5,6},{6,7},{7,8},{8,9},{9,10},{10,1... | collective-permute-start | bytes 26888 | tf_op jit(solution)/shard_map/ppermute | solution.py:356
  84.3 13.9 %collective-permute-start.19 = (f32[2,112,10]{1,0,2:T(2,128)S(1)}, f32[2,112,10]{1,0,2:T(2,128)S(1)}, u32[]{:S(2)}, u32[]{:S(2)}) collective-permute-start(f32[2,112,10]{1,0,2:T(2,128)S(1)} %pad_maximum_fusion), channel_id=1, source_target_pairs={{1,0},{2,1},{3,2},{4,3},{5,4},{6,5},{7,6},{8,7},{9,8},{10,9},{11,1... | collective-permute-start | bytes 26888 | tf_op jit(solution)/shard_map/ppermute | solution.py:357
  90.0 17.5 %collective-permute-start.16 = (bf16[8,16,2048]{2,1,0:T(8,128)(2,1)S(1)}, bf16[8,16,2048]{2,1,0:T(8,128)(2,1)S(1)}, u32[]{:S(2)}, u32[]{:S(2)}) collective-permute-start(bf16[8,16,2048]{2,1,0:T(8,128)(2,1)S(1)} %all-to-all-done.own), channel_id=1, source_target_pairs={{0,1},{1,2},{2,3},{3,4},{4,5},{5,6},{6,7},{7,8},{8,9},{9,10},{10,1... | collective-permute-start | bytes 1572872 | tf_op jit(solution)/shard_map/ppermute | solution.py:356
  94.6 22.9 %collective-permute-start.17 = (bf16[8,16,2048]{2,1,0:T(8,128)(2,1)S(1)}, bf16[8,16,2048]{2,1,0:T(8,128)(2,1)S(1)}, u32[]{:S(2)}, u32[]{:S(2)}) collective-permute-start(bf16[8,16,2048]{2,1,0:T(8,128)(2,1)S(1)} %all-to-all-done.own), channel_id=1, source_target_pairs={{1,0},{2,1},{3,2},{4,3},{5,4},{6,5},{7,6},{8,7},{9,8},{10,9},{11,1... | collective-permute-start | bytes 1572872 | tf_op jit(solution)/shard_map/ppermute | solution.py:357

commit v2 on v1

--- a/solution.py
+++ b/solution.py
@@ -18,9 +18,14 @@
 PSUB = 2048
 RING = 4
 HALF = NR // 2
-TILE = 2048
+READS = 4
+READ = NR // READS
+STEP = 2048
 SLAB = NR // 8
 COLS = 512
+PIECES = 2
+PIECE = SLAB // PIECES
+DIRECT = (True, True)
 SIDE = 208
 BEAM_COMP = ("y_hi", "z", "y_lo")
 SUB_BEAM_COMP = ("sub", "y_hi", "z", "y_lo")
@@ -72,7 +77,7 @@
     weights[1] = jnp.where(even, sine, cosine)
 
 
-def beam_products(weights, raw_ref, owners, z_first, outs):
+def beam_matrix(weights, owners, z_first):
     y = lax.axis_index("y_hi") * 2 + lax.axis_index("y_lo")
     z = lax.axis_index("z")
     picked = []
@@ -83,49 +88,86 @@
         start = pl.multiple_of(block * NB0, NB0)
         picked.append(weights[0, pl.ds(start, NB0), :])
         picked.append(weights[1, pl.ds(start, NB0), :])
-    matrix = jnp.concatenate(picked, 0).astype(BF)
-    raw = raw_ref[...].reshape(256, raw_ref.shape[2])
-    total = jnp.dot(matrix, raw, preferred_element_type=F4).astype(BF)
-    start = 0
-    for out in outs:
-        size = out.shape[0]
-        out[...] = total[start : start + size]
-        start += size
-
-
-def opening_kernel(angle_ref, raw_ref, plus, minus, weights):
-    @pl.when(pl.program_id(0) == 0)
-    def _():
-        steering_rows(angle_ref, weights)
-
-    beam_products(weights, raw_ref, SENT, True, (plus, minus))
-
-
-def later_kernel(owners, z_first, weights, raw_ref, *outs):
-    beam_products(weights, raw_ref, owners, z_first, outs)
-
-
-def beam_sums(kernel, small, raw, half, sizes, with_weights):
-    steps = HALF // TILE
-    weights = (2, 128, 256)
-
-    def fixed(shape):
-        return pl.BlockSpec(shape, lambda i: (0,) * len(shape))
-
-    return pl.pallas_call(
-        kernel,
-        grid=(steps,),
-        in_specs=[
-            fixed(small.shape),
-            pl.BlockSpec((128, 2, TILE), lambda i: (0, 0, i + half * steps)),
+    return jnp.concatenate(picked, 0).astype(BF)
+
+
+def opening_kernel(angle_ref, raw_ref, *refs):
+    outs, (weights, landed, angle_landed, sems) = refs[:4], refs[4:]
+    angle_read = pltpu.make_async_copy(angle_ref, angle_landed, sems.at[READS])
+    angle_read.start()
+
+    def read(k):
+        cols = pl.ds(k * READ, READ)
+        return pltpu.make_async_copy(raw_ref.at[:, :, cols], landed.at[k], sems.at[k])
+
+    for k in range(READS):
+        read(k).start()
+    angle_read.wait()
+    steering_rows(angle_landed, weights)
+    for k in range(READS):
+        half = k // (READS // 2)
+        matrix = beam_matrix(weights, SENT, half == 0)
+        read(k).wait()
+        base = k * READ - half * HALF
+        for part in range(READ // STEP):
+            raw = landed[k, :, :, part * STEP : (part + 1) * STEP].reshape(256, STEP)
+            total = jnp.dot(matrix, raw, preferred_element_type=F4).astype(BF)
+            cols = slice(base + part * STEP, base + (part + 1) * STEP)
+            outs[2 * half][:, cols] = total[:64]
+            outs[2 * half + 1][:, cols] = total[64:]
+
+
+def opening_sums(angles, raw):
+    vmem = pl.BlockSpec(memory_space=pltpu.VMEM)
+    outs = [jax.ShapeDtypeStruct((n, HALF), BF) for n in SENT_ROWS * 2]
+    outs += [jax.ShapeDtypeStruct((2, 128, 256), F4)]
+    results = pl.pallas_call(
+        opening_kernel,
+        in_specs=[pl.BlockSpec(memory_space=pltpu.HBM)] * 2,
+        out_specs=[vmem] * 5,
+        out_shape=outs,
+        scratch_shapes=[
+            pltpu.VMEM((READS, 128, 2, READ), BF),
+            pltpu.VMEM((128, 128), F4),
+            pltpu.SemaphoreType.DMA((READS + 1,)),
         ],
-        out_specs=[pl.BlockSpec((n, TILE), lambda i: (0, i)) for n in sizes]
-        + [fixed(weights)] * with_weights,
-        out_shape=[pltpu.HBM((n, HALF), BF) for n in sizes]
-        + [jax.ShapeDtypeStruct(weights, F4)] * with_weights,
-        compiler_params=params(16),
-        name="beam_sums",
-    )(small, pltpu.with_memory_space_constraint(raw, pltpu.HBM))
+        compiler_params=params(20),
+        name="opening_sums",
+    )(*(pltpu.with_memory_space_constraint(a, pltpu.HBM) for a in (angles, raw)))
+    return results[:2], results[2:4], results[4]
+
+
+def later_kernel(weights, raw_ref, *outs):
+    steps = pl.num_programs(0) // 2
+    for half in range(2):
+
+        @pl.when(pl.program_id(0) // steps == half)
+        def _():
+            matrix = beam_matrix(weights, KEPT, half == 0)
+            raw = raw_ref[...].reshape(256, READ)
+            total = jnp.dot(matrix, raw, preferred_element_type=F4).astype(BF)
+            step = lax.rem(pl.program_id(0), steps)
+            cols = pl.ds(pl.multiple_of(step * READ, READ), READ)
+            start = 0
+            for out in outs[3 * half : 3 * half + 3]:
+                size = out.shape[0]
+                out[:, cols] = total[start : start + size]
+                start += size
+
+
+def later_sums(weights, raw):
+    vmem = pl.BlockSpec(memory_space=pltpu.VMEM)
+    outs = [jax.ShapeDtypeStruct((n, HALF), BF) for n in KEPT_ROWS * 2]
+    kept = pl.pallas_call(
+        later_kernel,
+        grid=(READS,),
+        in_specs=[vmem, pl.BlockSpec((128, 2, READ), lambda i: (0, 0, i))],
+        out_specs=[vmem] * 6,
+        out_shape=outs,
+        compiler_params=params(20),
+        name="later_sums",
+    )(weights, pltpu.with_memory_space_constraint(raw, pltpu.HBM))
+    return kept[:3], kept[3:]
 
 
 def relay(q, received):
@@ -224,12 +266,51 @@
     )
 
 
-def table_kernel(start_ref, table_ref, matrix, near_a, near_b, far_cos, far_sin):
-    rows = table_ref.shape[0]
+def sided(near, far, direct):
+    if direct:
+        return near, far
+    even = lax.axis_index("y_lo") == 0
+    return jnp.where(even, far, near), jnp.where(even, near, far)
+
+
+def table_kernel(direct, start_ref, own_ref, near_ref, far_ref, *refs):
+    matrix, near_a, near_b, far_cos, far_sin, lines = refs
+
+    def columns(fields):
+        padded = jnp.concatenate([fields, jnp.zeros((112, 256), F4)], 0)
+        return jnp.concatenate([padded[:, :128].T, padded[:, 128:].T], 0)
+
+    def joined(ref):
+        parts = ref[0].astype(F4)
+        return parts[:, :256] + parts[:, 256:512] + parts[:, 512:768]
+
+    left, right = sided(joined(near_ref), joined(far_ref), direct)
+    own, left, right = columns(own_ref[...]), columns(left), columns(right)
+
+    def piece(source, side, first, count, shift):
+        rows = source[side * 128 + first : side * 128 + first + count]
+        field = lax.broadcasted_iota(jnp.int32, rows.shape, 1)
+        return rows + jnp.where(field == 0, float(shift), 0.0)
+
+    for side in range(2):
+        row = side * SIDE
+        for source, first, count, shift in (
+            (left, 8, 8, 0),
+            (own, 0, 16, 8),
+            (right, 0, 8, 16),
+            (left, 40, 8, -8),
+            (own, 16, 32, 8),
+            (right, 16, 8, 24),
+        ):
+            lines[row : row + count, :] = piece(source, side, first, count, shift)
+            row += count
+        for twin in range(2):
+            lines[pl.ds(row + twin, 64, stride=2), :] = piece(own, side, 48, 64, 8)
+    rows = 2 * SIDE
     lane = lax.broadcasted_iota(jnp.int32, (rows, 128), 1)
     row = lax.broadcasted_iota(jnp.int32, (rows, 128), 0) % SIDE
     lane_f = lane.astype(F4)
-    table = table_ref[...]
+    table = lines[...]
     offset = table[:, 0:1]
     total = jnp.zeros((rows, 128), F4)
     for tap in range(BAND):
@@ -251,20 +332,23 @@
         near_b[tile, :, 0:4] = value_b[:, lanes]
 
 
-def merge_tables(start, table):
-    rows = table.shape[0]
+def merge_tables(start, own, near, far, direct):
+    rows = 2 * SIDE
     tiles = SLAB // COLS
     one = jax.ShapeDtypeStruct((rows, 128), F4)
     many = jax.ShapeDtypeStruct((tiles, rows, 128), F4)
     vmem = pl.BlockSpec(memory_space=pltpu.VMEM)
+    packed = pl.BlockSpec((1, 16, PIECE), lambda i: (8, 0, 0))
     return pl.pallas_call(
-        table_kernel,
-        in_specs=[pl.BlockSpec(memory_space=pltpu.SMEM), vmem],
+        functools.partial(table_kernel, direct),
+        grid=(1,),
+        in_specs=[pl.BlockSpec(memory_space=pltpu.SMEM), vmem, packed, packed],
         out_specs=[vmem] * 5,
         out_shape=[one, many, many, one, one],
+        scratch_shapes=[pltpu.VMEM((rows, 128), F4)],
         compiler_params=params(12),
         name="merge_tables",
-    )(start, table)
+    )(start, own, near, far)
 
 
 def split_rows(matrix):
@@ -272,7 +356,8 @@
     return upper, (matrix - upper.astype(F4)).astype(BF)
 
 
-def merge_kernel(left, own, right, matrix, near_a, near_b, far_cos, far_sin, out):
+def merge_kernel(direct, near, own, far, matrix, near_a, near_b, far_cos, far_sin, *refs):
+    out = refs[-1]
     dot = functools.partial(jnp.dot, preferred_element_type=F4)
 
     def phases(first, count):
@@ -299,7 +384,8 @@
     zeros = jnp.zeros((8, COLS), F4)
     images = []
     for side in range(8):
-        parts = [ref[side].astype(F4) for ref in (left, own, right)]
+        left, right = sided(near[side].astype(F4), far[side].astype(F4), direct)
+        parts = (left, own[side].astype(F4), right)
         images.append(
             tuple(jnp.concatenate([p[8 * q : 8 * q + 8] for p in parts] + [zeros], 0) for q in (0, 1))
         )
@@ -334,45 +420,60 @@
     out[...] = total.reshape(64, 2, COLS)
 
 
-def merge(left, own, right, tables):
+def merge(near, own, far, tables, piece, direct, so_far):
     matrix, near_a, near_b, far_cos, far_sin = tables
     rows = matrix.shape[0]
+    steps = PIECE // COLS
+    first = piece * steps
     image = pl.BlockSpec((8, 16, COLS), lambda i: (0, 0, i))
     whole = pl.BlockSpec((rows, 128), lambda i: (0, 0))
-    tiled = pl.BlockSpec((1, rows, 128), lambda i: (i, 0, 0))
+    tiled = pl.BlockSpec((1, rows, 128), lambda i: (first + i, 0, 0))
     return pl.pallas_call(
-        merge_kernel,
-        grid=(SLAB // COLS,),
-        in_specs=[image] * 3 + [whole, tiled, tiled, whole, whole],
-        out_specs=pl.BlockSpec((64, 2, COLS), lambda i: (0, 0, i)),
+        functools.partial(merge_kernel, direct),
+        grid=(steps,),
+        in_specs=[image, pl.BlockSpec((8, 16, COLS), lambda i: (0, 0, first + i)), image]
+        + [whole, tiled, tiled, whole, whole]
+        + [pl.BlockSpec(memory_space=pl.ANY)] * len(so_far),
+        out_specs=pl.BlockSpec((64, 2, COLS), lambda i: (0, 0, first + i)),
         out_shape=jax.ShapeDtypeStruct((64, 2, SLAB), F4),
+        input_output_aliases={8: 0} if so_far else {},
         compiler_params=params(24),
         name="merge",
-    )(left, own, right, matrix, near_a, near_b, far_cos, far_sin)
-
-
-def from_neighbours(array):
+    )(near, own, far, matrix, near_a, near_b, far_cos, far_sin, *so_far)
+
+
+def from_neighbours(array, direct):
     blocks = lax.axis_size(BEAM_COMP)
-    left = lax.ppermute(array, BEAM_COMP, [(k, k + 1) for k in range(blocks - 1)])
-    right = lax.ppermute(array, BEAM_COMP, [(k + 1, k) for k in range(blocks - 1)])
-    return left, right
+    if direct:
+        steps = [(k, k + 1) for k in range(blocks - 1)]
+        left = lax.ppermute(array, BEAM_COMP, steps)
+        right = lax.ppermute(array, BEAM_COMP, [(b, a) for a, b in steps])
+        return left, right
+    near = lax.ppermute(array, BEAM_COMP, [(k, k ^ 1) for k in range(blocks)])
+    steps = [(k, k + 2 - 4 * (k % 2)) for k in range(blocks)]
+    far = lax.ppermute(near, BEAM_COMP, [(a, b) for a, b in steps if 0 <= b < blocks])
+    return near, far
 
 
 def own_table(band_offsets, band_weights, beam_delay):
-    return jnp.concatenate(
-        [band_offsets.astype(F4)[:, :, None], band_weights, beam_delay[:, :, None]], 2
+    fields = jnp.concatenate(
+        [
+            band_offsets.astype(F4)[None],
+            jnp.moveaxis(band_weights, 2, 0),
+            beam_delay[None],
+        ],
+        0,
     )
-
-
-def band_table(own):
-    left, right = from_neighbours(own)
-    pieces = [left[:, 8:16], own[:, 0:16], right[:, 0:8]]
-    pieces += [left[:, 40:48], own[:, 16:48], right[:, 16:24]]
-    pieces += [jnp.repeat(own[:, 48:112], 2, axis=1)]
-    base = np.zeros((1, SIDE, 10), np.float32)
-    spans = ((8, 0), (16, 8), (8, 16), (8, -8), (32, 8), (8, 24), (128, 8))
-    base[0, :, 0] = np.concatenate([np.full(n, v) for n, v in spans])
-    return (jnp.concatenate(pieces, 1) + base).reshape(2 * SIDE, 10)
+    return jnp.pad(fields, ((0, 6), (0, 0), (0, 16))).reshape(16, 256)
+
+
+def packed_table(table):
+    parts = []
+    for _ in range(3):
+        part = lax.reduce_precision(table, 8, 7)
+        parts.append(part.astype(BF))
+        table = table - part
+    return jnp.pad(jnp.concatenate(parts, 1), ((0, 0), (0, PIECE - 768)))[None]
 
 
 def ring_start(parts, first):
@@ -393,22 +494,28 @@
 
 
 def body(raw_pulses, range_filter, steer_angle, band_offsets, band_weights, beam_delay):
-    later = functools.partial
-    angles = pltpu.with_memory_space_constraint(steer_angle, pltpu.HBM)
-    *sent_z, weights = beam_sums(opening_kernel, angles, raw_pulses, 0, SENT_ROWS, True)
+    sent_z, sent_y, weights = opening_sums(steer_angle, raw_pulses)
     received_z = ring_start(sent_z, Z)
-    sent_y = beam_sums(later(later_kernel, SENT, False), weights, raw_pulses, 1, SENT_ROWS, False)
     received_y = ring_start(sent_y, Y)
-    kept_z = beam_sums(later(later_kernel, KEPT, True), weights, raw_pulses, 0, KEPT_ROWS, False)
-    kept_y = beam_sums(later(later_kernel, KEPT, False), weights, raw_pulses, 1, KEPT_ROWS, False)
+    table = own_table(band_offsets, band_weights, beam_delay)
+    packed = packed_table(table)
+    kept_z, kept_y = later_sums(weights, raw_pulses)
     start = (lax.axis_index("sub") * SLAB).astype(jnp.int32).reshape(1)
-    tables = merge_tables(start, band_table(own_table(band_offsets, band_weights, beam_delay)))
     pieces = ring_rest(kept_z, received_z, Z, Y)
     pieces += ring_rest(kept_y, received_y, Y, Z)
     beams = compressed_beams(pieces, range_filter)
     image = lax.all_to_all(beams, "sub", 0, 0, tiled=True)
-    left, right = from_neighbours(image)
-    return merge(left, image, right, tables)
+    scene = ()
+    for piece in range(PIECES):
+        direct = DIRECT[piece]
+        message = image[:, :, piece * PIECE : (piece + 1) * PIECE]
+        if piece == 0:
+            message = jnp.concatenate([message, packed], 0)
+        near, far = from_neighbours(message, direct)
+        if piece == 0:
+            tables = merge_tables(start, table, near, far, direct)
+        scene = (merge(near, image, far, tables, piece, direct, scene),)
+    return scene[0]
 
 
 def solution(mesh):

time: 125 us -> 117 us (0.936)
  the two profiles are of different devices: /device:TPU:16 before, /device:TPU:64 now
where the time goes in v2:
time: 117 us; the launch traced here: 116 us
  waiting for transfers between devices  51.4 us (44%)
  starting transfers between devices  40.2 us (34%)
  Pallas kernels  23.6 us (20%)
    ppermute x16, waiting for transfers between devices, ring_send(): return lax.ppermute(x, axis, [(k, (k + step) % RING) for k in range(RING)])  31 us
    ppermute x16, starting transfers between devices, ring_send(): return lax.ppermute(x, axis, [(k, (k + step) % RING) for k in range(RING)])  22.5 us
    all_to_all x1, waiting for transfers between devices, body(): image = lax.all_to_all(beams, 'sub', 0, 0, tiled=True)  10.2 us
    ppermute x2, waiting for transfers between devices, from_neighbours(): right = lax.ppermute(array, BEAM_COMP, [(b, a) for a, b in steps])  10.2 us
    ppermute x2, starting transfers between devices, from_neighbours(): right = lax.ppermute(array, BEAM_COMP, [(b, a) for a, b in steps])  8.25 us
    pallas_call x2, Pallas kernels, merge(): pl.pallas_call(functools.partial(merge_kernel, direct), grid=(steps,), in...  6.82 us
    pallas_call x1, Pallas kernels, later_sums(): pl.pallas_call(later_kernel, grid=(READS,), in_specs=[vmem, pl.BlockSpec(...  5.78 us
    ppermute x2, starting transfers between devices, from_neighbours(): left = lax.ppermute(array, BEAM_COMP, steps)  5.23 us
  transfers between devices with their start and end apart: 21, of which 9 were waited for; matrix products, arithmetic and copies ran while one was open for 1% of the time, Pallas kernels for 11%

profile of v2, /device:TPU:64, one launch (start us, length us, event | category | flops | bytes accessed | tf_op | source)
XLA Modules:
  0.0 116.3 jit_solution(5459921772542188933)
XLA Ops:
  0.0 5.0 %opening_sums.1 = (bf16[64,8192]{1,0:T(8,128)(2,1)S(1)}, bf16[64,8192]{1,0:T(8,128)(2,1)S(1)}, bf16[64,8192]{1,0:T(8,128)(2,1)S(1)}, bf16[64,8192]{1,0:T(8,128)(2,1)S(1)}, f32[2,128,256]{2,1,0:T(8,128)S(1)}) custom-call(f32[128,128]{1,0:T(8,128)} %angle_ref.1, bf16[128,2,16384]{2,1,0:T(2,128)(2,1)} %raw_ref.3), custom_call_target="tpu_custom_call" | custom-call | tf_op jit(solution)/shard_map/opening_sums/pallas_call | solution.py:124
  5.0 1.6 %collective-permute-start.8 = (bf16[64,8192]{1,0:T(8,128)(2,1)S(1)}, bf16[64,8192]{1,0:T(8,128)(2,1)S(1)}, u32[]{:S(2)}, u32[]{:S(2)}) collective-permute-start(bf16[64,8192]{1,0:T(8,128)(2,1)S(1)} %get-tuple-element.43), channel_id=1, source_target_pairs={{0,1},{1,8},{8,9},{9,0},{2,3},{3,10},{10,11},{11,2},{4,5},{5,12},{... | collective-permute-start | bytes 3145736 | tf_op jit(solution)/shard_map/ppermute | solution.py:62
  6.6 1.7 %collective-permute-start.9 = (bf16[64,8192]{1,0:T(8,128)(2,1)S(1)}, bf16[64,8192]{1,0:T(8,128)(2,1)S(1)}, u32[]{:S(2)}, u32[]{:S(2)}) collective-permute-start(bf16[64,8192]{1,0:T(8,128)(2,1)S(1)} %get-tuple-element.44), channel_id=1, source_target_pairs={{0,9},{1,0},{8,1},{9,8},{2,11},{3,2},{10,3},{11,10},{4,13},{5,4},{... | collective-permute-start | bytes 3145736 | tf_op jit(solution)/shard_map/ppermute | solution.py:62
  8.4 1.9 %collective-permute-start = (bf16[64,8192]{1,0:T(8,128)(2,1)S(1)}, bf16[64,8192]{1,0:T(8,128)(2,1)S(1)}, u32[]{:S(2)}, u32[]{:S(2)}) collective-permute-start(bf16[64,8192]{1,0:T(8,128)(2,1)S(1)} %get-tuple-element.33), channel_id=1, source_target_pairs={{0,2},{2,4},{4,6},{6,0},{1,3},{3,5},{5,7},{7,1},{8,10},{10,12},{12... | collective-permute-start | bytes 3145736 | tf_op jit(solution)/shard_map/ppermute | solution.py:62
  10.3 5.8 %later_sums.1 = (bf16[32,8192]{1,0:T(8,128)(2,1)S(1)}, bf16[32,8192]{1,0:T(8,128)(2,1)S(1)}, bf16[64,8192]{1,0:T(8,128)(2,1)S(1)}, bf16[32,8192]{1,0:T(8,128)(2,...) custom-call(f32[2,128,256]{2,1,0:T(8,128)S(1)} %get-tuple-element.31.weights, ...), custom_call_target="tpu_custom_call" | custom-call | tf_op jit(solution)/shard_map/later_sums/pallas_call | solution.py:161
  16.1 15.1 %collective-permute-done.8.p1 = bf16[64,8192]{1,0:T(8,128)(2,1)S(1)} collective-permute-done((bf16[64,8192]{1,0:T(8,128)(2,1)S(1)}, bf16[64,8192]{1,0:T(8,128)(2,1)S(1)}, u32[]{:S(2)}, u32[]{:S(2)}) %collective-permute-start.8) | collective-permute-done | bytes 1048608 | tf_op jit(solution)/shard_map/ppermute | solution.py:62
  31.3 0.4 collective-permute-start.10
  31.8 3.0 %collective-permute-start.11 = (bf16[32,8192]{1,0:T(8,128)(2,1)S(1)}, bf16[32,8192]{1,0:T(8,128)(2,1)S(1)}, u32[]{:S(2)}, u32[]{:S(2)}) collective-permute-start(bf16[32,8192]{1,0:T(8,128)(2,1)S(1)} %add_convert_fusion), channel_id=1, source_target_pairs={{0,9},{1,0},{8,1},{9,8},{2,11},{3,2},{10,3},{11,10},{4,13},{5,4},{... | collective-permute-start | bytes 1572872 | tf_op jit(solution)/shard_map/ppermute | solution.py:62
  35.3 2.0 %collective-permute-start.2 = (bf16[32,8192]{1,0:T(8,128)(2,1)S(1)}, bf16[32,8192]{1,0:T(8,128)(2,1)S(1)}, u32[]{:S(2)}, u32[]{:S(2)}) collective-permute-start(bf16[32,8192]{1,0:T(8,128)(2,1)S(1)} %add_convert_fusion.3), channel_id=1, source_target_pairs={{0,2},{2,4},{4,6},{6,0},{1,3},{3,5},{5,7},{7,1},{8,10},{10,12},{12... | collective-permute-start | bytes 1572872 | tf_op jit(solution)/shard_map/ppermute | solution.py:62
  37.3 8.2 %collective-permute-done.10.p2 = bf16[32,8192]{1,0:T(8,128)(2,1)S(1)} collective-permute-done((bf16[32,8192]{1,0:T(8,128)(2,1)S(1)}, bf16[32,8192]{1,0:T(8,128)(2,1)S(1)}, u32[]{:S(2)}, u32[]{:S(2)}) %collective-permute-start.10) | collective-permute-done | bytes 524320 | tf_op jit(solution)/shard_map/ppermute | solution.py:62
  45.5 0.5 middle_sums.3
  46.1 1.9 %collective-permute-start.12 = (bf16[16,8192]{1,0:T(8,128)(2,1)S(1)}, bf16[16,8192]{1,0:T(8,128)(2,1)S(1)}, u32[]{:S(2)}, u32[]{:S(2)}) collective-permute-start(bf16[16,8192]{1,0:T(8,128)(2,1)S(1)} %get-tuple-element.48), channel_id=1, source_target_pairs={{0,2},{2,4},{4,6},{6,0},{1,3},{3,5},{5,7},{7,1},{8,10},{10,12},{12... | collective-permute-start | bytes 786440 | tf_op jit(solution)/shard_map/ppermute | solution.py:62
  48.3 0.4 middle_sums.2
  48.8 2.9 %collective-permute-start.5 = (bf16[16,8192]{1,0:T(8,128)(2,1)S(1)}, bf16[16,8192]{1,0:T(8,128)(2,1)S(1)}, u32[]{:S(2)}, u32[]{:S(2)}) collective-permute-start(bf16[16,8192]{1,0:T(8,128)(2,1)S(1)} %get-tuple-element.39), channel_id=1, source_target_pairs={{0,9},{1,0},{8,1},{9,8},{2,11},{3,2},{10,3},{11,10},{4,13},{5,4},{... | collective-permute-start | bytes 786440 | tf_op jit(solution)/shard_map/ppermute | solution.py:62
  51.7 1.3 %collective-permute-done.13.refs_7_ = bf16[16,8192]{1,0:T(8,128)(2,1)S(1)} collective-permute-done((bf16[16,8192]{1,0:T(8,128)(2,1)S(1)}, bf16[16,8192]{1,0:T(8,128)(2,1)S(1)}, u32[]{:S(2)}, u32[]{:S(2)}) %collective-permute-start.13) | collective-permute-done | bytes 262176 | tf_op jit(solution)/shard_map/ppermute | solution.py:62
  53.0 0.4 collective-permute-start.15
  53.4 2.6 %collective-permute-start.14 = (bf16[8,8192]{1,0:T(8,128)(2,1)S(1)}, bf16[8,8192]{1,0:T(8,128)(2,1)S(1)}, u32[]{:S(2)}, u32[]{:S(2)}) collective-permute-start(bf16[8,8192]{1,0:T(8,128)(2,1)S(1)} %add_convert_fusion.5), channel_id=1, source_target_pairs={{0,2},{2,4},{4,6},{6,0},{1,3},{3,5},{5,7},{7,1},{8,10},{10,12},{12... | collective-permute-start | bytes 393224 | tf_op jit(solution)/shard_map/ppermute | solution.py:62
  56.1 3.3 %collective-permute-start.7 = (bf16[8,8192]{1,0:T(8,128)(2,1)S(1)}, bf16[8,8192]{1,0:T(8,128)(2,1)S(1)}, u32[]{:S(2)}, u32[]{:S(2)}) collective-permute-start(bf16[8,8192]{1,0:T(8,128)(2,1)S(1)} %add_convert_fusion.6), channel_id=1, source_target_pairs={{0,9},{1,0},{8,1},{9,8},{2,11},{3,2},{10,3},{11,10},{4,13},{5,4},{... | collective-permute-start | bytes 393224 | tf_op jit(solution)/shard_map/ppermute | solution.py:62
  59.8 2.2 %collective-permute-done.7.refs_4_ = bf16[8,8192]{1,0:T(8,128)(2,1)S(1)} collective-permute-done((bf16[8,8192]{1,0:T(8,128)(2,1)S(1)}, bf16[8,8192]{1,0:T(8,128)(2,1)S(1)}, u32[]{:S(2)}, u32[]{:S(2)}) %collective-permute-start.7) | collective-permute-done | bytes 131104 | tf_op jit(solution)/shard_map/ppermute | solution.py:62
  61.9 3.9 %collective-permute-done.6.refs_3_ = bf16[8,8192]{1,0:T(8,128)(2,1)S(1)} collective-permute-done((bf16[8,8192]{1,0:T(8,128)(2,1)S(1)}, bf16[8,8192]{1,0:T(8,128)(2,1)S(1)}, u32[]{:S(2)}, u32[]{:S(2)}) %collective-permute-start.6) | collective-permute-done | bytes 131104 | tf_op jit(solution)/shard_map/ppermute | solution.py:62
  65.9 2.1 %compressed_beams.1 = bf16[8,16,2048]{2,1,0:T(8,128)(2,1)} custom-call(f32[16,8192]{1,0:T(8,128)S(1)} %get-tuple-element.37.refs_0_, bf16[16,8192]{1,0:T(8,128)(2,1)S(1)} %collective-permute-done.4.refs_1_, bf16[16,8192]{1,0:T(8,128)(2,1)S(1)} %collective-permute-done.5.refs_2_, bf16[8,8192]{1,0:T(8,128)(2,1)S(1)} %collective-permute-done.6.refs_3_, ...), custom_call_target="tpu_custom_call" | custom-call | tf_op jit(solution)/shard_map/compressed_beams/pallas_call | solution.py:255
  67.9 4.3 %all-to-all-start = ((bf16[8,16,2048]{2,1,0:T(8,128)(2,1)}), bf16[8,16,2048]{2,1,0:T(8,128)(2,1)S(1)}, u32[]{:S(2)}, u32[]{:S(2)}) async-start(bf16[8,16,2048]{2,1,0:T(8,128)(2,1)} %compressed_beams.1), calls=%async_computation | async-start | bytes 1048576 | tf_op jit(solution)/shard_map/all_to_all | solution.py:507
  72.3 10.2 %all-to-all-done.own = bf16[8,16,2048]{2,1,0:T(8,128)(2,1)S(1)} async-done(((bf16[8,16,2048]{2,1,0:T(8,128)(2,1)}), bf16[8,16,2048]{2,1,0:T(8,128)(2,1)S(1)}, u32[]{:S(2)}, u32[]{:S(2)}) %all-to-all-start) | async-done | bytes 524320 | tf_op jit(solution)/shard_map/all_to_all | solution.py:507
  82.7 1.9 %collective-permute-start.18 = (bf16[9,16,1024]{2,1,0:T(8,128)(2,1)S(1)}, bf16[9,16,1024]{2,1,0:T(8,128)(2,1)S(1)}, u32[]{:S(2)}, u32[]{:S(2)}) collective-permute-start(bf16[9,16,1024]{2,1,0:T(8,128)(2,1)S(1)} %pad_maximum_fusion), channel_id=1, source_target_pairs={{0,1},{1,2},{2,3},{3,4},{4,5},{5,6},{6,7},{7,8},{8,9},{9,10},{10,1... | collective-permute-start | bytes 884744 | tf_op jit(solution)/shard_map/ppermute | solution.py:449
  84.6 4.8 %collective-permute-start.19 = (bf16[9,16,1024]{2,1,0:T(8,128)(2,1)S(1)}, bf16[9,16,1024]{2,1,0:T(8,128)(2,1)S(1)}, u32[]{:S(2)}, u32[]{:S(2)}) collective-permute-start(bf16[9,16,1024]{2,1,0:T(8,128)(2,1)S(1)} %pad_maximum_fusion), channel_id=1, source_target_pairs={{1,0},{2,1},{3,2},{4,3},{5,4},{6,5},{7,6},{8,7},{9,8},{10,9},{11,1... | collective-permute-start | bytes 884744 | tf_op jit(solution)/shard_map/ppermute | solution.py:450
  89.4 3.3 %collective-permute-start.16 = (bf16[8,16,1024]{2,1,0:T(8,128)(2,1)S(1)}, bf16[8,16,1024]{2,1,0:T(8,128)(2,1)S(1)}, u32[]{:S(2)}, u32[]{:S(2)}) collective-permute-start(bf16[8,16,1024]{2,1,0:T(8,128)(2,1)S(1)} %get-tuple-element.58), channel_id=1, source_target_pairs={{0,1},{1,2},{2,3},{3,4},{4,5},{5,6},{6,7},{7,8},{8,9},{9,10},{10,1... | collective-permute-start | bytes 786440 | tf_op jit(solution)/shard_map/ppermute | solution.py:449
  92.7 3.4 %collective-permute-start.17 = (bf16[8,16,1024]{2,1,0:T(8,128)(2,1)S(1)}, bf16[8,16,1024]{2,1,0:T(8,128)(2,1)S(1)}, u32[]{:S(2)}, u32[]{:S(2)}) collective-permute-start(bf16[8,16,1024]{2,1,0:T(8,128)(2,1)S(1)} %get-tuple-element.58), channel_id=1, source_target_pairs={{1,0},{2,1},{3,2},{4,3},{5,4},{6,5},{7,6},{8,7},{9,8},{10,9},{11,1... | collective-permute-start | bytes 786440 | tf_op jit(solution)/shard_map/ppermute | solution.py:450
  96.2 6.9 %collective-permute-done.19.far_ref.far = bf16[9,16,1024]{2,1,0:T(8,128)(2,1)S(1)} collective-permute-done((bf16[9,16,1024]{2,1,0:T(8,128)(2,1)S(1)}, bf16[9,16,1024]{2,1,0:T(8,128)(2,1)S(1)}, u32[]{:S(2)}, u32[]{:S(2)}) %collective-permute-start.19) | collective-permute-done | bytes 294944 | tf_op jit(solution)/shard_map/ppermute | solution.py:450
  103.1 3.1 %merge_tables.1 = (f32[416,128]{1,0:T(8,128)S(1)}, f32[4,416,128]{2,1,0:T(8,128)S(1)}, f32[4,416,128]{2,1,0:T(8,128)S(1)}, f32[416,128]{1,0:T(8,128)S(1)}, f32[416,128]{1,0:T(8,128)S(1)}) custom-call(s32[1]{0:T(128)} %bitcast.start_ref, f32[16,256]{1,0:T(8,128)S(1)} %bitcast.23, bf16[9,16,1024]{2,1,0:T(8,128)(2,1)S(1)} %collective-permute-done.18.near_ref.near, ...), custom_call_target="tpu_custom_call" | custom-call | tf_op jit(solution)/shard_map/merge_tables/pallas_call | solution.py:342
  106.2 3.4 %merge.2.refs_0_ = f32[64,2,2048]{2,1,0:T(2,128)} custom-call(bf16[9,16,1024]{2,1,0:T(8,128)(2,1)S(1)} %collective-permute-done.18.near_ref.near, bf16[8,16,2048]{2,1,0:T(8,128)(2,1)S(1)} %all-to-all-done.own, bf16[9,16,1024]{2,1,0:T(8,128)(2,1)S(1)} %collective-permute-done.19.far_ref.far, f32[416,128]{1,0:T(8,128)S(1)} %get-tuple-element.52.matrix, ...), custom_call_target="tpu_custom_call" | custom-call | tf_op jit(solution)/shard_map/merge/pallas_call | solution.py:431
  109.6 3.3 %collective-permute-done.17.far = bf16[8,16,1024]{2,1,0:T(8,128)(2,1)S(1)} collective-permute-done((bf16[8,16,1024]{2,1,0:T(8,128)(2,1)S(1)}, bf16[8,16,1024]{2,1,0:T(8,128)(2,1)S(1)}, u32[]{:S(2)}, u32[]{:S(2)}) %collective-permute-start.17) | collective-permute-done | bytes 262176 | tf_op jit(solution)/shard_map/ppermute | solution.py:450
  112.9 3.4 %merge.3 = f32[64,2,2048]{2,1,0:T(2,128)} custom-call(bf16[8,16,1024]{2,1,0:T(8,128)(2,1)S(1)} %collective-permute-done.16.near, bf16[8,16,2048]{2,1,0:T(8,128)(2,1)S(1)} %all-to-all-done.own, bf16[8,16,1024]{2,1,0:T(8,128)(2,1)S(1)} %collective-permute-done.17.far, f32[416,128]{1,0:T(8,128)S(1)} %get-tuple-element.52.matrix, ...), custom_call_target="tpu_custom_call", output_to_operand_aliasing={{}: (8, {})} | custom-call | tf_op jit(solution)/shard_map/merge/pallas_call | solution.py:431
  (48 shorter events, 1.8 us)
Async XLA Ops:
  5.0 26.2 %collective-permute-start.8 = (bf16[64,8192]{1,0:T(8,128)(2,1)S(1)}, bf16[64,8192]{1,0:T(8,128)(2,1)S(1)}, u32[]{:S(2)}, u32[]{:S(2)}) collective-permute-start(bf16[64,8192]{1,0:T(8,128)(2,1)S(1)} %get-tuple-element.43), channel_id=1, source_target_pairs={{0,1},{1,8},{8,9},{9,0},{2,3},{3,10},{10,11},{11,2},{4,5},{5,12},{... | collective-permute-start | bytes 3145736 | tf_op jit(solution)/shard_map/ppermute | solution.py:62
  6.6 25.1 %collective-permute-start.9 = (bf16[64,8192]{1,0:T(8,128)(2,1)S(1)}, bf16[64,8192]{1,0:T(8,128)(2,1)S(1)}, u32[]{:S(2)}, u32[]{:S(2)}) collective-permute-start(bf16[64,8192]{1,0:T(8,128)(2,1)S(1)} %get-tuple-element.44), channel_id=1, source_target_pairs={{0,9},{1,0},{8,1},{9,8},{2,11},{3,2},{10,3},{11,10},{4,13},{5,4},{... | collective-permute-start | bytes 3145736 | tf_op jit(solution)/shard_map/ppermute | solution.py:62
  8.3 26.6 %collective-permute-start.1 = (bf16[64,8192]{1,0:T(8,128)(2,1)S(1)}, bf16[64,8192]{1,0:T(8,128)(2,1)S(1)}, u32[]{:S(2)}, u32[]{:S(2)}) collective-permute-start(bf16[64,8192]{1,0:T(8,128)(2,1)S(1)} %get-tuple-element.34), channel_id=1, source_target_pairs={{0,6},{2,0},{4,2},{6,4},{1,7},{3,1},{5,3},{7,5},{8,14},{10,8},{12,... | collective-permute-start | bytes 3145736 | tf_op jit(solution)/shard_map/ppermute | solution.py:62
  8.4 26.8 %collective-permute-start = (bf16[64,8192]{1,0:T(8,128)(2,1)S(1)}, bf16[64,8192]{1,0:T(8,128)(2,1)S(1)}, u32[]{:S(2)}, u32[]{:S(2)}) collective-permute-start(bf16[64,8192]{1,0:T(8,128)(2,1)S(1)} %get-tuple-element.33), channel_id=1, source_target_pairs={{0,2},{2,4},{4,6},{6,0},{1,3},{3,5},{5,7},{7,1},{8,10},{10,12},{12... | collective-permute-start | bytes 3145736 | tf_op jit(solution)/shard_map/ppermute | solution.py:62
  16.1 43.6 %copy-start.2 = (f32[2,16384]{1,0:T(2,128)S(1)}, f32[2,16384]{1,0:T(2,128)}, u32[]{:S(2)}) copy-start(f32[2,16384]{1,0:T(2,128)} %param.9) | copy-start | bytes 393220
  16.1 49.8 %copy-start = (bf16[256,256]{1,0:T(8,128)(2,1)S(1)}, bf16[256,256]{1,0:T(8,128)(2,1)}, u32[]{:S(2)}) copy-start(bf16[256,256]{1,0:T(8,128)(2,1)} %constant.17.clone.refs_10_) | copy-start | bytes 393220
  16.1 49.8 %copy-start.1 = (f32[2,128,128]{2,1,0:T(8,128)S(1)}, f32[2,128,128]{2,1,0:T(8,128)}, u32[]{:S(2)}) copy-start(f32[2,128,128]{2,1,0:T(8,128)} %constant.18.clone.refs_11_) | copy-start | bytes 393220
  31.3 14.1 %collective-permute-start.10 = (bf16[32,8192]{1,0:T(8,128)(2,1)S(1)}, bf16[32,8192]{1,0:T(8,128)(2,1)S(1)}, u32[]{:S(2)}, u32[]{:S(2)}) collective-permute-start(bf16[32,8192]{1,0:T(8,128)(2,1)S(1)} %add_convert_fusion.1), channel_id=1, source_target_pairs={{0,1},{1,8},{8,9},{9,0},{2,3},{3,10},{10,11},{11,2},{4,5},{5,12},{... | collective-permute-start | bytes 1572872 | tf_op jit(solution)/shard_map/ppermute | solution.py:62
  31.8 13.7 %collective-permute-start.11 = (bf16[32,8192]{1,0:T(8,128)(2,1)S(1)}, bf16[32,8192]{1,0:T(8,128)(2,1)S(1)}, u32[]{:S(2)}, u32[]{:S(2)}) collective-permute-start(bf16[32,8192]{1,0:T(8,128)(2,1)S(1)} %add_convert_fusion), channel_id=1, source_target_pairs={{0,9},{1,0},{8,1},{9,8},{2,11},{3,2},{10,3},{11,10},{4,13},{5,4},{... | collective-permute-start | bytes 1572872 | tf_op jit(solution)/shard_map/ppermute | solution.py:62
  35.0 37.3 %copy-start.4 = (s32[2,112]{1,0:T(2,128)S(1)}, s32[2,112]{1,0:T(2,128)}, u32[]{:S(2)}) copy-start(s32[2,112]{1,0:T(2,128)} %param.11) | copy-start | bytes 2692
  35.0 37.3 %copy-start.3 = (f32[2,112,8]{1,2,0:T(8,128)S(1)}, f32[2,112,8]{1,2,0:T(8,128)}, u32[]{:S(2)}) copy-start(f32[2,112,8]{1,2,0:T(8,128)} %param.12) | copy-start | bytes 21508
  35.0 37.3 %copy-start.5 = (f32[2,112]{1,0:T(2,128)S(1)}, f32[2,112]{1,0:T(2,128)}, u32[]{:S(2)}) copy-start(f32[2,112]{1,0:T(2,128)} %param.13) | copy-start | bytes 2692
  35.0 13.0 %collective-permute-start.3 = (bf16[32,8192]{1,0:T(8,128)(2,1)S(1)}, bf16[32,8192]{1,0:T(8,128)(2,1)S(1)}, u32[]{:S(2)}, u32[]{:S(2)}) collective-permute-start(bf16[32,8192]{1,0:T(8,128)(2,1)S(1)} %add_convert_fusion.2), channel_id=1, source_target_pairs={{0,6},{2,0},{4,2},{6,4},{1,7},{3,1},{5,3},{7,5},{8,14},{10,8},{12,... | collective-permute-start | bytes 1572872 | tf_op jit(solution)/shard_map/ppermute | solution.py:62
  35.3 13.0 %collective-permute-start.2 = (bf16[32,8192]{1,0:T(8,128)(2,1)S(1)}, bf16[32,8192]{1,0:T(8,128)(2,1)S(1)}, u32[]{:S(2)}, u32[]{:S(2)}) collective-permute-start(bf16[32,8192]{1,0:T(8,128)(2,1)S(1)} %add_convert_fusion.3), channel_id=1, source_target_pairs={{0,2},{2,4},{4,6},{6,0},{1,3},{3,5},{5,7},{7,1},{8,10},{10,12},{12... | collective-permute-start | bytes 1572872 | tf_op jit(solution)/shard_map/ppermute | solution.py:62
  45.9 7.1 %collective-permute-start.13 = (bf16[16,8192]{1,0:T(8,128)(2,1)S(1)}, bf16[16,8192]{1,0:T(8,128)(2,1)S(1)}, u32[]{:S(2)}, u32[]{:S(2)}) collective-permute-start(bf16[16,8192]{1,0:T(8,128)(2,1)S(1)} %get-tuple-element.49), channel_id=1, source_target_pairs={{0,6},{2,0},{4,2},{6,4},{1,7},{3,1},{5,3},{7,5},{8,14},{10,8},{12,... | collective-permute-start | bytes 786440 | tf_op jit(solution)/shard_map/ppermute | solution.py:62
  46.1 7.3 %collective-permute-start.12 = (bf16[16,8192]{1,0:T(8,128)(2,1)S(1)}, bf16[16,8192]{1,0:T(8,128)(2,1)S(1)}, u32[]{:S(2)}, u32[]{:S(2)}) collective-permute-start(bf16[16,8192]{1,0:T(8,128)(2,1)S(1)} %get-tuple-element.48), channel_id=1, source_target_pairs={{0,2},{2,4},{4,6},{6,0},{1,3},{3,5},{5,7},{7,1},{8,10},{10,12},{12... | collective-permute-start | bytes 786440 | tf_op jit(solution)/shard_map/ppermute | solution.py:62
  48.8 7.3 %collective-permute-start.5 = (bf16[16,8192]{1,0:T(8,128)(2,1)S(1)}, bf16[16,8192]{1,0:T(8,128)(2,1)S(1)}, u32[]{:S(2)}, u32[]{:S(2)}) collective-permute-start(bf16[16,8192]{1,0:T(8,128)(2,1)S(1)} %get-tuple-element.39), channel_id=1, source_target_pairs={{0,9},{1,0},{8,1},{9,8},{2,11},{3,2},{10,3},{11,10},{4,13},{5,4},{... | collective-permute-start | bytes 786440 | tf_op jit(solution)/shard_map/ppermute | solution.py:62
  51.7 7.7 %collective-permute-start.4 = (bf16[16,8192]{1,0:T(8,128)(2,1)S(1)}, bf16[16,8192]{1,0:T(8,128)(2,1)S(1)}, u32[]{:S(2)}, u32[]{:S(2)}) collective-permute-start(bf16[16,8192]{1,0:T(8,128)(2,1)S(1)} %get-tuple-element.38), channel_id=1, source_target_pairs={{0,1},{1,8},{8,9},{9,0},{2,3},{3,10},{10,11},{11,2},{4,5},{5,12},{... | collective-permute-start | bytes 786440 | tf_op jit(solution)/shard_map/ppermute | solution.py:62
  53.0 6.7 %collective-permute-start.15 = (bf16[8,8192]{1,0:T(8,128)(2,1)S(1)}, bf16[8,8192]{1,0:T(8,128)(2,1)S(1)}, u32[]{:S(2)}, u32[]{:S(2)}) collective-permute-start(bf16[8,8192]{1,0:T(8,128)(2,1)S(1)} %add_convert_fusion.4), channel_id=1, source_target_pairs={{0,6},{2,0},{4,2},{6,4},{1,7},{3,1},{5,3},{7,5},{8,14},{10,8},{12,... | collective-permute-start | bytes 393224 | tf_op jit(solution)/shard_map/ppermute | solution.py:62
  53.4 6.3 %collective-permute-start.14 = (bf16[8,8192]{1,0:T(8,128)(2,1)S(1)}, bf16[8,8192]{1,0:T(8,128)(2,1)S(1)}, u32[]{:S(2)}, u32[]{:S(2)}) collective-permute-start(bf16[8,8192]{1,0:T(8,128)(2,1)S(1)} %add_convert_fusion.5), channel_id=1, source_target_pairs={{0,2},{2,4},{4,6},{6,0},{1,3},{3,5},{5,7},{7,1},{8,10},{10,12},{12... | collective-permute-start | bytes 393224 | tf_op jit(solution)/shard_map/ppermute | solution.py:62
  56.1 5.8 %collective-permute-start.7 = (bf16[8,8192]{1,0:T(8,128)(2,1)S(1)}, bf16[8,8192]{1,0:T(8,128)(2,1)S(1)}, u32[]{:S(2)}, u32[]{:S(2)}) collective-permute-start(bf16[8,8192]{1,0:T(8,128)(2,1)S(1)} %add_convert_fusion.6), channel_id=1, source_target_pairs={{0,9},{1,0},{8,1},{9,8},{2,11},{3,2},{10,3},{11,10},{4,13},{5,4},{... | collective-permute-start | bytes 393224 | tf_op jit(solution)/shard_map/ppermute | solution.py:62
  59.5 6.4 %collective-permute-start.6 = (bf16[8,8192]{1,0:T(8,128)(2,1)S(1)}, bf16[8,8192]{1,0:T(8,128)(2,1)S(1)}, u32[]{:S(2)}, u32[]{:S(2)}) collective-permute-start(bf16[8,8192]{1,0:T(8,128)(2,1)S(1)} %add_convert_fusion.7), channel_id=1, source_target_pairs={{0,1},{1,8},{8,9},{9,0},{2,3},{3,10},{10,11},{11,2},{4,5},{5,12},{... | collective-permute-start | bytes 393224 | tf_op jit(solution)/shard_map/ppermute | solution.py:62
  67.9 14.6 %all-to-all-start = ((bf16[8,16,2048]{2,1,0:T(8,128)(2,1)}), bf16[8,16,2048]{2,1,0:T(8,128)(2,1)S(1)}, u32[]{:S(2)}, u32[]{:S(2)}) async-start(bf16[8,16,2048]{2,1,0:T(8,128)(2,1)} %compressed_beams.1), calls=%async_computation | async-start | bytes 1048576 | tf_op jit(solution)/shard_map/all_to_all | solution.py:507
  82.7 13.5 %collective-permute-start.18 = (bf16[9,16,1024]{2,1,0:T(8,128)(2,1)S(1)}, bf16[9,16,1024]{2,1,0:T(8,128)(2,1)S(1)}, u32[]{:S(2)}, u32[]{:S(2)}) collective-permute-start(bf16[9,16,1024]{2,1,0:T(8,128)(2,1)S(1)} %pad_maximum_fusion), channel_id=1, source_target_pairs={{0,1},{1,2},{2,3},{3,4},{4,5},{5,6},{6,7},{7,8},{8,9},{9,10},{10,1... | collective-permute-start | bytes 884744 | tf_op jit(solution)/shard_map/ppermute | solution.py:449
  84.6 18.5 %collective-permute-start.19 = (bf16[9,16,1024]{2,1,0:T(8,128)(2,1)S(1)}, bf16[9,16,1024]{2,1,0:T(8,128)(2,1)S(1)}, u32[]{:S(2)}, u32[]{:S(2)}) collective-permute-start(bf16[9,16,1024]{2,1,0:T(8,128)(2,1)S(1)} %pad_maximum_fusion), channel_id=1, source_target_pairs={{1,0},{2,1},{3,2},{4,3},{5,4},{6,5},{7,6},{8,7},{9,8},{10,9},{11,1... | collective-permute-start | bytes 884744 | tf_op jit(solution)/shard_map/ppermute | solution.py:450
  89.4 20.2 %collective-permute-start.16 = (bf16[8,16,1024]{2,1,0:T(8,128)(2,1)S(1)}, bf16[8,16,1024]{2,1,0:T(8,128)(2,1)S(1)}, u32[]{:S(2)}, u32[]{:S(2)}) collective-permute-start(bf16[8,16,1024]{2,1,0:T(8,128)(2,1)S(1)} %get-tuple-element.58), channel_id=1, source_target_pairs={{0,1},{1,2},{2,3},{3,4},{4,5},{5,6},{6,7},{7,8},{8,9},{9,10},{10,1... | collective-permute-start | bytes 786440 | tf_op jit(solution)/shard_map/ppermute | solution.py:449
  92.7 20.2 %collective-permute-start.17 = (bf16[8,16,1024]{2,1,0:T(8,128)(2,1)S(1)}, bf16[8,16,1024]{2,1,0:T(8,128)(2,1)S(1)}, u32[]{:S(2)}, u32[]{:S(2)}) collective-permute-start(bf16[8,16,1024]{2,1,0:T(8,128)(2,1)S(1)} %get-tuple-element.58), channel_id=1, source_target_pairs={{1,0},{2,1},{3,2},{4,3},{5,4},{6,5},{7,6},{8,7},{9,8},{10,9},{11,1... | collective-permute-start | bytes 786440 | tf_op jit(solution)/shard_map/ppermute | solution.py:450

commit v3 on v2

v3 whole, which is shorter than its diff:
```python
import functools
import math

import jax
import jax.numpy as jnp
import ml_dtypes
import numpy as np
from jax import lax
from jax.experimental import pallas as pl
from jax.experimental.pallas import tpu as pltpu
from jax.sharding import Mesh
from jax.sharding import PartitionSpec as P

NR = 16384
RADIX = 128
NB0 = 8
BAND = 8
PSUB = 2048
RING = 4
HALF = NR // 2
READS = 4
READ = NR // READS
STEP = 2048
SLAB = NR // 8
COLS = 512
FIELDS = 256
SIDE = 144
BEAM_COMP = ("y_hi", "z", "y_lo")
SUB_BEAM_COMP = ("sub", "y_hi", "z", "y_lo")
Y = ("y_hi", "y_lo")
Z = "z"
BF = jnp.bfloat16
F4 = jnp.float32
SENT = ((2, 0), (2, 1), (1, 2), (1, 3), (2, 2), (2, 3), (3, 0), (3, 1))
KEPT = ((1, 0), (1, 1), (3, 2), (3, 3), (0, 0), (0, 1), (0, 2), (0, 3))
KEPT_ROWS = (32, 32, 64)


def params(mebibytes):
    return pltpu.CompilerParams(vmem_limit_bytes=mebibytes << 20)


def real_form_transposed():
    index = np.arange(RADIX)
    angle = (index[:, None] * index[None, :] % RADIX) * (2.0 * math.pi / RADIX)
    cos_part, sin_part = np.cos(angle), -np.sin(angle)
    upper = np.concatenate([cos_part, sin_part], 1)
    lower = np.concatenate([-sin_part, cos_part], 1)
    return np.concatenate([upper, lower], 0).T.astype(ml_dtypes.bfloat16)


def twiddle():
    index = np.arange(RADIX)
    angle = (index[:, None] * index[None, :] % NR) * (2.0 * math.pi / NR)
    return np.stack([np.cos(angle), -np.sin(angle)]).astype(np.float32)


def ring_send(x, axis, step):
    return lax.ppermute(x, axis, [(k, (k + step) % RING) for k in range(RING)])


def steering_rows(angle_ref, weights):
    factor = float(PSUB) ** -0.5
    rows = lax.broadcasted_iota(jnp.int32, (128, 256), 0)
    cols = lax.broadcasted_iota(jnp.int32, (128, 256), 1)
    spread = jnp.where(cols // 2 == rows, 1.0, 0.0).astype(BF)
    angle = angle_ref[...]
    cosine = (jnp.cos(angle) * factor).astype(BF)
    sine = (jnp.sin(angle) * factor).astype(BF)
    cosine = jnp.dot(cosine, spread, preferred_element_type=F4)
    sine = jnp.dot(sine, spread, preferred_element_type=F4)
    even = cols % 2 == 0
    weights[0] = jnp.where(even, cosine, -sine)
    weights[1] = jnp.where(even, sine, cosine)


def beam_matrix(weights, owners, z_first):
    y = lax.axis_index("y_hi") * 2 + lax.axis_index("y_lo")
    z = lax.axis_index("z")
    picked = []
    for first, second in owners:
        y_step, z_step = (second, first) if z_first else (first, second)
        y_of, z_of = lax.rem(y + y_step, RING), lax.rem(z + z_step, RING)
        block = lax.div(y_of, 2) * 8 + z_of * 2 + lax.rem(y_of, 2)
        start = pl.multiple_of(block * NB0, NB0)
        picked.append(weights[0, pl.ds(start, NB0), :])
        picked.append(weights[1, pl.ds(start, NB0), :])
    return jnp.concatenate(picked, 0).astype(BF)


def split_three(table):
    parts = []
    for _ in range(3):
        part = table.astype(BF)
        parts.append(part)
        table = table - part.astype(F4)
    return parts


def opening_kernel(angle_ref, offset_ref, band_ref, delay_ref, raw_ref, *refs):
    outs, (weights, table) = refs[:4], refs[4:6]
    landed, angle_landed, offset_landed, band_landed, delay_landed, sems = refs[6:]
    small = (
        (angle_ref, angle_landed),
        (offset_ref, offset_landed),
        (band_ref, band_landed),
        (delay_ref, delay_landed),
    )
    small_reads = [
        pltpu.make_async_copy(source, target, sems.at[READS + k])
        for k, (source, target) in enumerate(small)
    ]
    for copy in small_reads:
        copy.start()

    def read(k):
        cols = pl.ds(k * READ, READ)
        return pltpu.make_async_copy(raw_ref.at[:, :, cols], landed.at[k], sems.at[k])

    for k in range(READS):
        read(k).start()
    for copy in small_reads:
        copy.wait()
    steering_rows(angle_landed, weights)
    width = offset_landed.shape[1]
    table[...] = jnp.zeros_like(table)
    for side in range(2):
        cols = slice(side * 128, side * 128 + width)
        table[0:1, cols] = offset_landed[side : side + 1, :].astype(F4)
        table[1:9, cols] = band_landed[side]
        table[9:10, cols] = delay_landed[side : side + 1, :]
    parts = split_three(table[...])
    packed = jnp.concatenate([*parts, jnp.zeros_like(parts[0])], 0)
    for out in outs[2:]:
        out[:, HALF:] = packed
    for k in range(READS):
        half = k // (READS // 2)
        matrix = beam_matrix(weights, SENT, half == 0)
        read(k).wait()
        base = k * READ - half * HALF
        for part in range(READ // STEP):
            raw = landed[k, :, :, part * STEP : (part + 1) * STEP].reshape(256, STEP)
            total = jnp.dot(matrix, raw, preferred_element_type=F4).astype(BF)
            cols = slice(base + part * STEP, base + (part + 1) * STEP)
            outs[2 * half][:, cols] = total[:64]
            outs[2 * half + 1][:, cols] = total[64:]


def opening_sums(raw, *small):
    vmem = pl.BlockSpec(memory_space=pltpu.VMEM)
    outs = [jax.ShapeDtypeStruct((64, c), BF) for c in (HALF, HALF, HALF + FIELDS, HALF + FIELDS)]
    outs += [jax.ShapeDtypeStruct((2, 128, 256), F4), jax.ShapeDtypeStruct((16, FIELDS), F4)]
    results = pl.pallas_call(
        opening_kernel,
        in_specs=[pl.BlockSpec(memory_space=pltpu.HBM)] * 5,
        out_specs=[vmem] * 6,
        out_shape=outs,
        scratch_shapes=[pltpu.VMEM((READS, 128, 2, READ), BF)]
        + [pltpu.VMEM(array.shape, array.dtype) for array in small]
        + [pltpu.SemaphoreType.DMA((READS + 4,))],
        compiler_params=params(20),
        name="opening_sums",
    )(*(pltpu.with_memory_space_constraint(a, pltpu.HBM) for a in (*small, raw)))
    return results[:2], results[2:4], *results[4:]


def later_kernel(weights, raw_ref, *outs):
    steps = pl.num_programs(0) // 2
    for half in range(2):

        @pl.when(pl.program_id(0) // steps == half)
        def _():
            matrix = beam_matrix(weights, KEPT, half == 0)
            raw = raw_ref[...].reshape(256, READ)
            total = jnp.dot(matrix, raw, preferred_element_type=F4).astype(BF)
            step = lax.rem(pl.program_id(0), steps)
            cols = pl.ds(pl.multiple_of(step * READ, READ), READ)
            start = 0
            for out in outs[3 * half : 3 * half + 3]:
                size = out.shape[0]
                out[:, cols] = total[start : start + size]
                start += size


def later_sums(weights, raw):
    vmem = pl.BlockSpec(memory_space=pltpu.VMEM)
    outs = [jax.ShapeDtypeStruct((n, HALF), BF) for n in KEPT_ROWS * 2]
    kept = pl.pallas_call(
        later_kernel,
        grid=(READS,),
        in_specs=[vmem, pl.BlockSpec((128, 2, READ), lambda i: (0, 0, i))],
        out_specs=[vmem] * 6,
        out_shape=outs,
        compiler_params=params(20),
        name="later_sums",
    )(weights, pltpu.with_memory_space_constraint(raw, pltpu.HBM))
    return kept[:3], kept[3:]


def relay(q, received):
    rows, cols = q.shape
    return (q.astype(F4) + received[:rows, :cols].astype(F4)).astype(BF)


def middle_kernel(own, p1, m1, p2, m2, plus, minus, q1, q3, keep):
    tile = 512

    def step(k, carry):
        cols = pl.ds(pl.multiple_of(k * tile, tile), tile)
        low = own[:32, cols].astype(F4) + m1[32:, cols].astype(F4) + p2[:, cols].astype(F4)
        high = own[32:, cols].astype(F4) + p1[32:, cols].astype(F4) + m2[:, cols].astype(F4)
        keep[:, cols] = low[:16]
        q1[:, cols] = low[16:24].astype(BF)
        plus[:, cols] = jnp.concatenate([high[:8], low[24:]], 0).astype(BF)
        minus[:, cols] = jnp.concatenate([high[8:16], high[16:24]], 0).astype(BF)
        q3[:, cols] = high[24:].astype(BF)
        return carry

    lax.fori_loop(0, HALF // tile, step, 0)
    if plus.shape[1] > HALF:
        for j, received in enumerate((p1, m1)):
            for k in range(3):
                first = HALF + (3 * j + k) * FIELDS
                part = received[16 * k : 16 * k + 16, HALF:]
                plus[:, first : first + FIELDS] = part
                minus[:, first : first + FIELDS] = part


def middle_sums(own, p1, m1, p2, m2):
    wide = HALF + 6 * (p1.shape[1] - HALF)
    outs = ((16, wide, BF), (16, wide, BF), (8, HALF, BF), (8, HALF, BF), (16, HALF, F4))
    vmem = pl.BlockSpec(memory_space=pltpu.VMEM)
    return pl.pallas_call(
        middle_kernel,
        in_specs=[vmem] * 5,
        out_specs=[vmem] * 5,
        out_shape=[jax.ShapeDtypeStruct((n, c), d) for n, c, d in outs],
        compiler_params=params(4),
        name="middle_sums",
    )(own, p1, m1, p2, m2)


def compress_kernel(*refs):
    ins, (form_ref, turn_ref, filter_ref, out, lines, bins) = refs[:10], refs[10:]
    for half in range(2):
        keep, p3, m3, p4, m4 = ins[5 * half : 5 * half + 5]
        sums = (
            keep[:8] + m3[:, :HALF].astype(F4)[8:] + p4[...].astype(F4),
            keep[8:] + p3[:, :HALF].astype(F4)[8:] + m4[...].astype(F4),
        )
        for part in range(2):
            for k in range(64):
                row = (half * 64 + k) * 8
                lines[part, row : row + 8, :] = sums[part][:, k * 128 : (k + 1) * 128]
    form = form_ref[...]
    cos_part, sin_part = turn_ref[0], turn_ref[1]
    scale = NR ** (-0.5)
    real_filter, imag_filter = filter_ref[0] * scale, filter_ref[1] * scale
    for beam in range(NB0):
        picked = pl.ds(beam, 128, stride=8)
        data = jnp.concatenate([lines[0, picked, :], lines[1, picked, :]], 0)
        upper = data.astype(BF)
        lower = (data - upper.astype(F4)).astype(BF)
        one = jnp.dot(form, jnp.concatenate([upper, lower], 1), preferred_element_type=F4)
        one = one[:, :128] + one[:, 128:]
        real_in, imag_in = one[:128], one[128:]
        turned = jnp.concatenate(
            [real_in * cos_part - imag_in * sin_part, real_in * sin_part + imag_in * cos_part], 1
        )
        upper = turned.astype(BF)
        lower = (turned - upper.astype(F4)).astype(BF)
        two = lax.dot_general(
            form,
            jnp.concatenate([upper, lower], 0),
            (((1,), (1,)), ((), ())),
            preferred_element_type=F4,
        )
        two = two[:, :128] + two[:, 128:]
        real_in, imag_in = two[:128], two[128:]
        bins[0, picked, :] = real_in * real_filter - imag_in * imag_filter
        bins[1, picked, :] = real_in * imag_filter + imag_in * real_filter
    for slab in range(8):
        for k in range(16):
            row = (slab * 16 + k) * 8
            both = jnp.concatenate([bins[0, row : row + 8, :], bins[1, row : row + 8, :]], 0)
            out[slab, :, k * 128 : (k + 1) * 128] = both.astype(BF)


def compressed_beams(pieces, range_filter):
    return pl.pallas_call(
        compress_kernel,
        out_shape=jax.ShapeDtypeStruct((8, 16, SLAB), BF),
        scratch_shapes=[pltpu.VMEM((2, 1024, 128), F4), pltpu.VMEM((2, 1024, 128), F4)],
        compiler_params=params(12),
        name="compressed_beams",
    )(
        *pieces,
        jnp.asarray(real_form_transposed()),
        jnp.asarray(twiddle()),
        range_filter.reshape(2, 128, 128),
    )


def sided(near, far):
    even = lax.axis_index("y_lo") == 0
    return jnp.where(even, far, near), jnp.where(even, near, far)


def table_kernel(start_ref, own_ref, y_below, y_above, z_below, z_above, *refs):
    matrix, near_cos, near_sin, far_cos, far_sin, lines = refs
    y_hi, z = lax.axis_index("y_hi"), lax.axis_index("z")
    even = lax.axis_index("y_lo") == 0

    def columns(fields):
        padded = jnp.concatenate([fields, jnp.zeros((112, 256), F4)], 0)
        return jnp.concatenate([padded[:, :128].T, padded[:, 128:].T], 0)

    def from_rows(ref):
        parts = ref[:48, HALF:].astype(F4)
        return parts[:16] + parts[16:32] + parts[32:]

    def from_cols(ref, j):
        first = HALF + 3 * j * FIELDS
        parts = ref[:, first : first + 3 * FIELDS].astype(F4)
        return parts[:, :256] + parts[:, 256:512] + parts[:, 512:]

    near = jnp.where(even, from_rows(y_above), from_rows(y_below))
    left = jnp.where(z > 0, from_cols(z_below, 1), from_cols(z_below, 0))
    right = jnp.where(z < RING - 1, from_cols(z_above, 0), from_cols(z_above, 1))
    left = jnp.where((z > 0) | (y_hi > 0), left, 0.0)
    right = jnp.where((z < RING - 1) | (y_hi == 0), right, 0.0)
    left, right = sided(near, jnp.where(even, left, right))
    own, left, right = columns(own_ref[...]), columns(left), columns(right)

    def piece(source, side, first, count, shift):
        rows = source[side * 128 + first : side * 128 + first + count]
        field = lax.broadcasted_iota(jnp.int32, rows.shape, 1)
        return rows + jnp.where(field == 0, float(shift), 0.0)

    for side in range(2):
        row = side * SIDE
        for source, first, count, shift in (
            (left, 8, 8, 0),
            (own, 0, 16, 8),
            (right, 0, 8, 16),
            (left, 40, 8, -8),
            (own, 16, 32, 8),
            (right, 16, 8, 24),
            (own, 48, 64, 8),
        ):
            lines[row : row + count, :] = piece(source, side, first, count, shift)
            row += count
    rows = 2 * SIDE
    table = lines[...]
    lane = lax.broadcasted_iota(jnp.int32, (rows, 256), 1)
    row = lax.broadcasted_iota(jnp.int32, (rows, 256), 0) % SIDE
    depth = jnp.where(row < 80, 32, 48)
    term = lane // depth
    place = (lane - term * depth).astype(F4) - table[:, 0:1]
    band = jnp.zeros((rows, 256), F4)
    for tap in range(BAND):
        band = band + jnp.where(place == float(tap), table[:, tap + 1 : tap + 2], 0.0)
    upper = band.astype(BF).astype(F4)
    matrix[...] = jnp.where(term == 1, band - upper, upper).astype(BF)
    delay = table[:, 9:10]
    lane = lax.broadcasted_iota(jnp.int32, (rows, 128), 1).astype(F4)
    step = delay * (lane * (1.0 / NR))
    far_cos[...] = jnp.cos(step)
    far_sin[...] = jnp.sin(step)
    first = start_ref[0].astype(F4)
    base = delay * (1.0 + (first + lane * 128.0) * (1.0 / NR))
    near_cos[...] = jnp.cos(base)
    near_sin[...] = jnp.sin(base)


def merge_tables(start, own, *received):
    rows = 2 * SIDE
    vmem = pl.BlockSpec(memory_space=pltpu.VMEM)
    return pl.pallas_call(
        table_kernel,
        grid=(1,),
        in_specs=[pl.BlockSpec(memory_space=pltpu.SMEM)] + [vmem] * 5,
        out_specs=[pl.BlockSpec((rows, 256), lambda i: (0, 0))]
        + [pl.BlockSpec((rows, 128), lambda i: (0, 0))] * 4,
        out_shape=[pltpu.HBM((rows, 256), BF)] + [pltpu.HBM((rows, 128), F4)] * 4,
        scratch_shapes=[pltpu.VMEM((rows, 128), F4)],
        compiler_params=params(12),
        name="merge_tables",
    )(start, own, *received)


def merge_kernel(near, own, far, matrix, near_cos, near_sin, far_cos, far_sin, out, lines):
    groups = COLS // 128
    shift = lax.rem(128 - groups * pl.program_id(0), 128)
    cosines = pltpu.roll(near_cos[...], shift, 1)
    sines = pltpu.roll(near_sin[...], shift, 1)

    def phases(first, count):
        rows = slice(first, first + count)
        cosine, sine = far_cos[rows, :], far_sin[rows, :]
        real_parts, imag_parts = [], []
        for k in range(groups):
            a, b = cosines[rows, k : k + 1], sines[rows, k : k + 1]
            real_parts.append(a * cosine - b * sine)
            imag_parts.append(b * cosine + a * sine)
        return jnp.concatenate(real_parts, 1), jnp.concatenate(imag_parts, 1)

    def stacked(image, exact):
        upper = image.astype(BF)
        if exact:
            return jnp.concatenate([upper, upper], 0)
        lower = (image - upper.astype(F4)).astype(BF)
        return jnp.concatenate([upper, upper, lower], 0)

    zeros = jnp.zeros((8, COLS), F4)
    images = []
    for sub in range(8):
        left, right = sided(near[sub].astype(F4), far[sub].astype(F4))
        parts = (left, own[sub].astype(F4), right)
        images.append(
            tuple(jnp.concatenate([p[8 * q : 8 * q + 8] for p in parts] + [zeros], 0) for q in (0, 1))
        )
    for first, count, terms in ((0, 32, 64), (32, 48, 96), (80, 64, 144)):
        merged = [None] * (len(images) // 2)
        for side in range(2):
            start = side * SIDE + first
            band = matrix[start : start + count, :terms]
            cosine, sine = phases(start, count)
            for group in range(len(merged)):
                real_in, imag_in = (
                    jnp.dot(band, stacked(part, first == 0), preferred_element_type=F4)
                    for part in images[2 * group + side]
                )
                real_out = cosine * real_in - sine * imag_in
                imag_out = sine * real_in + cosine * imag_in
                if side:
                    real_out, imag_out = merged[group][0] + real_out, merged[group][1] + imag_out
                merged[group] = (real_out, imag_out)
        images = merged
    for k in range(groups):
        cols = slice(k * 128, (k + 1) * 128)
        for part in range(2):
            lines[k, pl.ds(part, 64, stride=2), :] = images[0][part][:, cols]
        out[:, :, cols] = lines[k].reshape(64, 2, 128)


def merge(near, own, far, tables):
    rows = 2 * SIDE
    image = pl.BlockSpec((8, 16, COLS), lambda i: (0, 0, i))
    whole = pl.BlockSpec((rows, 128), lambda i: (0, 0))
    return pl.pallas_call(
        merge_kernel,
        grid=(SLAB // COLS,),
        in_specs=[image] * 3 + [pl.BlockSpec((rows, 256), lambda i: (0, 0))] + [whole] * 4,
        out_specs=pl.BlockSpec((64, 2, COLS), lambda i: (0, 0, i)),
        out_shape=jax.ShapeDtypeStruct((64, 2, SLAB), F4),
        scratch_shapes=[pltpu.VMEM((COLS // 128, 128, 128), F4)],
        compiler_params=params(16),
        name="merge",
    )(near, own, far, *(pltpu.with_memory_space_constraint(t, pltpu.HBM) for t in tables))


def from_near(array):
    blocks = lax.axis_size(BEAM_COMP)
    return lax.ppermute(array, BEAM_COMP, [(k, k ^ 1) for k in range(blocks)])


def from_far(array):
    blocks = lax.axis_size(BEAM_COMP)
    steps = [(k, k - 1 + 2 * (k % 2)) for k in range(1, blocks - 1)]
    return lax.ppermute(array, BEAM_COMP, steps)


def ring_start(parts, first):
    return ring_send(parts[0], first, 1), ring_send(parts[1], first, -1)


def ring_rest(kept, received, first, second):
    q1, q3, own = kept
    p1, m1 = received
    p2 = ring_send(relay(q1, p1), first, 1)
    m2 = ring_send(relay(q3, m1), first, -1)
    plus, minus, q1, q3, keep = middle_sums(own, p1, m1, p2, m2)
    p3 = ring_send(plus, second, 1)
    m3 = ring_send(minus, second, -1)
    p4 = ring_send(relay(q1, p3), second, 1)
    m4 = ring_send(relay(q3, m3), second, -1)
    return keep, p3, m3, p4, m4


def body(raw_pulses, range_filter, steer_angle, band_offsets, band_weights, beam_delay):
    sent_z, sent_y, weights, table = opening_sums(
        raw_pulses, steer_angle, band_offsets, jnp.moveaxis(band_weights, 2, 1), beam_delay
    )
    received_z = ring_start(sent_z, Z)
    received_y = ring_start(sent_y, Y)
    kept_z, kept_y = later_sums(weights, raw_pulses)
    start = (lax.axis_index("sub") * SLAB).astype(jnp.int32).reshape(1)
    pieces_z = ring_rest(kept_z, received_z, Z, Y)
    pieces_y = ring_rest(kept_y, received_y, Y, Z)
    tables = merge_tables(start, table, *received_y, *pieces_y[1:3])
    beams = compressed_beams(pieces_z + pieces_y, range_filter)
    near_beams = from_near(beams)
    image = lax.all_to_all(beams, "sub", 0, 0, tiled=True)
    near = lax.all_to_all(near_beams, "sub", 0, 0, tiled=True)
    return merge(near, image, from_far(image), tables)


def solution(mesh):
    split = Mesh(
        mesh.devices.reshape(mesh.shape["sub"], 2, RING, mesh.shape["comp"]), SUB_BEAM_COMP
    )
    return jax.shard_map(
        body,
        mesh=split,
        in_specs=(
            P(SUB_BEAM_COMP, None, None),
            P(),
            P(None, SUB_BEAM_COMP),
            P(None, BEAM_COMP),
            P(None, BEAM_COMP, None),
            P(None, BEAM_COMP),
        ),
        out_specs=P(BEAM_COMP, None, "sub"),
        check_vma=False,
    )
```

time: 117 us -> 108 us (0.923)
  the two profiles are of different devices: /device:TPU:64 before, /device:TPU:16 now
where the time goes in v3:
time: 108 us; the launch traced here: 107 us
  waiting for transfers between devices  34.3 us (32%)
  starting transfers between devices  32.5 us (30%)
  Pallas kernels  24.2 us (22%)
  blocking collectives  14.5 us (13%)
    ppermute x16, waiting for transfers between devices, ring_send(): return lax.ppermute(x, axis, [(k, (k + step) % RING) for k in range(RING)])  30.2 us
    ppermute x16, starting transfers between devices, ring_send(): return lax.ppermute(x, axis, [(k, (k + step) % RING) for k in range(RING)])  22.8 us
    all_to_all x1, blocking collectives, body(): image = lax.all_to_all(beams, 'sub', 0, 0, tiled=True)  14.5 us
    pallas_call x1, Pallas kernels, merge(): pl.pallas_call(merge_kernel, grid=(SLAB // COLS,), in_specs=[image] * 3 +...  6.04 us
    pallas_call x1, Pallas kernels, later_sums(): pl.pallas_call(later_kernel, grid=(READS,), in_specs=[vmem, pl.BlockSpec(...  5.78 us
    pallas_call x1, Pallas kernels, merge_tables(): pl.pallas_call(table_kernel, grid=(1,), in_specs=[pl.BlockSpec(memory_spa...  5.2 us
    pallas_call x1, Pallas kernels, opening_sums(): pl.pallas_call(opening_kernel, in_specs=[pl.BlockSpec(memory_space=pltpu....  5.06 us
    ppermute x1, starting transfers between devices, from_far(): return lax.ppermute(array, BEAM_COMP, steps)  4.82 us
  transfers between devices with their start and end apart: 19, of which 7 were waited for; matrix products, arithmetic and copies ran while one was open for 1% of the time, Pallas kernels for 11%

profile of v3, /device:TPU:16, one launch (start us, length us, event | category | flops | bytes accessed | tf_op | source)
XLA Modules:
  0.0 107.4 jit_solution(1152611129017046278)
XLA Ops:
  0.0 5.1 %opening_sums.1 = (bf16[64,8192]{1,0:T(8,128)(2,1)S(1)}, bf16[64,8192]{1,0:T(8,128)(2,1)S(1)}, bf16[64,8448]{1,0:T(8,128)(2,1)S(1)}, bf16[64,8448]{1,0:T(8,128)(...) custom-call(f32[128,128]{1,0:T(8,128)} %angle_ref.1, s32[2,112]{1,0:T(2,128)} %offset_ref.1, ...), custom_call_target="tpu_custom_call" | custom-call | tf_op jit(solution)/shard_map/opening_sums/pallas_call | solution.py:153
  5.1 2.0 %collective-permute-start = (bf16[64,8192]{1,0:T(8,128)(2,1)S(1)}, bf16[64,8192]{1,0:T(8,128)(2,1)S(1)}, u32[]{:S(2)}, u32[]{:S(2)}) collective-permute-start(bf16[64,8192]{1,0:T(8,128)(2,1)S(1)} %get-tuple-element.34), channel_id=1, source_target_pairs={{0,2},{2,4},{4,6},{6,0},{1,3},{3,5},{5,7},{7,1},{8,10},{10,12},{12... | collective-permute-start | bytes 3145736 | tf_op jit(solution)/shard_map/ppermute | solution.py:59
  7.1 2.2 %collective-permute-start.1 = (bf16[64,8192]{1,0:T(8,128)(2,1)S(1)}, bf16[64,8192]{1,0:T(8,128)(2,1)S(1)}, u32[]{:S(2)}, u32[]{:S(2)}) collective-permute-start(bf16[64,8192]{1,0:T(8,128)(2,1)S(1)} %get-tuple-element.35), channel_id=1, source_target_pairs={{0,6},{2,0},{4,2},{6,4},{1,7},{3,1},{5,3},{7,5},{8,14},{10,8},{12,... | collective-permute-start | bytes 3145736 | tf_op jit(solution)/shard_map/ppermute | solution.py:59
  9.3 1.3 %collective-permute-start.8 = (bf16[64,8448]{1,0:T(8,128)(2,1)S(1)}, bf16[64,8448]{1,0:T(8,128)(2,1)S(1)}, u32[]{:S(2)}, u32[]{:S(2)}) collective-permute-start(bf16[64,8448]{1,0:T(8,128)(2,1)S(1)} %get-tuple-element.44), channel_id=1, source_target_pairs={{0,1},{1,8},{8,9},{9,0},{2,3},{3,10},{10,11},{11,2},{4,5},{5,12},{... | collective-permute-start | bytes 3244040 | tf_op jit(solution)/shard_map/ppermute | solution.py:59
  10.5 0.7 collective-permute-start.9
  11.3 5.8 %later_sums.1 = (bf16[32,8192]{1,0:T(8,128)(2,1)S(1)}, bf16[32,8192]{1,0:T(8,128)(2,1)S(1)}, bf16[64,8192]{1,0:T(8,128)(2,1)S(1)}, bf16[32,8192]{1,0:T(8,128)(2,...) custom-call(f32[2,128,256]{2,1,0:T(8,128)S(1)} %get-tuple-element.32.weights, ...), custom_call_target="tpu_custom_call" | custom-call | tf_op jit(solution)/shard_map/later_sums/pallas_call | solution.py:188
  17.1 15.3 %collective-permute-done.p1 = bf16[64,8192]{1,0:T(8,128)(2,1)S(1)} collective-permute-done((bf16[64,8192]{1,0:T(8,128)(2,1)S(1)}, bf16[64,8192]{1,0:T(8,128)(2,1)S(1)}, u32[]{:S(2)}, u32[]{:S(2)}) %collective-permute-start) | collective-permute-done | bytes 1048608 | tf_op jit(solution)/shard_map/ppermute | solution.py:59
  32.5 0.1 add_convert_fusion.2
  32.7 3.3 %collective-permute-start.3 = (bf16[32,8192]{1,0:T(8,128)(2,1)S(1)}, bf16[32,8192]{1,0:T(8,128)(2,1)S(1)}, u32[]{:S(2)}, u32[]{:S(2)}) collective-permute-start(bf16[32,8192]{1,0:T(8,128)(2,1)S(1)} %add_convert_fusion.2), channel_id=1, source_target_pairs={{0,6},{2,0},{4,2},{6,4},{1,7},{3,1},{5,3},{7,5},{8,14},{10,8},{12,... | collective-permute-start | bytes 1572872 | tf_op jit(solution)/shard_map/ppermute | solution.py:59
  36.1 1.4 %collective-permute-start.10 = (bf16[32,8192]{1,0:T(8,128)(2,1)S(1)}, bf16[32,8192]{1,0:T(8,128)(2,1)S(1)}, u32[]{:S(2)}, u32[]{:S(2)}) collective-permute-start(bf16[32,8192]{1,0:T(8,128)(2,1)S(1)} %add_convert_fusion.1), channel_id=1, source_target_pairs={{0,1},{1,8},{8,9},{9,0},{2,3},{3,10},{10,11},{11,2},{4,5},{5,12},{... | collective-permute-start | bytes 1572872 | tf_op jit(solution)/shard_map/ppermute | solution.py:59
  37.6 0.8 collective-permute-start.11
  38.4 8.5 %collective-permute-done.2.p2 = bf16[32,8192]{1,0:T(8,128)(2,1)S(1)} collective-permute-done((bf16[32,8192]{1,0:T(8,128)(2,1)S(1)}, bf16[32,8192]{1,0:T(8,128)(2,1)S(1)}, u32[]{:S(2)}, u32[]{:S(2)}) %collective-permute-start.2) | collective-permute-done | bytes 524320 | tf_op jit(solution)/shard_map/ppermute | solution.py:59
  46.8 0.5 middle_sums.2
  47.3 1.4 %collective-permute-start.4 = (bf16[16,8192]{1,0:T(8,128)(2,1)S(1)}, bf16[16,8192]{1,0:T(8,128)(2,1)S(1)}, u32[]{:S(2)}, u32[]{:S(2)}) collective-permute-start(bf16[16,8192]{1,0:T(8,128)(2,1)S(1)} %get-tuple-element.39), channel_id=1, source_target_pairs={{0,1},{1,8},{8,9},{9,0},{2,3},{3,10},{10,11},{11,2},{4,5},{5,12},{... | collective-permute-start | bytes 786440 | tf_op jit(solution)/shard_map/ppermute | solution.py:59
  48.6 0.7 collective-permute-start.5
  49.4 1.0 collective-permute-done.11.m2
  50.4 0.4 middle_sums.3
  51.0 3.2 %collective-permute-start.13 = (bf16[16,9728]{1,0:T(8,128)(2,1)S(1)}, bf16[16,9728]{1,0:T(8,128)(2,1)S(1)}, u32[]{:S(2)}, u32[]{:S(2)}) collective-permute-start(bf16[16,9728]{1,0:T(8,128)(2,1)S(1)} %get-tuple-element.50), channel_id=1, source_target_pairs={{0,6},{2,0},{4,2},{6,4},{1,7},{3,1},{5,3},{7,5},{8,14},{10,8},{12,... | collective-permute-start | bytes 933896 | tf_op jit(solution)/shard_map/ppermute | solution.py:59
  54.3 1.4 %collective-permute-start.6 = (bf16[8,8192]{1,0:T(8,128)(2,1)S(1)}, bf16[8,8192]{1,0:T(8,128)(2,1)S(1)}, u32[]{:S(2)}, u32[]{:S(2)}) collective-permute-start(bf16[8,8192]{1,0:T(8,128)(2,1)S(1)} %add_convert_fusion.7), channel_id=1, source_target_pairs={{0,1},{1,8},{8,9},{9,0},{2,3},{3,10},{10,11},{11,2},{4,5},{5,12},{... | collective-permute-start | bytes 393224 | tf_op jit(solution)/shard_map/ppermute | solution.py:59
  55.8 0.7 collective-permute-start.7
  56.6 2.7 %collective-permute-done.12.refs_6_.z_below = bf16[16,9728]{1,0:T(8,128)(2,1)S(1)} collective-permute-done((bf16[16,9728]{1,0:T(8,128)(2,1)S(1)}, bf16[16,9728]{1,0:T(8,128)(2,1)S(1)}, u32[]{:S(2)}, u32[]{:S(2)}) %collective-permute-start.12) | collective-permute-done | bytes 311328 | tf_op jit(solution)/shard_map/ppermute | solution.py:59
  59.4 3.4 %collective-permute-start.15 = (bf16[8,8192]{1,0:T(8,128)(2,1)S(1)}, bf16[8,8192]{1,0:T(8,128)(2,1)S(1)}, u32[]{:S(2)}, u32[]{:S(2)}) collective-permute-start(bf16[8,8192]{1,0:T(8,128)(2,1)S(1)} %add_convert_fusion.4), channel_id=1, source_target_pairs={{0,6},{2,0},{4,2},{6,4},{1,7},{3,1},{5,3},{7,5},{8,14},{10,8},{12,... | collective-permute-start | bytes 393224 | tf_op jit(solution)/shard_map/ppermute | solution.py:59
  62.9 2.6 %collective-permute-done.14.refs_8_ = bf16[8,8192]{1,0:T(8,128)(2,1)S(1)} collective-permute-done((bf16[8,8192]{1,0:T(8,128)(2,1)S(1)}, bf16[8,8192]{1,0:T(8,128)(2,1)S(1)}, u32[]{:S(2)}, u32[]{:S(2)}) %collective-permute-start.14) | collective-permute-done | bytes 131104 | tf_op jit(solution)/shard_map/ppermute | solution.py:59
  65.6 1.3 %compressed_beams.1 = bf16[8,16,2048]{2,1,0:T(8,128)(2,1)S(1)} custom-call(f32[16,8192]{1,0:T(8,128)S(1)} %get-tuple-element.38.refs_0_, bf16[16,8192]{1,0:T(8,128)(2,1)S(1)} %collective-permute-done.4.refs_1_, bf16[16,8192]{1,0:T(8,128)(2,1)S(1)} %collective-permute-done.5.refs_2_, bf16[8,8192]{1,0:T(8,128)(2,1)S(1)} %collective-permute-done.6.refs_3_, ...), custom_call_target="tpu_custom_call" | custom-call | tf_op jit(solution)/shard_map/compressed_beams/pallas_call | solution.py:290
  66.8 1.4 %collective-permute-start.16 = (bf16[8,16,2048]{2,1,0:T(8,128)(2,1)S(1)}, bf16[8,16,2048]{2,1,0:T(8,128)(2,1)}, u32[]{:S(2)}, u32[]{:S(2)}) collective-permute-start(bf16[8,16,2048]{2,1,0:T(8,128)(2,1)S(1)} %compressed_beams.1), channel_id=1, source_target_pairs={{0,1},{1,0},{2,3},{3,2},{4,5},{5,4},{6,7},{7,6},{8,9},{9,8},{10,11... | collective-permute-start | bytes 1572872 | tf_op jit(solution)/shard_map/ppermute | solution.py:465
  68.2 14.5 %all_to_all.10.own = bf16[8,16,2048]{2,1,0:T(8,128)(2,1)S(1)} all-to-all(bf16[8,16,2048]{2,1,0:T(8,128)(2,1)S(1)} %compressed_beams.1), channel_id=1, replica_groups=mesh['sub'=8,'y_hi'=2,'z'=4,'y_lo'=2] {'sub'}, dimensions={0} | all-to-all | bytes 1048576 | tf_op jit(solution)/shard_map/all_to_all | solution.py:504
  82.7 4.8 %collective-permute-start.17 = (bf16[8,16,2048]{2,1,0:T(8,128)(2,1)S(1)}, bf16[8,16,2048]{2,1,0:T(8,128)(2,1)}, u32[]{:S(2)}, u32[]{:S(2)}) collective-permute-start(bf16[8,16,2048]{2,1,0:T(8,128)(2,1)S(1)} %all_to_all.10.own), channel_id=1, source_target_pairs={{1,2},{2,1},{3,4},{4,3},{5,6},{6,5},{7,8},{8,7},{9,10},{10,9},{11,... | collective-permute-start | bytes 1572872 | tf_op jit(solution)/shard_map/ppermute | solution.py:471
  87.5 3.5 %all-to-all-start = ((bf16[8,16,2048]{2,1,0:T(8,128)(2,1)}), bf16[8,16,2048]{2,1,0:T(8,128)(2,1)S(1)}, u32[]{:S(2)}, u32[]{:S(2)}) async-start(bf16[8,16,2048]{2,1,0:T(8,128)(2,1)} %collective-permute-done.16), calls=%async_computation | async-start | bytes 1048576 | tf_op jit(solution)/shard_map/all_to_all | solution.py:505
  91.1 1.0 copy-done.1
  92.0 5.2 %merge_tables.1 = (bf16[288,256]{1,0:T(8,128)(2,1)}, f32[288,128]{1,0:T(8,128)}, f32[288,128]{1,0:T(8,128)}, f32[288,128]{1,0:T(8,128)}, f32[288,128]{1,0:T(8,128)}) custom-call(s32[1]{0:T(128)} %bitcast.1.start_ref, f32[16,256]{1,0:T(8,128)S(1)} %get-tuple-element.53.own_ref, bf16[64,8448]{1,0:T(8,128)(2,1)S(1)} %collective-permute-done.8.p1.y_below, ...), custom_call_target="tpu_custom_call" | custom-call | tf_op jit(solution)/shard_map/merge_tables/pallas_call | solution.py:379
  97.2 4.1 %all-to-all-done.near = bf16[8,16,2048]{2,1,0:T(8,128)(2,1)S(1)} async-done(((bf16[8,16,2048]{2,1,0:T(8,128)(2,1)}), bf16[8,16,2048]{2,1,0:T(8,128)(2,1)S(1)}, u32[]{:S(2)}, u32[]{:S(2)}) %all-to-all-start) | async-done | bytes 524320 | tf_op jit(solution)/shard_map/all_to_all | solution.py:505
  101.3 6.0 %merge.1 = f32[64,2,2048]{2,1,0:T(2,128)} custom-call(bf16[8,16,2048]{2,1,0:T(8,128)(2,1)S(1)} %all-to-all-done.near, bf16[8,16,2048]{2,1,0:T(8,128)(2,1)S(1)} %all_to_all.10.own, bf16[8,16,2048]{2,1,0:T(8,128)(2,1)} %collective-permute-done.17.far, bf16[288,256]{1,0:T(8,128)(2,1)} %get-tuple-element.54.matrix, f32[288,128]{1,0:T(8,128)} %get-tuple-element.55.near_cos, ...), custom_call_target="tpu_custom_call" | custom-call | tf_op jit(solution)/shard_map/merge/pallas_call | solution.py:451
  (33 shorter events, 0.9 us)
Async XLA Ops:
  5.1 27.3 %collective-permute-start = (bf16[64,8192]{1,0:T(8,128)(2,1)S(1)}, bf16[64,8192]{1,0:T(8,128)(2,1)S(1)}, u32[]{:S(2)}, u32[]{:S(2)}) collective-permute-start(bf16[64,8192]{1,0:T(8,128)(2,1)S(1)} %get-tuple-element.34), channel_id=1, source_target_pairs={{0,2},{2,4},{4,6},{6,0},{1,3},{3,5},{5,7},{7,1},{8,10},{10,12},{12... | collective-permute-start | bytes 3145736 | tf_op jit(solution)/shard_map/ppermute | solution.py:59
  7.1 25.5 %collective-permute-start.1 = (bf16[64,8192]{1,0:T(8,128)(2,1)S(1)}, bf16[64,8192]{1,0:T(8,128)(2,1)S(1)}, u32[]{:S(2)}, u32[]{:S(2)}) collective-permute-start(bf16[64,8192]{1,0:T(8,128)(2,1)S(1)} %get-tuple-element.35), channel_id=1, source_target_pairs={{0,6},{2,0},{4,2},{6,4},{1,7},{3,1},{5,3},{7,5},{8,14},{10,8},{12,... | collective-permute-start | bytes 3145736 | tf_op jit(solution)/shard_map/ppermute | solution.py:59
  9.3 26.7 %collective-permute-start.8 = (bf16[64,8448]{1,0:T(8,128)(2,1)S(1)}, bf16[64,8448]{1,0:T(8,128)(2,1)S(1)}, u32[]{:S(2)}, u32[]{:S(2)}) collective-permute-start(bf16[64,8448]{1,0:T(8,128)(2,1)S(1)} %get-tuple-element.44), channel_id=1, source_target_pairs={{0,1},{1,8},{8,9},{9,0},{2,3},{3,10},{10,11},{11,2},{4,5},{5,12},{... | collective-permute-start | bytes 3244040 | tf_op jit(solution)/shard_map/ppermute | solution.py:59
  10.5 26.9 %collective-permute-start.9 = (bf16[64,8448]{1,0:T(8,128)(2,1)S(1)}, bf16[64,8448]{1,0:T(8,128)(2,1)S(1)}, u32[]{:S(2)}, u32[]{:S(2)}) collective-permute-start(bf16[64,8448]{1,0:T(8,128)(2,1)S(1)} %get-tuple-element.45), channel_id=1, source_target_pairs={{0,9},{1,0},{8,1},{9,8},{2,11},{3,2},{10,3},{11,10},{4,13},{5,4},{... | collective-permute-start | bytes 3244040 | tf_op jit(solution)/shard_map/ppermute | solution.py:59
  32.5 14.4 %collective-permute-start.2 = (bf16[32,8192]{1,0:T(8,128)(2,1)S(1)}, bf16[32,8192]{1,0:T(8,128)(2,1)S(1)}, u32[]{:S(2)}, u32[]{:S(2)}) collective-permute-start(bf16[32,8192]{1,0:T(8,128)(2,1)S(1)} %add_convert_fusion.3), channel_id=1, source_target_pairs={{0,2},{2,4},{4,6},{6,0},{1,3},{3,5},{5,7},{7,1},{8,10},{10,12},{12... | collective-permute-start | bytes 1572872 | tf_op jit(solution)/shard_map/ppermute | solution.py:59
  32.7 14.2 %collective-permute-start.3 = (bf16[32,8192]{1,0:T(8,128)(2,1)S(1)}, bf16[32,8192]{1,0:T(8,128)(2,1)S(1)}, u32[]{:S(2)}, u32[]{:S(2)}) collective-permute-start(bf16[32,8192]{1,0:T(8,128)(2,1)S(1)} %add_convert_fusion.2), channel_id=1, source_target_pairs={{0,6},{2,0},{4,2},{6,4},{1,7},{3,1},{5,3},{7,5},{8,14},{10,8},{12,... | collective-permute-start | bytes 1572872 | tf_op jit(solution)/shard_map/ppermute | solution.py:59
  36.1 13.3 %collective-permute-start.10 = (bf16[32,8192]{1,0:T(8,128)(2,1)S(1)}, bf16[32,8192]{1,0:T(8,128)(2,1)S(1)}, u32[]{:S(2)}, u32[]{:S(2)}) collective-permute-start(bf16[32,8192]{1,0:T(8,128)(2,1)S(1)} %add_convert_fusion.1), channel_id=1, source_target_pairs={{0,1},{1,8},{8,9},{9,0},{2,3},{3,10},{10,11},{11,2},{4,5},{5,12},{... | collective-permute-start | bytes 1572872 | tf_op jit(solution)/shard_map/ppermute | solution.py:59
  37.6 12.8 %collective-permute-start.11 = (bf16[32,8192]{1,0:T(8,128)(2,1)S(1)}, bf16[32,8192]{1,0:T(8,128)(2,1)S(1)}, u32[]{:S(2)}, u32[]{:S(2)}) collective-permute-start(bf16[32,8192]{1,0:T(8,128)(2,1)S(1)} %add_convert_fusion), channel_id=1, source_target_pairs={{0,9},{1,0},{8,1},{9,8},{2,11},{3,2},{10,3},{11,10},{4,13},{5,4},{... | collective-permute-start | bytes 1572872 | tf_op jit(solution)/shard_map/ppermute | solution.py:59
  47.3 7.0 %collective-permute-start.4 = (bf16[16,8192]{1,0:T(8,128)(2,1)S(1)}, bf16[16,8192]{1,0:T(8,128)(2,1)S(1)}, u32[]{:S(2)}, u32[]{:S(2)}) collective-permute-start(bf16[16,8192]{1,0:T(8,128)(2,1)S(1)} %get-tuple-element.39), channel_id=1, source_target_pairs={{0,1},{1,8},{8,9},{9,0},{2,3},{3,10},{10,11},{11,2},{4,5},{5,12},{... | collective-permute-start | bytes 786440 | tf_op jit(solution)/shard_map/ppermute | solution.py:59
  48.6 7.1 %collective-permute-start.5 = (bf16[16,8192]{1,0:T(8,128)(2,1)S(1)}, bf16[16,8192]{1,0:T(8,128)(2,1)S(1)}, u32[]{:S(2)}, u32[]{:S(2)}) collective-permute-start(bf16[16,8192]{1,0:T(8,128)(2,1)S(1)} %get-tuple-element.40), channel_id=1, source_target_pairs={{0,9},{1,0},{8,1},{9,8},{2,11},{3,2},{10,3},{11,10},{4,13},{5,4},{... | collective-permute-start | bytes 786440 | tf_op jit(solution)/shard_map/ppermute | solution.py:59
  50.9 12.0 %copy-start.4 = (f32[2,16384]{1,0:T(2,128)S(1)}, f32[2,16384]{1,0:T(2,128)}, u32[]{:S(2)}) copy-start(f32[2,16384]{1,0:T(2,128)} %param.9) | copy-start | bytes 393220
  50.9 14.7 %copy-start.2 = (bf16[256,256]{1,0:T(8,128)(2,1)S(1)}, bf16[256,256]{1,0:T(8,128)(2,1)}, u32[]{:S(2)}) copy-start(bf16[256,256]{1,0:T(8,128)(2,1)} %constant.12.clone.refs_10_) | copy-start | bytes 393220
  50.9 14.7 %copy-start.3 = (f32[2,128,128]{2,1,0:T(8,128)S(1)}, f32[2,128,128]{2,1,0:T(8,128)}, u32[]{:S(2)}) copy-start(f32[2,128,128]{2,1,0:T(8,128)} %constant.13.clone.refs_11_) | copy-start | bytes 393220
  50.9 8.4 %collective-permute-start.12 = (bf16[16,9728]{1,0:T(8,128)(2,1)S(1)}, bf16[16,9728]{1,0:T(8,128)(2,1)S(1)}, u32[]{:S(2)}, u32[]{:S(2)}) collective-permute-start(bf16[16,9728]{1,0:T(8,128)(2,1)S(1)} %get-tuple-element.49), channel_id=1, source_target_pairs={{0,2},{2,4},{4,6},{6,0},{1,3},{3,5},{5,7},{7,1},{8,10},{10,12},{12... | collective-permute-start | bytes 933896 | tf_op jit(solution)/shard_map/ppermute | solution.py:59
  51.0 8.4 %collective-permute-start.13 = (bf16[16,9728]{1,0:T(8,128)(2,1)S(1)}, bf16[16,9728]{1,0:T(8,128)(2,1)S(1)}, u32[]{:S(2)}, u32[]{:S(2)}) collective-permute-start(bf16[16,9728]{1,0:T(8,128)(2,1)S(1)} %get-tuple-element.50), channel_id=1, source_target_pairs={{0,6},{2,0},{4,2},{6,4},{1,7},{3,1},{5,3},{7,5},{8,14},{10,8},{12,... | collective-permute-start | bytes 933896 | tf_op jit(solution)/shard_map/ppermute | solution.py:59
  54.3 8.6 %collective-permute-start.6 = (bf16[8,8192]{1,0:T(8,128)(2,1)S(1)}, bf16[8,8192]{1,0:T(8,128)(2,1)S(1)}, u32[]{:S(2)}, u32[]{:S(2)}) collective-permute-start(bf16[8,8192]{1,0:T(8,128)(2,1)S(1)} %add_convert_fusion.7), channel_id=1, source_target_pairs={{0,1},{1,8},{8,9},{9,0},{2,3},{3,10},{10,11},{11,2},{4,5},{5,12},{... | collective-permute-start | bytes 393224 | tf_op jit(solution)/shard_map/ppermute | solution.py:59
  55.8 7.1 %collective-permute-start.7 = (bf16[8,8192]{1,0:T(8,128)(2,1)S(1)}, bf16[8,8192]{1,0:T(8,128)(2,1)S(1)}, u32[]{:S(2)}, u32[]{:S(2)}) collective-permute-start(bf16[8,8192]{1,0:T(8,128)(2,1)S(1)} %add_convert_fusion.6), channel_id=1, source_target_pairs={{0,9},{1,0},{8,1},{9,8},{2,11},{3,2},{10,3},{11,10},{4,13},{5,4},{... | collective-permute-start | bytes 393224 | tf_op jit(solution)/shard_map/ppermute | solution.py:59
  59.3 6.2 %collective-permute-start.14 = (bf16[8,8192]{1,0:T(8,128)(2,1)S(1)}, bf16[8,8192]{1,0:T(8,128)(2,1)S(1)}, u32[]{:S(2)}, u32[]{:S(2)}) collective-permute-start(bf16[8,8192]{1,0:T(8,128)(2,1)S(1)} %add_convert_fusion.5), channel_id=1, source_target_pairs={{0,2},{2,4},{4,6},{6,0},{1,3},{3,5},{5,7},{7,1},{8,10},{10,12},{12... | collective-permute-start | bytes 393224 | tf_op jit(solution)/shard_map/ppermute | solution.py:59
  59.4 7.4 %copy-start = (bf16[16,9728]{1,0:T(8,128)(2,1)}, bf16[16,9728]{1,0:T(8,128)(2,1)S(1)}, u32[]{:S(2)}) copy-start(bf16[16,9728]{1,0:T(8,128)(2,1)S(1)} %collective-permute-done.13.refs_7_.z_above) | copy-start | bytes 933892
  59.4 6.1 %collective-permute-start.15 = (bf16[8,8192]{1,0:T(8,128)(2,1)S(1)}, bf16[8,8192]{1,0:T(8,128)(2,1)S(1)}, u32[]{:S(2)}, u32[]{:S(2)}) collective-permute-start(bf16[8,8192]{1,0:T(8,128)(2,1)S(1)} %add_convert_fusion.4), channel_id=1, source_target_pairs={{0,6},{2,0},{4,2},{6,4},{1,7},{3,1},{5,3},{7,5},{8,14},{10,8},{12,... | collective-permute-start | bytes 393224 | tf_op jit(solution)/shard_map/ppermute | solution.py:59
  66.8 20.7 %collective-permute-start.16 = (bf16[8,16,2048]{2,1,0:T(8,128)(2,1)S(1)}, bf16[8,16,2048]{2,1,0:T(8,128)(2,1)}, u32[]{:S(2)}, u32[]{:S(2)}) collective-permute-start(bf16[8,16,2048]{2,1,0:T(8,128)(2,1)S(1)} %compressed_beams.1), channel_id=1, source_target_pairs={{0,1},{1,0},{2,3},{3,2},{4,5},{5,4},{6,7},{7,6},{8,9},{9,8},{10,11... | collective-permute-start | bytes 1572872 | tf_op jit(solution)/shard_map/ppermute | solution.py:465
  82.7 18.6 %collective-permute-start.17 = (bf16[8,16,2048]{2,1,0:T(8,128)(2,1)S(1)}, bf16[8,16,2048]{2,1,0:T(8,128)(2,1)}, u32[]{:S(2)}, u32[]{:S(2)}) collective-permute-start(bf16[8,16,2048]{2,1,0:T(8,128)(2,1)S(1)} %all_to_all.10.own), channel_id=1, source_target_pairs={{1,2},{2,1},{3,4},{4,3},{5,6},{6,5},{7,8},{8,7},{9,10},{10,9},{11,... | collective-permute-start | bytes 1572872 | tf_op jit(solution)/shard_map/ppermute | solution.py:471
  87.5 13.8 %all-to-all-start = ((bf16[8,16,2048]{2,1,0:T(8,128)(2,1)}), bf16[8,16,2048]{2,1,0:T(8,128)(2,1)S(1)}, u32[]{:S(2)}, u32[]{:S(2)}) async-start(bf16[8,16,2048]{2,1,0:T(8,128)(2,1)} %collective-permute-done.16), calls=%async_computation | async-start | bytes 1048576 | tf_op jit(solution)/shard_map/all_to_all | solution.py:505
  91.0 1.0 copy-start.1

commit v4 on v3

--- a/solution.py
+++ b/solution.py
@@ -17,13 +17,14 @@
 BAND = 8
 PSUB = 2048
 RING = 4
-HALF = NR // 2
-READS = 4
+WIDTHS = (8192, 8192)
+READS = 8
 READ = NR // READS
 STEP = 2048
 SLAB = NR // 8
 COLS = 512
 FIELDS = 256
+CARRIED = 128
 SIDE = 144
 BEAM_COMP = ("y_hi", "z", "y_lo")
 SUB_BEAM_COMP = ("sub", "y_hi", "z", "y_lo")
@@ -88,6 +89,19 @@
     return jnp.concatenate(picked, 0).astype(BF)
 
 
+def spans(read):
+    parts = []
+    place = read * READ
+    while place < (read + 1) * READ:
+        half = int(place >= WIDTHS[0])
+        limit = min((read + 1) * READ, place + STEP)
+        if half == 0:
+            limit = min(limit, WIDTHS[0])
+        parts.append((half, place - read * READ, place - half * WIDTHS[0], limit - place))
+        place = limit
+    return parts
+
+
 def split_three(table):
     parts = []
     for _ in range(3):
@@ -95,6 +109,23 @@
         parts.append(part)
         table = table - part.astype(F4)
     return parts
+
+
+def carried_tables(parts):
+    even = lax.axis_index("y_lo") == 0
+    row = lax.broadcasted_iota(jnp.int32, (FIELDS, CARRIED), 0)
+    lane = lax.broadcasted_iota(jnp.int32, (FIELDS, CARRIED), 1)
+    side, k = lane % 32 // 16, lane % 16
+    last = side * 128 + jnp.where(k < 8, k + 8, k + 32)
+    first = side * 128 + jnp.where(k < 8, k, k + 8)
+    rows = []
+    for source in (jnp.where(even, last, first), jnp.where(even, first, last)):
+        total = jnp.zeros((16, CARRIED), F4)
+        for term, part in enumerate(parts):
+            pick = jnp.where((row == source) & (lane // 32 == term), 1.0, 0.0).astype(BF)
+            total = total + jnp.dot(part, pick, preferred_element_type=F4)
+        rows.append(total)
+    return jnp.concatenate([*rows, jnp.zeros((32, CARRIED), F4)], 0).astype(BF)
 
 
 def opening_kernel(angle_ref, offset_ref, band_ref, delay_ref, raw_ref, *refs):
@@ -129,26 +160,22 @@
         table[0:1, cols] = offset_landed[side : side + 1, :].astype(F4)
         table[1:9, cols] = band_landed[side]
         table[9:10, cols] = delay_landed[side : side + 1, :]
-    parts = split_three(table[...])
-    packed = jnp.concatenate([*parts, jnp.zeros_like(parts[0])], 0)
+    packed = carried_tables(split_three(table[...]))
     for out in outs[2:]:
-        out[:, HALF:] = packed
+        out[:, WIDTHS[1] :] = packed
+    matrices = [beam_matrix(weights, SENT, half == 0) for half in range(2)]
     for k in range(READS):
-        half = k // (READS // 2)
-        matrix = beam_matrix(weights, SENT, half == 0)
         read(k).wait()
-        base = k * READ - half * HALF
-        for part in range(READ // STEP):
-            raw = landed[k, :, :, part * STEP : (part + 1) * STEP].reshape(256, STEP)
-            total = jnp.dot(matrix, raw, preferred_element_type=F4).astype(BF)
-            cols = slice(base + part * STEP, base + (part + 1) * STEP)
-            outs[2 * half][:, cols] = total[:64]
-            outs[2 * half + 1][:, cols] = total[64:]
+        for half, source, target, size in spans(k):
+            raw = landed[k, :, :, source : source + size].reshape(256, size)
+            total = jnp.dot(matrices[half], raw, preferred_element_type=F4).astype(BF)
+            outs[2 * half][:, target : target + size] = total[:64]
+            outs[2 * half + 1][:, target : target + size] = total[64:]
 
 
 def opening_sums(raw, *small):
     vmem = pl.BlockSpec(memory_space=pltpu.VMEM)
-    outs = [jax.ShapeDtypeStruct((64, c), BF) for c in (HALF, HALF, HALF + FIELDS, HALF + FIELDS)]
+    outs = [jax.ShapeDtypeStruct((64, c), BF) for c in (WIDTHS[0],) * 2 + (WIDTHS[1] + CARRIED,) * 2]
     outs += [jax.ShapeDtypeStruct((2, 128, 256), F4), jax.ShapeDtypeStruct((16, FIELDS), F4)]
     results = pl.pallas_call(
         opening_kernel,
@@ -165,26 +192,24 @@
 
 
 def later_kernel(weights, raw_ref, *outs):
-    steps = pl.num_programs(0) // 2
-    for half in range(2):
-
-        @pl.when(pl.program_id(0) // steps == half)
+    for k in range(READS):
+
+        @pl.when(pl.program_id(0) == k)
         def _():
-            matrix = beam_matrix(weights, KEPT, half == 0)
-            raw = raw_ref[...].reshape(256, READ)
-            total = jnp.dot(matrix, raw, preferred_element_type=F4).astype(BF)
-            step = lax.rem(pl.program_id(0), steps)
-            cols = pl.ds(pl.multiple_of(step * READ, READ), READ)
-            start = 0
-            for out in outs[3 * half : 3 * half + 3]:
-                size = out.shape[0]
-                out[:, cols] = total[start : start + size]
-                start += size
+            for half, source, target, width in spans(k):
+                matrix = beam_matrix(weights, KEPT, half == 0)
+                raw = raw_ref[:, :, source : source + width].reshape(256, width)
+                total = jnp.dot(matrix, raw, preferred_element_type=F4).astype(BF)
+                start = 0
+                for out in outs[3 * half : 3 * half + 3]:
+                    size = out.shape[0]
+                    out[:, target : target + width] = total[start : start + size]
+                    start += size
 
 
 def later_sums(weights, raw):
     vmem = pl.BlockSpec(memory_space=pltpu.VMEM)
-    outs = [jax.ShapeDtypeStruct((n, HALF), BF) for n in KEPT_ROWS * 2]
+    outs = [jax.ShapeDtypeStruct((n, c), BF) for c in WIDTHS for n in KEPT_ROWS]
     kept = pl.pallas_call(
         later_kernel,
         grid=(READS,),
@@ -216,19 +241,19 @@
         q3[:, cols] = high[24:].astype(BF)
         return carry
 
-    lax.fori_loop(0, HALF // tile, step, 0)
-    if plus.shape[1] > HALF:
+    width = own.shape[1]
+    lax.fori_loop(0, width // tile, step, 0)
+    if plus.shape[1] > width:
         for j, received in enumerate((p1, m1)):
-            for k in range(3):
-                first = HALF + (3 * j + k) * FIELDS
-                part = received[16 * k : 16 * k + 16, HALF:]
-                plus[:, first : first + FIELDS] = part
-                minus[:, first : first + FIELDS] = part
+            cols = slice(width + j * CARRIED, width + (j + 1) * CARRIED)
+            plus[:, cols] = received[16:32, width:]
+            minus[:, cols] = received[16:32, width:]
 
 
 def middle_sums(own, p1, m1, p2, m2):
-    wide = HALF + 6 * (p1.shape[1] - HALF)
-    outs = ((16, wide, BF), (16, wide, BF), (8, HALF, BF), (8, HALF, BF), (16, HALF, F4))
+    width = own.shape[1]
+    wide = width + 2 * (p1.shape[1] - width)
+    outs = ((16, wide, BF), (16, wide, BF), (8, width, BF), (8, width, BF), (16, width, F4))
     vmem = pl.BlockSpec(memory_space=pltpu.VMEM)
     return pl.pallas_call(
         middle_kernel,
@@ -242,15 +267,15 @@
 
 def compress_kernel(*refs):
     ins, (form_ref, turn_ref, filter_ref, out, lines, bins) = refs[:10], refs[10:]
-    for half in range(2):
+    for half, width in enumerate(WIDTHS):
         keep, p3, m3, p4, m4 = ins[5 * half : 5 * half + 5]
         sums = (
-            keep[:8] + m3[:, :HALF].astype(F4)[8:] + p4[...].astype(F4),
-            keep[8:] + p3[:, :HALF].astype(F4)[8:] + m4[...].astype(F4),
+            keep[:8] + m3[:, :width].astype(F4)[8:] + p4[...].astype(F4),
+            keep[8:] + p3[:, :width].astype(F4)[8:] + m4[...].astype(F4),
         )
         for part in range(2):
-            for k in range(64):
-                row = (half * 64 + k) * 8
+            for k in range(width // 128):
+                row = half * WIDTHS[0] // 16 + k * 8
                 lines[part, row : row + 8, :] = sums[part][:, k * 128 : (k + 1) * 128]
     form = form_ref[...]
     cos_part, sin_part = turn_ref[0], turn_ref[1]
@@ -307,7 +332,7 @@
 
 
 def table_kernel(start_ref, own_ref, y_below, y_above, z_below, z_above, *refs):
-    matrix, near_cos, near_sin, far_cos, far_sin, lines = refs
+    first_matrix, matrix, near_cos, near_sin, far_cos, far_sin, lines = refs
     y_hi, z = lax.axis_index("y_hi"), lax.axis_index("z")
     even = lax.axis_index("y_lo") == 0
 
@@ -315,14 +340,18 @@
         padded = jnp.concatenate([fields, jnp.zeros((112, 256), F4)], 0)
         return jnp.concatenate([padded[:, :128].T, padded[:, 128:].T], 0)
 
+    def joined(parts):
+        parts = parts.astype(F4)
+        total = parts[:, :32] + parts[:, 32:64] + parts[:, 64:96]
+        total = jnp.concatenate([total, jnp.zeros((16, 96), F4)], 1)
+        return jnp.concatenate([total, jnp.zeros((112, 128), F4)], 0).T
+
     def from_rows(ref):
-        parts = ref[:48, HALF:].astype(F4)
-        return parts[:16] + parts[16:32] + parts[32:]
+        return joined(ref[:16, WIDTHS[1] :])
 
     def from_cols(ref, j):
-        first = HALF + 3 * j * FIELDS
-        parts = ref[:, first : first + 3 * FIELDS].astype(F4)
-        return parts[:, :256] + parts[:, 256:512] + parts[:, 512:]
+        first = WIDTHS[1] + j * CARRIED
+        return joined(ref[:, first : first + CARRIED])
 
     near = jnp.where(even, from_rows(y_above), from_rows(y_below))
     left = jnp.where(z > 0, from_cols(z_below, 1), from_cols(z_below, 0))
@@ -330,22 +359,23 @@
     left = jnp.where((z > 0) | (y_hi > 0), left, 0.0)
     right = jnp.where((z < RING - 1) | (y_hi == 0), right, 0.0)
     left, right = sided(near, jnp.where(even, left, right))
-    own, left, right = columns(own_ref[...]), columns(left), columns(right)
+    own = columns(own_ref[...])
 
     def piece(source, side, first, count, shift):
-        rows = source[side * 128 + first : side * 128 + first + count]
+        start = side * (128 if source is own else 16) + first
+        rows = source[start : start + count]
         field = lax.broadcasted_iota(jnp.int32, rows.shape, 1)
         return rows + jnp.where(field == 0, float(shift), 0.0)
 
     for side in range(2):
         row = side * SIDE
         for source, first, count, shift in (
-            (left, 8, 8, 0),
+            (left, 0, 8, 0),
             (own, 0, 16, 8),
             (right, 0, 8, 16),
-            (left, 40, 8, -8),
+            (left, 8, 8, -8),
             (own, 16, 32, 8),
-            (right, 16, 8, 24),
+            (right, 8, 8, 24),
             (own, 48, 64, 8),
         ):
             lines[row : row + count, :] = piece(source, side, first, count, shift)
@@ -362,6 +392,22 @@
         band = band + jnp.where(place == float(tap), table[:, tap + 1 : tap + 2], 0.0)
     upper = band.astype(BF).astype(F4)
     matrix[...] = jnp.where(term == 1, band - upper, upper).astype(BF)
+    lane = lax.broadcasted_iota(jnp.int32, (32, 128), 1)
+    term, inner = lane // 48, lane % 48
+    block = jnp.where(even, 2 - inner // 16, inner // 16)
+    child = (block * 8 + inner % 8).astype(F4)
+    for side in range(2):
+        fields = lines[side * SIDE : side * SIDE + 32, :]
+        band = jnp.zeros((32, 128), F4)
+        for tap in range(BAND):
+            hit = child - fields[:, 0:1] == float(tap)
+            band = band + jnp.where(hit, fields[:, tap + 1 : tap + 2], 0.0)
+        upper = band.astype(BF).astype(F4)
+        band = jnp.where(term == 1, band - upper, upper)
+        for part in range(2):
+            row = side * 64 + part * 32
+            own_part = inner // 8 % 2 == part
+            first_matrix[row : row + 32, :] = jnp.where(own_part, band, 0.0).astype(BF)
     delay = table[:, 9:10]
     lane = lax.broadcasted_iota(jnp.int32, (rows, 128), 1).astype(F4)
     step = delay * (lane * (1.0 / NR))
@@ -380,17 +426,21 @@
         table_kernel,
         grid=(1,),
         in_specs=[pl.BlockSpec(memory_space=pltpu.SMEM)] + [vmem] * 5,
-        out_specs=[pl.BlockSpec((rows, 256), lambda i: (0, 0))]
+        out_specs=[pl.BlockSpec((128, 128), lambda i: (0, 0))]
+        + [pl.BlockSpec((rows, 256), lambda i: (0, 0))]
         + [pl.BlockSpec((rows, 128), lambda i: (0, 0))] * 4,
-        out_shape=[pltpu.HBM((rows, 256), BF)] + [pltpu.HBM((rows, 128), F4)] * 4,
+        out_shape=[pltpu.HBM((128, 128), BF), pltpu.HBM((rows, 256), BF)]
+        + [pltpu.HBM((rows, 128), F4)] * 4,
         scratch_shapes=[pltpu.VMEM((rows, 128), F4)],
         compiler_params=params(12),
         name="merge_tables",
     )(start, own, *received)
 
 
-def merge_kernel(near, own, far, matrix, near_cos, near_sin, far_cos, far_sin, out, lines):
+def merge_kernel(near, own, far, first_matrix, matrix, *refs):
+    near_cos, near_sin, far_cos, far_sin, out, lines = refs
     groups = COLS // 128
+    place = pl.ds(pl.multiple_of(pl.program_id(0) * COLS, COLS), COLS)
     shift = lax.rem(128 - groups * pl.program_id(0), 128)
     cosines = pltpu.roll(near_cos[...], shift, 1)
     sines = pltpu.roll(near_sin[...], shift, 1)
@@ -405,32 +455,32 @@
             imag_parts.append(b * cosine + a * sine)
         return jnp.concatenate(real_parts, 1), jnp.concatenate(imag_parts, 1)
 
-    def stacked(image, exact):
+    def stacked(image):
         upper = image.astype(BF)
-        if exact:
-            return jnp.concatenate([upper, upper], 0)
         lower = (image - upper.astype(F4)).astype(BF)
         return jnp.concatenate([upper, upper, lower], 0)
 
-    zeros = jnp.zeros((8, COLS), F4)
-    images = []
-    for sub in range(8):
-        left, right = sided(near[sub].astype(F4), far[sub].astype(F4))
-        parts = (left, own[sub].astype(F4), right)
-        images.append(
-            tuple(jnp.concatenate([p[8 * q : 8 * q + 8] for p in parts] + [zeros], 0) for q in (0, 1))
-        )
-    for first, count, terms in ((0, 32, 64), (32, 48, 96), (80, 64, 144)):
+    def first_blend(side, sub):
+        image = jnp.concatenate([ref[sub, :, place] for ref in (near, own, far)], 0)
+        band = first_matrix[side * 64 : side * 64 + 64, :96]
+        both = jnp.dot(band, jnp.concatenate([image, image], 0), preferred_element_type=F4)
+        return both[:32], both[32:]
+
+    images = range(8)
+    for first, count, terms in ((0, 32, 0), (32, 48, 96), (80, 64, 144)):
         merged = [None] * (len(images) // 2)
         for side in range(2):
             start = side * SIDE + first
-            band = matrix[start : start + count, :terms]
             cosine, sine = phases(start, count)
             for group in range(len(merged)):
-                real_in, imag_in = (
-                    jnp.dot(band, stacked(part, first == 0), preferred_element_type=F4)
-                    for part in images[2 * group + side]
-                )
+                image = images[2 * group + side]
+                if terms:
+                    band = matrix[start : start + count, :terms]
+                    real_in, imag_in = (
+                        jnp.dot(band, stacked(part), preferred_element_type=F4) for part in image
+                    )
+                else:
+                    real_in, imag_in = first_blend(side, image)
                 real_out = cosine * real_in - sine * imag_in
                 imag_out = sine * real_in + cosine * imag_in
                 if side:
@@ -446,16 +496,18 @@
 
 def merge(near, own, far, tables):
     rows = 2 * SIDE
-    image = pl.BlockSpec((8, 16, COLS), lambda i: (0, 0, i))
+    image = pl.BlockSpec(memory_space=pltpu.VMEM)
     whole = pl.BlockSpec((rows, 128), lambda i: (0, 0))
     return pl.pallas_call(
         merge_kernel,
         grid=(SLAB // COLS,),
-        in_specs=[image] * 3 + [pl.BlockSpec((rows, 256), lambda i: (0, 0))] + [whole] * 4,
+        in_specs=[image] * 3
+        + [pl.BlockSpec((128, 128), lambda i: (0, 0)), pl.BlockSpec((rows, 256), lambda i: (0, 0))]
+        + [whole] * 4,
         out_specs=pl.BlockSpec((64, 2, COLS), lambda i: (0, 0, i)),
         out_shape=jax.ShapeDtypeStruct((64, 2, SLAB), F4),
         scratch_shapes=[pltpu.VMEM((COLS // 128, 128, 128), F4)],
-        compiler_params=params(16),
+        compiler_params=params(24),
         name="merge",
     )(near, own, far, *(pltpu.with_memory_space_constraint(t, pltpu.HBM) for t in tables))
 

time: 108 us -> 106 us (0.981)
  waiting for transfers between devices: 34.3 us -> 32.5 us
    ppermute x16, waiting for transfers between devices: 30.2 us -> 28.5 us  [ring_send(): return lax.ppermute(x, axis, [(k, (k + step) % RING) for k in range(RING)])]
    pallas_call x1, Pallas kernels: 5.78 us -> 6.97 us  [later_sums(): pl.pallas_call(later_kernel, grid=(READS,), in_specs=[vmem, pl.BlockSpec(...]
  transfers between devices with their start and end apart: 19 -> 19, of which waited for: 7 -> 7; matrix products, arithmetic and copies ran while one was open for 1% -> 1% of each run, Pallas kernels for 11% -> 12%
where the time goes in v4:
time: 106 us
  waiting for transfers between devices  32.5 us (31%)
  starting transfers between devices  32.4 us (31%)
  Pallas kernels  24.6 us (23%)
  blocking collectives  14.5 us (14%)
    ppermute x16, waiting for transfers between devices, ring_send(): return lax.ppermute(x, axis, [(k, (k + step) % RING) for k in range(RING)])  28.5 us
    ppermute x16, starting transfers between devices, ring_send(): return lax.ppermute(x, axis, [(k, (k + step) % RING) for k in range(RING)])  22.8 us
    all_to_all x1, blocking collectives, body(): image = lax.all_to_all(beams, 'sub', 0, 0, tiled=True)  14.5 us
    pallas_call x1, Pallas kernels, later_sums(): pl.pallas_call(later_kernel, grid=(READS,), in_specs=[vmem, pl.BlockSpec(...  6.97 us
    pallas_call x1, Pallas kernels, merge(): pl.pallas_call(merge_kernel, grid=(SLAB // COLS,), in_specs=[image] * 3 +...  6 us
    pallas_call x1, Pallas kernels, merge_tables(): pl.pallas_call(table_kernel, grid=(1,), in_specs=[pl.BlockSpec(memory_spa...  5.33 us
    ppermute x1, starting transfers between devices, from_far(): return lax.ppermute(array, BEAM_COMP, steps)  4.69 us
    pallas_call x1, Pallas kernels, opening_sums(): pl.pallas_call(opening_kernel, in_specs=[pl.BlockSpec(memory_space=pltpu....  4.1 us
  transfers between devices with their start and end apart: 19, of which 7 were waited for; matrix products, arithmetic and copies ran while one was open for 1% of the time, Pallas kernels for 12%

profile of v4, /device:TPU:16, one launch (start us, length us, event | category | flops | bytes accessed | tf_op | source)
XLA Modules:
  0.0 105.8 jit_solution(1822795368662140128)
XLA Ops:
  0.0 4.1 %opening_sums.1 = (bf16[64,8192]{1,0:T(8,128)(2,1)S(1)}, bf16[64,8192]{1,0:T(8,128)(2,1)S(1)}, bf16[64,8320]{1,0:T(8,128)(2,1)S(1)}, bf16[64,8320]{1,0:T(8,128)(...) custom-call(f32[128,128]{1,0:T(8,128)} %angle_ref.1, s32[2,112]{1,0:T(2,128)} %offset_ref.1, ...), custom_call_target="tpu_custom_call" | custom-call | tf_op jit(solution)/shard_map/opening_sums/pallas_call | solution.py:180
  4.1 2.0 %collective-permute-start = (bf16[64,8192]{1,0:T(8,128)(2,1)S(1)}, bf16[64,8192]{1,0:T(8,128)(2,1)S(1)}, u32[]{:S(2)}, u32[]{:S(2)}) collective-permute-start(bf16[64,8192]{1,0:T(8,128)(2,1)S(1)} %get-tuple-element.35), channel_id=1, source_target_pairs={{0,2},{2,4},{4,6},{6,0},{1,3},{3,5},{5,7},{7,1},{8,10},{10,12},{12... | collective-permute-start | bytes 3145736 | tf_op jit(solution)/shard_map/ppermute | solution.py:60
  6.1 2.2 %collective-permute-start.1 = (bf16[64,8192]{1,0:T(8,128)(2,1)S(1)}, bf16[64,8192]{1,0:T(8,128)(2,1)S(1)}, u32[]{:S(2)}, u32[]{:S(2)}) collective-permute-start(bf16[64,8192]{1,0:T(8,128)(2,1)S(1)} %get-tuple-element.36), channel_id=1, source_target_pairs={{0,6},{2,0},{4,2},{6,4},{1,7},{3,1},{5,3},{7,5},{8,14},{10,8},{12,... | collective-permute-start | bytes 3145736 | tf_op jit(solution)/shard_map/ppermute | solution.py:60
  8.3 1.3 %collective-permute-start.8 = (bf16[64,8320]{1,0:T(8,128)(2,1)S(1)}, bf16[64,8320]{1,0:T(8,128)(2,1)S(1)}, u32[]{:S(2)}, u32[]{:S(2)}) collective-permute-start(bf16[64,8320]{1,0:T(8,128)(2,1)S(1)} %get-tuple-element.45), channel_id=1, source_target_pairs={{0,1},{1,8},{8,9},{9,0},{2,3},{3,10},{10,11},{11,2},{4,5},{5,12},{... | collective-permute-start | bytes 3194888 | tf_op jit(solution)/shard_map/ppermute | solution.py:60
  9.6 0.7 collective-permute-start.9
  10.3 7.0 %later_sums.1 = (bf16[32,8192]{1,0:T(8,128)(2,1)S(1)}, bf16[32,8192]{1,0:T(8,128)(2,1)S(1)}, bf16[64,8192]{1,0:T(8,128)(2,1)S(1)}, bf16[32,8192]{1,0:T(8,128)(2,...) custom-call(f32[2,128,256]{2,1,0:T(8,128)S(1)} %get-tuple-element.33.weights, ...), custom_call_target="tpu_custom_call" | custom-call | tf_op jit(solution)/shard_map/later_sums/pallas_call | solution.py:213
  17.3 14.1 %collective-permute-done.p1 = bf16[64,8192]{1,0:T(8,128)(2,1)S(1)} collective-permute-done((bf16[64,8192]{1,0:T(8,128)(2,1)S(1)}, bf16[64,8192]{1,0:T(8,128)(2,1)S(1)}, u32[]{:S(2)}, u32[]{:S(2)}) %collective-permute-start) | collective-permute-done | bytes 1048608 | tf_op jit(solution)/shard_map/ppermute | solution.py:60
  31.6 0.1 add_convert_fusion.2
  31.7 3.3 %collective-permute-start.3 = (bf16[32,8192]{1,0:T(8,128)(2,1)S(1)}, bf16[32,8192]{1,0:T(8,128)(2,1)S(1)}, u32[]{:S(2)}, u32[]{:S(2)}) collective-permute-start(bf16[32,8192]{1,0:T(8,128)(2,1)S(1)} %add_convert_fusion.2), channel_id=1, source_target_pairs={{0,6},{2,0},{4,2},{6,4},{1,7},{3,1},{5,3},{7,5},{8,14},{10,8},{12,... | collective-permute-start | bytes 1572872 | tf_op jit(solution)/shard_map/ppermute | solution.py:60
  35.1 1.4 %collective-permute-start.10 = (bf16[32,8192]{1,0:T(8,128)(2,1)S(1)}, bf16[32,8192]{1,0:T(8,128)(2,1)S(1)}, u32[]{:S(2)}, u32[]{:S(2)}) collective-permute-start(bf16[32,8192]{1,0:T(8,128)(2,1)S(1)} %add_convert_fusion.1), channel_id=1, source_target_pairs={{0,1},{1,8},{8,9},{9,0},{2,3},{3,10},{10,11},{11,2},{4,5},{5,12},{... | collective-permute-start | bytes 1572872 | tf_op jit(solution)/shard_map/ppermute | solution.py:60
  36.6 0.8 collective-permute-start.11
  37.4 8.5 %collective-permute-done.2.p2 = bf16[32,8192]{1,0:T(8,128)(2,1)S(1)} collective-permute-done((bf16[32,8192]{1,0:T(8,128)(2,1)S(1)}, bf16[32,8192]{1,0:T(8,128)(2,1)S(1)}, u32[]{:S(2)}, u32[]{:S(2)}) %collective-permute-start.2) | collective-permute-done | bytes 524320 | tf_op jit(solution)/shard_map/ppermute | solution.py:60
  45.9 0.5 middle_sums.2
  46.4 1.4 %collective-permute-start.4 = (bf16[16,8192]{1,0:T(8,128)(2,1)S(1)}, bf16[16,8192]{1,0:T(8,128)(2,1)S(1)}, u32[]{:S(2)}, u32[]{:S(2)}) collective-permute-start(bf16[16,8192]{1,0:T(8,128)(2,1)S(1)} %get-tuple-element.40), channel_id=1, source_target_pairs={{0,1},{1,8},{8,9},{9,0},{2,3},{3,10},{10,11},{11,2},{4,5},{5,12},{... | collective-permute-start | bytes 786440 | tf_op jit(solution)/shard_map/ppermute | solution.py:60
  47.7 0.7 collective-permute-start.5
  48.5 1.0 collective-permute-done.11.m2
  49.5 0.4 middle_sums.3
  50.0 3.2 %collective-permute-start.13 = (bf16[16,8448]{1,0:T(8,128)(2,1)S(1)}, bf16[16,8448]{1,0:T(8,128)(2,1)S(1)}, u32[]{:S(2)}, u32[]{:S(2)}) collective-permute-start(bf16[16,8448]{1,0:T(8,128)(2,1)S(1)} %get-tuple-element.51), channel_id=1, source_target_pairs={{0,6},{2,0},{4,2},{6,4},{1,7},{3,1},{5,3},{7,5},{8,14},{10,8},{12,... | collective-permute-start | bytes 811016 | tf_op jit(solution)/shard_map/ppermute | solution.py:60
  53.4 1.4 %collective-permute-start.6 = (bf16[8,8192]{1,0:T(8,128)(2,1)S(1)}, bf16[8,8192]{1,0:T(8,128)(2,1)S(1)}, u32[]{:S(2)}, u32[]{:S(2)}) collective-permute-start(bf16[8,8192]{1,0:T(8,128)(2,1)S(1)} %add_convert_fusion.7), channel_id=1, source_target_pairs={{0,1},{1,8},{8,9},{9,0},{2,3},{3,10},{10,11},{11,2},{4,5},{5,12},{... | collective-permute-start | bytes 393224 | tf_op jit(solution)/shard_map/ppermute | solution.py:60
  54.9 0.7 collective-permute-start.7
  55.6 2.2 %collective-permute-done.12.refs_6_.z_below = bf16[16,8448]{1,0:T(8,128)(2,1)S(1)} collective-permute-done((bf16[16,8448]{1,0:T(8,128)(2,1)S(1)}, bf16[16,8448]{1,0:T(8,128)(2,1)S(1)}, u32[]{:S(2)}, u32[]{:S(2)}) %collective-permute-start.12) | collective-permute-done | bytes 270368 | tf_op jit(solution)/shard_map/ppermute | solution.py:60
  58.0 3.4 %collective-permute-start.15 = (bf16[8,8192]{1,0:T(8,128)(2,1)S(1)}, bf16[8,8192]{1,0:T(8,128)(2,1)S(1)}, u32[]{:S(2)}, u32[]{:S(2)}) collective-permute-start(bf16[8,8192]{1,0:T(8,128)(2,1)S(1)} %add_convert_fusion.4), channel_id=1, source_target_pairs={{0,6},{2,0},{4,2},{6,4},{1,7},{3,1},{5,3},{7,5},{8,14},{10,8},{12,... | collective-permute-start | bytes 393224 | tf_op jit(solution)/shard_map/ppermute | solution.py:60
  61.5 2.6 %collective-permute-done.14.refs_8_ = bf16[8,8192]{1,0:T(8,128)(2,1)S(1)} collective-permute-done((bf16[8,8192]{1,0:T(8,128)(2,1)S(1)}, bf16[8,8192]{1,0:T(8,128)(2,1)S(1)}, u32[]{:S(2)}, u32[]{:S(2)}) %collective-permute-start.14) | collective-permute-done | bytes 131104 | tf_op jit(solution)/shard_map/ppermute | solution.py:60
  64.1 1.3 %compressed_beams.1 = bf16[8,16,2048]{2,1,0:T(8,128)(2,1)S(1)} custom-call(f32[16,8192]{1,0:T(8,128)S(1)} %get-tuple-element.39.refs_0_, bf16[16,8192]{1,0:T(8,128)(2,1)S(1)} %collective-permute-done.4.refs_1_, bf16[16,8192]{1,0:T(8,128)(2,1)S(1)} %collective-permute-done.5.refs_2_, bf16[8,8192]{1,0:T(8,128)(2,1)S(1)} %collective-permute-done.6.refs_3_, ...), custom_call_target="tpu_custom_call" | custom-call | tf_op jit(solution)/shard_map/compressed_beams/pallas_call | solution.py:315
  65.4 1.4 %collective-permute-start.16 = (bf16[8,16,2048]{2,1,0:T(8,128)(2,1)S(1)}, bf16[8,16,2048]{2,1,0:T(8,128)(2,1)}, u32[]{:S(2)}, u32[]{:S(2)}) collective-permute-start(bf16[8,16,2048]{2,1,0:T(8,128)(2,1)S(1)} %compressed_beams.1), channel_id=1, source_target_pairs={{0,1},{1,0},{2,3},{3,2},{4,5},{5,4},{6,7},{7,6},{8,9},{9,8},{10,11... | collective-permute-start | bytes 1572872 | tf_op jit(solution)/shard_map/ppermute | solution.py:517
  66.8 14.5 %all_to_all.10.own = bf16[8,16,2048]{2,1,0:T(8,128)(2,1)S(1)} all-to-all(bf16[8,16,2048]{2,1,0:T(8,128)(2,1)S(1)} %compressed_beams.1), channel_id=1, replica_groups=mesh['sub'=8,'y_hi'=2,'z'=4,'y_lo'=2] {'sub'}, dimensions={0} | all-to-all | bytes 1048576 | tf_op jit(solution)/shard_map/all_to_all | solution.py:556
  81.3 4.7 %collective-permute-start.17 = (bf16[8,16,2048]{2,1,0:T(8,128)(2,1)S(1)}, bf16[8,16,2048]{2,1,0:T(8,128)(2,1)}, u32[]{:S(2)}, u32[]{:S(2)}) collective-permute-start(bf16[8,16,2048]{2,1,0:T(8,128)(2,1)S(1)} %all_to_all.10.own), channel_id=1, source_target_pairs={{1,2},{2,1},{3,4},{4,3},{5,6},{6,5},{7,8},{8,7},{9,10},{10,9},{11,... | collective-permute-start | bytes 1572872 | tf_op jit(solution)/shard_map/ppermute | solution.py:523
  86.0 3.5 %all-to-all-start = ((bf16[8,16,2048]{2,1,0:T(8,128)(2,1)}), bf16[8,16,2048]{2,1,0:T(8,128)(2,1)S(1)}, u32[]{:S(2)}, u32[]{:S(2)}) async-start(bf16[8,16,2048]{2,1,0:T(8,128)(2,1)} %collective-permute-done.16), calls=%async_computation | async-start | bytes 1048576 | tf_op jit(solution)/shard_map/all_to_all | solution.py:557
  89.5 0.9 copy-done.1
  90.5 5.3 %merge_tables.1 = (bf16[128,128]{1,0:T(8,128)(2,1)}, bf16[288,256]{1,0:T(8,128)(2,1)}, f32[288,128]{1,0:T(8,128)}, f32[288,128]{1,0:T(8,128)}, f32[288,128]{1,0:T(8,128)}, /*index=5*/f32[288,128]{1,0:T(8,128)}) custom-call(s32[1]{0:T(128)} %bitcast.1.start_ref, f32[16,256]{1,0:T(8,128)S(1)} %get-tuple-element.54.own_ref, ...), custom_call_target="tpu_custom_call" | custom-call | tf_op jit(solution)/shard_map/merge_tables/pallas_call | solution.py:425
  95.8 4.0 %all-to-all-done.near = bf16[8,16,2048]{2,1,0:T(8,128)(2,1)S(1)} async-done(((bf16[8,16,2048]{2,1,0:T(8,128)(2,1)}), bf16[8,16,2048]{2,1,0:T(8,128)(2,1)S(1)}, u32[]{:S(2)}, u32[]{:S(2)}) %all-to-all-start) | async-done | bytes 524320 | tf_op jit(solution)/shard_map/all_to_all | solution.py:557
  99.8 6.0 %merge.1 = f32[64,2,2048]{2,1,0:T(2,128)} custom-call(bf16[8,16,2048]{2,1,0:T(8,128)(2,1)S(1)} %all-to-all-done.near, bf16[8,16,2048]{2,1,0:T(8,128)(2,1)S(1)} %all_to_all.10.own, bf16[8,16,2048]{2,1,0:T(8,128)(2,1)} %collective-permute-done.17.far, bf16[128,128]{1,0:T(8,128)(2,1)} %get-tuple-element.55.first_matrix, ...), custom_call_target="tpu_custom_call" | custom-call | tf_op jit(solution)/shard_map/merge/pallas_call | solution.py:501
  (33 shorter events, 0.9 us)
Async XLA Ops:
  4.1 27.3 %collective-permute-start = (bf16[64,8192]{1,0:T(8,128)(2,1)S(1)}, bf16[64,8192]{1,0:T(8,128)(2,1)S(1)}, u32[]{:S(2)}, u32[]{:S(2)}) collective-permute-start(bf16[64,8192]{1,0:T(8,128)(2,1)S(1)} %get-tuple-element.35), channel_id=1, source_target_pairs={{0,2},{2,4},{4,6},{6,0},{1,3},{3,5},{5,7},{7,1},{8,10},{10,12},{12... | collective-permute-start | bytes 3145736 | tf_op jit(solution)/shard_map/ppermute | solution.py:60
  6.1 25.5 %collective-permute-start.1 = (bf16[64,8192]{1,0:T(8,128)(2,1)S(1)}, bf16[64,8192]{1,0:T(8,128)(2,1)S(1)}, u32[]{:S(2)}, u32[]{:S(2)}) collective-permute-start(bf16[64,8192]{1,0:T(8,128)(2,1)S(1)} %get-tuple-element.36), channel_id=1, source_target_pairs={{0,6},{2,0},{4,2},{6,4},{1,7},{3,1},{5,3},{7,5},{8,14},{10,8},{12,... | collective-permute-start | bytes 3145736 | tf_op jit(solution)/shard_map/ppermute | solution.py:60
  8.3 26.7 %collective-permute-start.8 = (bf16[64,8320]{1,0:T(8,128)(2,1)S(1)}, bf16[64,8320]{1,0:T(8,128)(2,1)S(1)}, u32[]{:S(2)}, u32[]{:S(2)}) collective-permute-start(bf16[64,8320]{1,0:T(8,128)(2,1)S(1)} %get-tuple-element.45), channel_id=1, source_target_pairs={{0,1},{1,8},{8,9},{9,0},{2,3},{3,10},{10,11},{11,2},{4,5},{5,12},{... | collective-permute-start | bytes 3194888 | tf_op jit(solution)/shard_map/ppermute | solution.py:60
  9.6 26.9 %collective-permute-start.9 = (bf16[64,8320]{1,0:T(8,128)(2,1)S(1)}, bf16[64,8320]{1,0:T(8,128)(2,1)S(1)}, u32[]{:S(2)}, u32[]{:S(2)}) collective-permute-start(bf16[64,8320]{1,0:T(8,128)(2,1)S(1)} %get-tuple-element.46), channel_id=1, source_target_pairs={{0,9},{1,0},{8,1},{9,8},{2,11},{3,2},{10,3},{11,10},{4,13},{5,4},{... | collective-permute-start | bytes 3194888 | tf_op jit(solution)/shard_map/ppermute | solution.py:60
  31.5 14.4 %collective-permute-start.2 = (bf16[32,8192]{1,0:T(8,128)(2,1)S(1)}, bf16[32,8192]{1,0:T(8,128)(2,1)S(1)}, u32[]{:S(2)}, u32[]{:S(2)}) collective-permute-start(bf16[32,8192]{1,0:T(8,128)(2,1)S(1)} %add_convert_fusion.3), channel_id=1, source_target_pairs={{0,2},{2,4},{4,6},{6,0},{1,3},{3,5},{5,7},{7,1},{8,10},{10,12},{12... | collective-permute-start | bytes 1572872 | tf_op jit(solution)/shard_map/ppermute | solution.py:60
  31.7 14.2 %collective-permute-start.3 = (bf16[32,8192]{1,0:T(8,128)(2,1)S(1)}, bf16[32,8192]{1,0:T(8,128)(2,1)S(1)}, u32[]{:S(2)}, u32[]{:S(2)}) collective-permute-start(bf16[32,8192]{1,0:T(8,128)(2,1)S(1)} %add_convert_fusion.2), channel_id=1, source_target_pairs={{0,6},{2,0},{4,2},{6,4},{1,7},{3,1},{5,3},{7,5},{8,14},{10,8},{12,... | collective-permute-start | bytes 1572872 | tf_op jit(solution)/shard_map/ppermute | solution.py:60
  35.1 13.3 %collective-permute-start.10 = (bf16[32,8192]{1,0:T(8,128)(2,1)S(1)}, bf16[32,8192]{1,0:T(8,128)(2,1)S(1)}, u32[]{:S(2)}, u32[]{:S(2)}) collective-permute-start(bf16[32,8192]{1,0:T(8,128)(2,1)S(1)} %add_convert_fusion.1), channel_id=1, source_target_pairs={{0,1},{1,8},{8,9},{9,0},{2,3},{3,10},{10,11},{11,2},{4,5},{5,12},{... | collective-permute-start | bytes 1572872 | tf_op jit(solution)/shard_map/ppermute | solution.py:60
  36.6 12.8 %collective-permute-start.11 = (bf16[32,8192]{1,0:T(8,128)(2,1)S(1)}, bf16[32,8192]{1,0:T(8,128)(2,1)S(1)}, u32[]{:S(2)}, u32[]{:S(2)}) collective-permute-start(bf16[32,8192]{1,0:T(8,128)(2,1)S(1)} %add_convert_fusion), channel_id=1, source_target_pairs={{0,9},{1,0},{8,1},{9,8},{2,11},{3,2},{10,3},{11,10},{4,13},{5,4},{... | collective-permute-start | bytes 1572872 | tf_op jit(solution)/shard_map/ppermute | solution.py:60
  46.4 7.0 %collective-permute-start.4 = (bf16[16,8192]{1,0:T(8,128)(2,1)S(1)}, bf16[16,8192]{1,0:T(8,128)(2,1)S(1)}, u32[]{:S(2)}, u32[]{:S(2)}) collective-permute-start(bf16[16,8192]{1,0:T(8,128)(2,1)S(1)} %get-tuple-element.40), channel_id=1, source_target_pairs={{0,1},{1,8},{8,9},{9,0},{2,3},{3,10},{10,11},{11,2},{4,5},{5,12},{... | collective-permute-start | bytes 786440 | tf_op jit(solution)/shard_map/ppermute | solution.py:60
  47.7 7.1 %collective-permute-start.5 = (bf16[16,8192]{1,0:T(8,128)(2,1)S(1)}, bf16[16,8192]{1,0:T(8,128)(2,1)S(1)}, u32[]{:S(2)}, u32[]{:S(2)}) collective-permute-start(bf16[16,8192]{1,0:T(8,128)(2,1)S(1)} %get-tuple-element.41), channel_id=1, source_target_pairs={{0,9},{1,0},{8,1},{9,8},{2,11},{3,2},{10,3},{11,10},{4,13},{5,4},{... | collective-permute-start | bytes 786440 | tf_op jit(solution)/shard_map/ppermute | solution.py:60
  49.9 11.6 %copy-start.4 = (f32[2,16384]{1,0:T(2,128)S(1)}, f32[2,16384]{1,0:T(2,128)}, u32[]{:S(2)}) copy-start(f32[2,16384]{1,0:T(2,128)} %param.9) | copy-start | bytes 393220
  49.9 14.2 %copy-start.2 = (bf16[256,256]{1,0:T(8,128)(2,1)S(1)}, bf16[256,256]{1,0:T(8,128)(2,1)}, u32[]{:S(2)}) copy-start(bf16[256,256]{1,0:T(8,128)(2,1)} %constant.12.clone.refs_10_) | copy-start | bytes 393220
  49.9 14.2 %copy-start.3 = (f32[2,128,128]{2,1,0:T(8,128)S(1)}, f32[2,128,128]{2,1,0:T(8,128)}, u32[]{:S(2)}) copy-start(f32[2,128,128]{2,1,0:T(8,128)} %constant.13.clone.refs_11_) | copy-start | bytes 393220
  50.0 7.9 %collective-permute-start.12 = (bf16[16,8448]{1,0:T(8,128)(2,1)S(1)}, bf16[16,8448]{1,0:T(8,128)(2,1)S(1)}, u32[]{:S(2)}, u32[]{:S(2)}) collective-permute-start(bf16[16,8448]{1,0:T(8,128)(2,1)S(1)} %get-tuple-element.50), channel_id=1, source_target_pairs={{0,2},{2,4},{4,6},{6,0},{1,3},{3,5},{5,7},{7,1},{8,10},{10,12},{12... | collective-permute-start | bytes 811016 | tf_op jit(solution)/shard_map/ppermute | solution.py:60
  50.0 7.9 %collective-permute-start.13 = (bf16[16,8448]{1,0:T(8,128)(2,1)S(1)}, bf16[16,8448]{1,0:T(8,128)(2,1)S(1)}, u32[]{:S(2)}, u32[]{:S(2)}) collective-permute-start(bf16[16,8448]{1,0:T(8,128)(2,1)S(1)} %get-tuple-element.51), channel_id=1, source_target_pairs={{0,6},{2,0},{4,2},{6,4},{1,7},{3,1},{5,3},{7,5},{8,14},{10,8},{12,... | collective-permute-start | bytes 811016 | tf_op jit(solution)/shard_map/ppermute | solution.py:60
  53.4 8.1 %collective-permute-start.6 = (bf16[8,8192]{1,0:T(8,128)(2,1)S(1)}, bf16[8,8192]{1,0:T(8,128)(2,1)S(1)}, u32[]{:S(2)}, u32[]{:S(2)}) collective-permute-start(bf16[8,8192]{1,0:T(8,128)(2,1)S(1)} %add_convert_fusion.7), channel_id=1, source_target_pairs={{0,1},{1,8},{8,9},{9,0},{2,3},{3,10},{10,11},{11,2},{4,5},{5,12},{... | collective-permute-start | bytes 393224 | tf_op jit(solution)/shard_map/ppermute | solution.py:60
  54.9 6.6 %collective-permute-start.7 = (bf16[8,8192]{1,0:T(8,128)(2,1)S(1)}, bf16[8,8192]{1,0:T(8,128)(2,1)S(1)}, u32[]{:S(2)}, u32[]{:S(2)}) collective-permute-start(bf16[8,8192]{1,0:T(8,128)(2,1)S(1)} %add_convert_fusion.6), channel_id=1, source_target_pairs={{0,9},{1,0},{8,1},{9,8},{2,11},{3,2},{10,3},{11,10},{4,13},{5,4},{... | collective-permute-start | bytes 393224 | tf_op jit(solution)/shard_map/ppermute | solution.py:60
  57.9 6.2 %collective-permute-start.14 = (bf16[8,8192]{1,0:T(8,128)(2,1)S(1)}, bf16[8,8192]{1,0:T(8,128)(2,1)S(1)}, u32[]{:S(2)}, u32[]{:S(2)}) collective-permute-start(bf16[8,8192]{1,0:T(8,128)(2,1)S(1)} %add_convert_fusion.5), channel_id=1, source_target_pairs={{0,2},{2,4},{4,6},{6,0},{1,3},{3,5},{5,7},{7,1},{8,10},{10,12},{12... | collective-permute-start | bytes 393224 | tf_op jit(solution)/shard_map/ppermute | solution.py:60
  58.0 7.4 %copy-start = (bf16[16,8448]{1,0:T(8,128)(2,1)}, bf16[16,8448]{1,0:T(8,128)(2,1)S(1)}, u32[]{:S(2)}) copy-start(bf16[16,8448]{1,0:T(8,128)(2,1)S(1)} %collective-permute-done.13.refs_7_.z_above) | copy-start | bytes 811012
  58.0 6.1 %collective-permute-start.15 = (bf16[8,8192]{1,0:T(8,128)(2,1)S(1)}, bf16[8,8192]{1,0:T(8,128)(2,1)S(1)}, u32[]{:S(2)}, u32[]{:S(2)}) collective-permute-start(bf16[8,8192]{1,0:T(8,128)(2,1)S(1)} %add_convert_fusion.4), channel_id=1, source_target_pairs={{0,6},{2,0},{4,2},{6,4},{1,7},{3,1},{5,3},{7,5},{8,14},{10,8},{12,... | collective-permute-start | bytes 393224 | tf_op jit(solution)/shard_map/ppermute | solution.py:60
  65.4 20.6 %collective-permute-start.16 = (bf16[8,16,2048]{2,1,0:T(8,128)(2,1)S(1)}, bf16[8,16,2048]{2,1,0:T(8,128)(2,1)}, u32[]{:S(2)}, u32[]{:S(2)}) collective-permute-start(bf16[8,16,2048]{2,1,0:T(8,128)(2,1)S(1)} %compressed_beams.1), channel_id=1, source_target_pairs={{0,1},{1,0},{2,3},{3,2},{4,5},{5,4},{6,7},{7,6},{8,9},{9,8},{10,11... | collective-permute-start | bytes 1572872 | tf_op jit(solution)/shard_map/ppermute | solution.py:517
  81.3 18.5 %collective-permute-start.17 = (bf16[8,16,2048]{2,1,0:T(8,128)(2,1)S(1)}, bf16[8,16,2048]{2,1,0:T(8,128)(2,1)}, u32[]{:S(2)}, u32[]{:S(2)}) collective-permute-start(bf16[8,16,2048]{2,1,0:T(8,128)(2,1)S(1)} %all_to_all.10.own), channel_id=1, source_target_pairs={{1,2},{2,1},{3,4},{4,3},{5,6},{6,5},{7,8},{8,7},{9,10},{10,9},{11,... | collective-permute-start | bytes 1572872 | tf_op jit(solution)/shard_map/ppermute | solution.py:523
  86.0 13.8 %all-to-all-start = ((bf16[8,16,2048]{2,1,0:T(8,128)(2,1)}), bf16[8,16,2048]{2,1,0:T(8,128)(2,1)S(1)}, u32[]{:S(2)}, u32[]{:S(2)}) async-start(bf16[8,16,2048]{2,1,0:T(8,128)(2,1)} %collective-permute-done.16), calls=%async_computation | async-start | bytes 1048576 | tf_op jit(solution)/shard_map/all_to_all | solution.py:557
  89.5 1.0 copy-start.1

commit v5 on v4

--- a/solution.py
+++ b/solution.py
@@ -22,7 +22,7 @@
 READ = NR // READS
 STEP = 2048
 SLAB = NR // 8
-COLS = 512
+COLS = 1024
 FIELDS = 256
 CARRIED = 128
 SIDE = 144
@@ -228,7 +228,7 @@
 
 
 def middle_kernel(own, p1, m1, p2, m2, plus, minus, q1, q3, keep):
-    tile = 512
+    tile = 1024
 
     def step(k, carry):
         cols = pl.ds(pl.multiple_of(k * tile, tile), tile)

time: 106 us -> 106 us (level)
  no operation moved by 1% of the time
where the time goes in v5:
time: 106 us
  waiting for transfers between devices  32.7 us (31%)
  starting transfers between devices  32.3 us (30%)
  Pallas kernels  24.5 us (23%)
  blocking collectives  14.5 us (14%)
    ppermute x16, waiting for transfers between devices, ring_send(): return lax.ppermute(x, axis, [(k, (k + step) % RING) for k in range(RING)])  28.7 us
    ppermute x16, starting transfers between devices, ring_send(): return lax.ppermute(x, axis, [(k, (k + step) % RING) for k in range(RING)])  22.8 us
    all_to_all x1, blocking collectives, body(): image = lax.all_to_all(beams, 'sub', 0, 0, tiled=True)  14.5 us
    pallas_call x1, Pallas kernels, later_sums(): pl.pallas_call(later_kernel, grid=(READS,), in_specs=[vmem, pl.BlockSpec(...  6.97 us
    pallas_call x1, Pallas kernels, merge(): pl.pallas_call(merge_kernel, grid=(SLAB // COLS,), in_specs=[image] * 3 +...  5.98 us
    pallas_call x1, Pallas kernels, merge_tables(): pl.pallas_call(table_kernel, grid=(1,), in_specs=[pl.BlockSpec(memory_spa...  5.33 us
    ppermute x1, starting transfers between devices, from_far(): return lax.ppermute(array, BEAM_COMP, steps)  4.68 us
    pallas_call x1, Pallas kernels, opening_sums(): pl.pallas_call(opening_kernel, in_specs=[pl.BlockSpec(memory_space=pltpu....  4.1 us
  transfers between devices with their start and end apart: 19, of which 7 were waited for; matrix products, arithmetic and copies ran while one was open for 1% of the time, Pallas kernels for 12%

profile of v5, /device:TPU:16, one launch (start us, length us, event | category | flops | bytes accessed | tf_op | source)
XLA Modules:
  0.0 105.8 jit_solution(14798677759275897342)
XLA Ops:
  0.0 4.1 %opening_sums.1 = (bf16[64,8192]{1,0:T(8,128)(2,1)S(1)}, bf16[64,8192]{1,0:T(8,128)(2,1)S(1)}, bf16[64,8320]{1,0:T(8,128)(2,1)S(1)}, bf16[64,8320]{1,0:T(8,128)(...) custom-call(f32[128,128]{1,0:T(8,128)} %angle_ref.1, s32[2,112]{1,0:T(2,128)} %offset_ref.1, ...), custom_call_target="tpu_custom_call" | custom-call | tf_op jit(solution)/shard_map/opening_sums/pallas_call | solution.py:180
  4.1 2.0 %collective-permute-start = (bf16[64,8192]{1,0:T(8,128)(2,1)S(1)}, bf16[64,8192]{1,0:T(8,128)(2,1)S(1)}, u32[]{:S(2)}, u32[]{:S(2)}) collective-permute-start(bf16[64,8192]{1,0:T(8,128)(2,1)S(1)} %get-tuple-element.35), channel_id=1, source_target_pairs={{0,2},{2,4},{4,6},{6,0},{1,3},{3,5},{5,7},{7,1},{8,10},{10,12},{12... | collective-permute-start | bytes 3145736 | tf_op jit(solution)/shard_map/ppermute | solution.py:60
  6.1 2.2 %collective-permute-start.1 = (bf16[64,8192]{1,0:T(8,128)(2,1)S(1)}, bf16[64,8192]{1,0:T(8,128)(2,1)S(1)}, u32[]{:S(2)}, u32[]{:S(2)}) collective-permute-start(bf16[64,8192]{1,0:T(8,128)(2,1)S(1)} %get-tuple-element.36), channel_id=1, source_target_pairs={{0,6},{2,0},{4,2},{6,4},{1,7},{3,1},{5,3},{7,5},{8,14},{10,8},{12,... | collective-permute-start | bytes 3145736 | tf_op jit(solution)/shard_map/ppermute | solution.py:60
  8.3 1.3 %collective-permute-start.8 = (bf16[64,8320]{1,0:T(8,128)(2,1)S(1)}, bf16[64,8320]{1,0:T(8,128)(2,1)S(1)}, u32[]{:S(2)}, u32[]{:S(2)}) collective-permute-start(bf16[64,8320]{1,0:T(8,128)(2,1)S(1)} %get-tuple-element.45), channel_id=1, source_target_pairs={{0,1},{1,8},{8,9},{9,0},{2,3},{3,10},{10,11},{11,2},{4,5},{5,12},{... | collective-permute-start | bytes 3194888 | tf_op jit(solution)/shard_map/ppermute | solution.py:60
  9.6 0.7 collective-permute-start.9
  10.3 7.0 %later_sums.1 = (bf16[32,8192]{1,0:T(8,128)(2,1)S(1)}, bf16[32,8192]{1,0:T(8,128)(2,1)S(1)}, bf16[64,8192]{1,0:T(8,128)(2,1)S(1)}, bf16[32,8192]{1,0:T(8,128)(2,...) custom-call(f32[2,128,256]{2,1,0:T(8,128)S(1)} %get-tuple-element.33.weights, ...), custom_call_target="tpu_custom_call" | custom-call | tf_op jit(solution)/shard_map/later_sums/pallas_call | solution.py:213
  17.3 14.1 %collective-permute-done.p1 = bf16[64,8192]{1,0:T(8,128)(2,1)S(1)} collective-permute-done((bf16[64,8192]{1,0:T(8,128)(2,1)S(1)}, bf16[64,8192]{1,0:T(8,128)(2,1)S(1)}, u32[]{:S(2)}, u32[]{:S(2)}) %collective-permute-start) | collective-permute-done | bytes 1048608 | tf_op jit(solution)/shard_map/ppermute | solution.py:60
  31.6 0.1 add_convert_fusion.2
  31.7 3.3 %collective-permute-start.3 = (bf16[32,8192]{1,0:T(8,128)(2,1)S(1)}, bf16[32,8192]{1,0:T(8,128)(2,1)S(1)}, u32[]{:S(2)}, u32[]{:S(2)}) collective-permute-start(bf16[32,8192]{1,0:T(8,128)(2,1)S(1)} %add_convert_fusion.2), channel_id=1, source_target_pairs={{0,6},{2,0},{4,2},{6,4},{1,7},{3,1},{5,3},{7,5},{8,14},{10,8},{12,... | collective-permute-start | bytes 1572872 | tf_op jit(solution)/shard_map/ppermute | solution.py:60
  35.1 1.4 %collective-permute-start.10 = (bf16[32,8192]{1,0:T(8,128)(2,1)S(1)}, bf16[32,8192]{1,0:T(8,128)(2,1)S(1)}, u32[]{:S(2)}, u32[]{:S(2)}) collective-permute-start(bf16[32,8192]{1,0:T(8,128)(2,1)S(1)} %add_convert_fusion.1), channel_id=1, source_target_pairs={{0,1},{1,8},{8,9},{9,0},{2,3},{3,10},{10,11},{11,2},{4,5},{5,12},{... | collective-permute-start | bytes 1572872 | tf_op jit(solution)/shard_map/ppermute | solution.py:60
  36.6 0.8 collective-permute-start.11
  37.4 8.5 %collective-permute-done.2.p2 = bf16[32,8192]{1,0:T(8,128)(2,1)S(1)} collective-permute-done((bf16[32,8192]{1,0:T(8,128)(2,1)S(1)}, bf16[32,8192]{1,0:T(8,128)(2,1)S(1)}, u32[]{:S(2)}, u32[]{:S(2)}) %collective-permute-start.2) | collective-permute-done | bytes 524320 | tf_op jit(solution)/shard_map/ppermute | solution.py:60
  45.9 0.4 middle_sums.2
  46.3 1.4 %collective-permute-start.4 = (bf16[16,8192]{1,0:T(8,128)(2,1)S(1)}, bf16[16,8192]{1,0:T(8,128)(2,1)S(1)}, u32[]{:S(2)}, u32[]{:S(2)}) collective-permute-start(bf16[16,8192]{1,0:T(8,128)(2,1)S(1)} %get-tuple-element.40), channel_id=1, source_target_pairs={{0,1},{1,8},{8,9},{9,0},{2,3},{3,10},{10,11},{11,2},{4,5},{5,12},{... | collective-permute-start | bytes 786440 | tf_op jit(solution)/shard_map/ppermute | solution.py:60
  47.7 0.7 collective-permute-start.5
  48.4 1.1 %collective-permute-done.11.m2 = bf16[32,8192]{1,0:T(8,128)(2,1)S(1)} collective-permute-done((bf16[32,8192]{1,0:T(8,128)(2,1)S(1)}, bf16[32,8192]{1,0:T(8,128)(2,1)S(1)}, u32[]{:S(2)}, u32[]{:S(2)}) %collective-permute-start.11) | collective-permute-done | bytes 524320 | tf_op jit(solution)/shard_map/ppermute | solution.py:60
  49.5 0.4 middle_sums.3
  50.0 3.2 %collective-permute-start.13 = (bf16[16,8448]{1,0:T(8,128)(2,1)S(1)}, bf16[16,8448]{1,0:T(8,128)(2,1)S(1)}, u32[]{:S(2)}, u32[]{:S(2)}) collective-permute-start(bf16[16,8448]{1,0:T(8,128)(2,1)S(1)} %get-tuple-element.51), channel_id=1, source_target_pairs={{0,6},{2,0},{4,2},{6,4},{1,7},{3,1},{5,3},{7,5},{8,14},{10,8},{12,... | collective-permute-start | bytes 811016 | tf_op jit(solution)/shard_map/ppermute | solution.py:60
  53.4 1.4 %collective-permute-start.6 = (bf16[8,8192]{1,0:T(8,128)(2,1)S(1)}, bf16[8,8192]{1,0:T(8,128)(2,1)S(1)}, u32[]{:S(2)}, u32[]{:S(2)}) collective-permute-start(bf16[8,8192]{1,0:T(8,128)(2,1)S(1)} %add_convert_fusion.7), channel_id=1, source_target_pairs={{0,1},{1,8},{8,9},{9,0},{2,3},{3,10},{10,11},{11,2},{4,5},{5,12},{... | collective-permute-start | bytes 393224 | tf_op jit(solution)/shard_map/ppermute | solution.py:60
  54.9 0.7 collective-permute-start.7
  55.6 2.3 %collective-permute-done.12.refs_6_.z_below = bf16[16,8448]{1,0:T(8,128)(2,1)S(1)} collective-permute-done((bf16[16,8448]{1,0:T(8,128)(2,1)S(1)}, bf16[16,8448]{1,0:T(8,128)(2,1)S(1)}, u32[]{:S(2)}, u32[]{:S(2)}) %collective-permute-start.12) | collective-permute-done | bytes 270368 | tf_op jit(solution)/shard_map/ppermute | solution.py:60
  58.1 3.4 %collective-permute-start.15 = (bf16[8,8192]{1,0:T(8,128)(2,1)S(1)}, bf16[8,8192]{1,0:T(8,128)(2,1)S(1)}, u32[]{:S(2)}, u32[]{:S(2)}) collective-permute-start(bf16[8,8192]{1,0:T(8,128)(2,1)S(1)} %add_convert_fusion.4), channel_id=1, source_target_pairs={{0,6},{2,0},{4,2},{6,4},{1,7},{3,1},{5,3},{7,5},{8,14},{10,8},{12,... | collective-permute-start | bytes 393224 | tf_op jit(solution)/shard_map/ppermute | solution.py:60
  61.6 2.6 %collective-permute-done.14.refs_8_ = bf16[8,8192]{1,0:T(8,128)(2,1)S(1)} collective-permute-done((bf16[8,8192]{1,0:T(8,128)(2,1)S(1)}, bf16[8,8192]{1,0:T(8,128)(2,1)S(1)}, u32[]{:S(2)}, u32[]{:S(2)}) %collective-permute-start.14) | collective-permute-done | bytes 131104 | tf_op jit(solution)/shard_map/ppermute | solution.py:60
  64.2 1.3 %compressed_beams.1 = bf16[8,16,2048]{2,1,0:T(8,128)(2,1)S(1)} custom-call(f32[16,8192]{1,0:T(8,128)S(1)} %get-tuple-element.39.refs_0_, bf16[16,8192]{1,0:T(8,128)(2,1)S(1)} %collective-permute-done.4.refs_1_, bf16[16,8192]{1,0:T(8,128)(2,1)S(1)} %collective-permute-done.5.refs_2_, bf16[8,8192]{1,0:T(8,128)(2,1)S(1)} %collective-permute-done.6.refs_3_, ...), custom_call_target="tpu_custom_call" | custom-call | tf_op jit(solution)/shard_map/compressed_beams/pallas_call | solution.py:315
  65.5 1.3 %collective-permute-start.16 = (bf16[8,16,2048]{2,1,0:T(8,128)(2,1)S(1)}, bf16[8,16,2048]{2,1,0:T(8,128)(2,1)}, u32[]{:S(2)}, u32[]{:S(2)}) collective-permute-start(bf16[8,16,2048]{2,1,0:T(8,128)(2,1)S(1)} %compressed_beams.1), channel_id=1, source_target_pairs={{0,1},{1,0},{2,3},{3,2},{4,5},{5,4},{6,7},{7,6},{8,9},{9,8},{10,11... | collective-permute-start | bytes 1572872 | tf_op jit(solution)/shard_map/ppermute | solution.py:517
  66.8 14.5 %all_to_all.10.own = bf16[8,16,2048]{2,1,0:T(8,128)(2,1)S(1)} all-to-all(bf16[8,16,2048]{2,1,0:T(8,128)(2,1)S(1)} %compressed_beams.1), channel_id=1, replica_groups=mesh['sub'=8,'y_hi'=2,'z'=4,'y_lo'=2] {'sub'}, dimensions={0} | all-to-all | bytes 1048576 | tf_op jit(solution)/shard_map/all_to_all | solution.py:556
  81.3 4.7 %collective-permute-start.17 = (bf16[8,16,2048]{2,1,0:T(8,128)(2,1)S(1)}, bf16[8,16,2048]{2,1,0:T(8,128)(2,1)}, u32[]{:S(2)}, u32[]{:S(2)}) collective-permute-start(bf16[8,16,2048]{2,1,0:T(8,128)(2,1)S(1)} %all_to_all.10.own), channel_id=1, source_target_pairs={{1,2},{2,1},{3,4},{4,3},{5,6},{6,5},{7,8},{8,7},{9,10},{10,9},{11,... | collective-permute-start | bytes 1572872 | tf_op jit(solution)/shard_map/ppermute | solution.py:523
  86.0 3.5 %all-to-all-start = ((bf16[8,16,2048]{2,1,0:T(8,128)(2,1)}), bf16[8,16,2048]{2,1,0:T(8,128)(2,1)S(1)}, u32[]{:S(2)}, u32[]{:S(2)}) async-start(bf16[8,16,2048]{2,1,0:T(8,128)(2,1)} %collective-permute-done.16), calls=%async_computation | async-start | bytes 1048576 | tf_op jit(solution)/shard_map/all_to_all | solution.py:557
  89.5 0.9 copy-done.1
  90.5 5.3 %merge_tables.1 = (bf16[128,128]{1,0:T(8,128)(2,1)}, bf16[288,256]{1,0:T(8,128)(2,1)}, f32[288,128]{1,0:T(8,128)}, f32[288,128]{1,0:T(8,128)}, f32[288,128]{1,0:T(8,128)}, /*index=5*/f32[288,128]{1,0:T(8,128)}) custom-call(s32[1]{0:T(128)} %bitcast.1.start_ref, f32[16,256]{1,0:T(8,128)S(1)} %get-tuple-element.54.own_ref, ...), custom_call_target="tpu_custom_call" | custom-call | tf_op jit(solution)/shard_map/merge_tables/pallas_call | solution.py:425
  95.8 4.0 %all-to-all-done.near = bf16[8,16,2048]{2,1,0:T(8,128)(2,1)S(1)} async-done(((bf16[8,16,2048]{2,1,0:T(8,128)(2,1)}), bf16[8,16,2048]{2,1,0:T(8,128)(2,1)S(1)}, u32[]{:S(2)}, u32[]{:S(2)}) %all-to-all-start) | async-done | bytes 524320 | tf_op jit(solution)/shard_map/all_to_all | solution.py:557
  99.8 6.0 %merge.1 = f32[64,2,2048]{2,1,0:T(2,128)} custom-call(bf16[8,16,2048]{2,1,0:T(8,128)(2,1)S(1)} %all-to-all-done.near, bf16[8,16,2048]{2,1,0:T(8,128)(2,1)S(1)} %all_to_all.10.own, bf16[8,16,2048]{2,1,0:T(8,128)(2,1)} %collective-permute-done.17.far, bf16[128,128]{1,0:T(8,128)(2,1)} %get-tuple-element.55.first_matrix, ...), custom_call_target="tpu_custom_call" | custom-call | tf_op jit(solution)/shard_map/merge/pallas_call | solution.py:501
  (33 shorter events, 0.9 us)
Async XLA Ops:
  4.1 27.3 %collective-permute-start = (bf16[64,8192]{1,0:T(8,128)(2,1)S(1)}, bf16[64,8192]{1,0:T(8,128)(2,1)S(1)}, u32[]{:S(2)}, u32[]{:S(2)}) collective-permute-start(bf16[64,8192]{1,0:T(8,128)(2,1)S(1)} %get-tuple-element.35), channel_id=1, source_target_pairs={{0,2},{2,4},{4,6},{6,0},{1,3},{3,5},{5,7},{7,1},{8,10},{10,12},{12... | collective-permute-start | bytes 3145736 | tf_op jit(solution)/shard_map/ppermute | solution.py:60
  6.1 25.5 %collective-permute-start.1 = (bf16[64,8192]{1,0:T(8,128)(2,1)S(1)}, bf16[64,8192]{1,0:T(8,128)(2,1)S(1)}, u32[]{:S(2)}, u32[]{:S(2)}) collective-permute-start(bf16[64,8192]{1,0:T(8,128)(2,1)S(1)} %get-tuple-element.36), channel_id=1, source_target_pairs={{0,6},{2,0},{4,2},{6,4},{1,7},{3,1},{5,3},{7,5},{8,14},{10,8},{12,... | collective-permute-start | bytes 3145736 | tf_op jit(solution)/shard_map/ppermute | solution.py:60
  8.3 26.7 %collective-permute-start.8 = (bf16[64,8320]{1,0:T(8,128)(2,1)S(1)}, bf16[64,8320]{1,0:T(8,128)(2,1)S(1)}, u32[]{:S(2)}, u32[]{:S(2)}) collective-permute-start(bf16[64,8320]{1,0:T(8,128)(2,1)S(1)} %get-tuple-element.45), channel_id=1, source_target_pairs={{0,1},{1,8},{8,9},{9,0},{2,3},{3,10},{10,11},{11,2},{4,5},{5,12},{... | collective-permute-start | bytes 3194888 | tf_op jit(solution)/shard_map/ppermute | solution.py:60
  9.6 26.9 %collective-permute-start.9 = (bf16[64,8320]{1,0:T(8,128)(2,1)S(1)}, bf16[64,8320]{1,0:T(8,128)(2,1)S(1)}, u32[]{:S(2)}, u32[]{:S(2)}) collective-permute-start(bf16[64,8320]{1,0:T(8,128)(2,1)S(1)} %get-tuple-element.46), channel_id=1, source_target_pairs={{0,9},{1,0},{8,1},{9,8},{2,11},{3,2},{10,3},{11,10},{4,13},{5,4},{... | collective-permute-start | bytes 3194888 | tf_op jit(solution)/shard_map/ppermute | solution.py:60
  31.5 14.4 %collective-permute-start.2 = (bf16[32,8192]{1,0:T(8,128)(2,1)S(1)}, bf16[32,8192]{1,0:T(8,128)(2,1)S(1)}, u32[]{:S(2)}, u32[]{:S(2)}) collective-permute-start(bf16[32,8192]{1,0:T(8,128)(2,1)S(1)} %add_convert_fusion.3), channel_id=1, source_target_pairs={{0,2},{2,4},{4,6},{6,0},{1,3},{3,5},{5,7},{7,1},{8,10},{10,12},{12... | collective-permute-start | bytes 1572872 | tf_op jit(solution)/shard_map/ppermute | solution.py:60
  31.7 14.2 %collective-permute-start.3 = (bf16[32,8192]{1,0:T(8,128)(2,1)S(1)}, bf16[32,8192]{1,0:T(8,128)(2,1)S(1)}, u32[]{:S(2)}, u32[]{:S(2)}) collective-permute-start(bf16[32,8192]{1,0:T(8,128)(2,1)S(1)} %add_convert_fusion.2), channel_id=1, source_target_pairs={{0,6},{2,0},{4,2},{6,4},{1,7},{3,1},{5,3},{7,5},{8,14},{10,8},{12,... | collective-permute-start | bytes 1572872 | tf_op jit(solution)/shard_map/ppermute | solution.py:60
  35.1 13.3 %collective-permute-start.10 = (bf16[32,8192]{1,0:T(8,128)(2,1)S(1)}, bf16[32,8192]{1,0:T(8,128)(2,1)S(1)}, u32[]{:S(2)}, u32[]{:S(2)}) collective-permute-start(bf16[32,8192]{1,0:T(8,128)(2,1)S(1)} %add_convert_fusion.1), channel_id=1, source_target_pairs={{0,1},{1,8},{8,9},{9,0},{2,3},{3,10},{10,11},{11,2},{4,5},{5,12},{... | collective-permute-start | bytes 1572872 | tf_op jit(solution)/shard_map/ppermute | solution.py:60
  36.6 12.9 %collective-permute-start.11 = (bf16[32,8192]{1,0:T(8,128)(2,1)S(1)}, bf16[32,8192]{1,0:T(8,128)(2,1)S(1)}, u32[]{:S(2)}, u32[]{:S(2)}) collective-permute-start(bf16[32,8192]{1,0:T(8,128)(2,1)S(1)} %add_convert_fusion), channel_id=1, source_target_pairs={{0,9},{1,0},{8,1},{9,8},{2,11},{3,2},{10,3},{11,10},{4,13},{5,4},{... | collective-permute-start | bytes 1572872 | tf_op jit(solution)/shard_map/ppermute | solution.py:60
  46.3 7.1 %collective-permute-start.4 = (bf16[16,8192]{1,0:T(8,128)(2,1)S(1)}, bf16[16,8192]{1,0:T(8,128)(2,1)S(1)}, u32[]{:S(2)}, u32[]{:S(2)}) collective-permute-start(bf16[16,8192]{1,0:T(8,128)(2,1)S(1)} %get-tuple-element.40), channel_id=1, source_target_pairs={{0,1},{1,8},{8,9},{9,0},{2,3},{3,10},{10,11},{11,2},{4,5},{5,12},{... | collective-permute-start | bytes 786440 | tf_op jit(solution)/shard_map/ppermute | solution.py:60
  47.7 7.2 %collective-permute-start.5 = (bf16[16,8192]{1,0:T(8,128)(2,1)S(1)}, bf16[16,8192]{1,0:T(8,128)(2,1)S(1)}, u32[]{:S(2)}, u32[]{:S(2)}) collective-permute-start(bf16[16,8192]{1,0:T(8,128)(2,1)S(1)} %get-tuple-element.41), channel_id=1, source_target_pairs={{0,9},{1,0},{8,1},{9,8},{2,11},{3,2},{10,3},{11,10},{4,13},{5,4},{... | collective-permute-start | bytes 786440 | tf_op jit(solution)/shard_map/ppermute | solution.py:60
  49.9 11.6 %copy-start.4 = (f32[2,16384]{1,0:T(2,128)S(1)}, f32[2,16384]{1,0:T(2,128)}, u32[]{:S(2)}) copy-start(f32[2,16384]{1,0:T(2,128)} %param.9) | copy-start | bytes 393220
  49.9 14.3 %copy-start.2 = (bf16[256,256]{1,0:T(8,128)(2,1)S(1)}, bf16[256,256]{1,0:T(8,128)(2,1)}, u32[]{:S(2)}) copy-start(bf16[256,256]{1,0:T(8,128)(2,1)} %constant.12.clone.refs_10_) | copy-start | bytes 393220
  49.9 14.3 %copy-start.3 = (f32[2,128,128]{2,1,0:T(8,128)S(1)}, f32[2,128,128]{2,1,0:T(8,128)}, u32[]{:S(2)}) copy-start(f32[2,128,128]{2,1,0:T(8,128)} %constant.13.clone.refs_11_) | copy-start | bytes 393220
  50.0 7.9 %collective-permute-start.12 = (bf16[16,8448]{1,0:T(8,128)(2,1)S(1)}, bf16[16,8448]{1,0:T(8,128)(2,1)S(1)}, u32[]{:S(2)}, u32[]{:S(2)}) collective-permute-start(bf16[16,8448]{1,0:T(8,128)(2,1)S(1)} %get-tuple-element.50), channel_id=1, source_target_pairs={{0,2},{2,4},{4,6},{6,0},{1,3},{3,5},{5,7},{7,1},{8,10},{10,12},{12... | collective-permute-start | bytes 811016 | tf_op jit(solution)/shard_map/ppermute | solution.py:60
  50.0 8.0 %collective-permute-start.13 = (bf16[16,8448]{1,0:T(8,128)(2,1)S(1)}, bf16[16,8448]{1,0:T(8,128)(2,1)S(1)}, u32[]{:S(2)}, u32[]{:S(2)}) collective-permute-start(bf16[16,8448]{1,0:T(8,128)(2,1)S(1)} %get-tuple-element.51), channel_id=1, source_target_pairs={{0,6},{2,0},{4,2},{6,4},{1,7},{3,1},{5,3},{7,5},{8,14},{10,8},{12,... | collective-permute-start | bytes 811016 | tf_op jit(solution)/shard_map/ppermute | solution.py:60
  53.4 8.2 %collective-permute-start.6 = (bf16[8,8192]{1,0:T(8,128)(2,1)S(1)}, bf16[8,8192]{1,0:T(8,128)(2,1)S(1)}, u32[]{:S(2)}, u32[]{:S(2)}) collective-permute-start(bf16[8,8192]{1,0:T(8,128)(2,1)S(1)} %add_convert_fusion.7), channel_id=1, source_target_pairs={{0,1},{1,8},{8,9},{9,0},{2,3},{3,10},{10,11},{11,2},{4,5},{5,12},{... | collective-permute-start | bytes 393224 | tf_op jit(solution)/shard_map/ppermute | solution.py:60
  54.9 6.7 %collective-permute-start.7 = (bf16[8,8192]{1,0:T(8,128)(2,1)S(1)}, bf16[8,8192]{1,0:T(8,128)(2,1)S(1)}, u32[]{:S(2)}, u32[]{:S(2)}) collective-permute-start(bf16[8,8192]{1,0:T(8,128)(2,1)S(1)} %add_convert_fusion.6), channel_id=1, source_target_pairs={{0,9},{1,0},{8,1},{9,8},{2,11},{3,2},{10,3},{11,10},{4,13},{5,4},{... | collective-permute-start | bytes 393224 | tf_op jit(solution)/shard_map/ppermute | solution.py:60
  57.9 6.2 %collective-permute-start.14 = (bf16[8,8192]{1,0:T(8,128)(2,1)S(1)}, bf16[8,8192]{1,0:T(8,128)(2,1)S(1)}, u32[]{:S(2)}, u32[]{:S(2)}) collective-permute-start(bf16[8,8192]{1,0:T(8,128)(2,1)S(1)} %add_convert_fusion.5), channel_id=1, source_target_pairs={{0,2},{2,4},{4,6},{6,0},{1,3},{3,5},{5,7},{7,1},{8,10},{10,12},{12... | collective-permute-start | bytes 393224 | tf_op jit(solution)/shard_map/ppermute | solution.py:60
  58.0 7.4 %copy-start = (bf16[16,8448]{1,0:T(8,128)(2,1)}, bf16[16,8448]{1,0:T(8,128)(2,1)S(1)}, u32[]{:S(2)}) copy-start(bf16[16,8448]{1,0:T(8,128)(2,1)S(1)} %collective-permute-done.13.refs_7_.z_above) | copy-start | bytes 811012
  58.1 6.1 %collective-permute-start.15 = (bf16[8,8192]{1,0:T(8,128)(2,1)S(1)}, bf16[8,8192]{1,0:T(8,128)(2,1)S(1)}, u32[]{:S(2)}, u32[]{:S(2)}) collective-permute-start(bf16[8,8192]{1,0:T(8,128)(2,1)S(1)} %add_convert_fusion.4), channel_id=1, source_target_pairs={{0,6},{2,0},{4,2},{6,4},{1,7},{3,1},{5,3},{7,5},{8,14},{10,8},{12,... | collective-permute-start | bytes 393224 | tf_op jit(solution)/shard_map/ppermute | solution.py:60
  65.5 20.5 %collective-permute-start.16 = (bf16[8,16,2048]{2,1,0:T(8,128)(2,1)S(1)}, bf16[8,16,2048]{2,1,0:T(8,128)(2,1)}, u32[]{:S(2)}, u32[]{:S(2)}) collective-permute-start(bf16[8,16,2048]{2,1,0:T(8,128)(2,1)S(1)} %compressed_beams.1), channel_id=1, source_target_pairs={{0,1},{1,0},{2,3},{3,2},{4,5},{5,4},{6,7},{7,6},{8,9},{9,8},{10,11... | collective-permute-start | bytes 1572872 | tf_op jit(solution)/shard_map/ppermute | solution.py:517
  81.3 18.5 %collective-permute-start.17 = (bf16[8,16,2048]{2,1,0:T(8,128)(2,1)S(1)}, bf16[8,16,2048]{2,1,0:T(8,128)(2,1)}, u32[]{:S(2)}, u32[]{:S(2)}) collective-permute-start(bf16[8,16,2048]{2,1,0:T(8,128)(2,1)S(1)} %all_to_all.10.own), channel_id=1, source_target_pairs={{1,2},{2,1},{3,4},{4,3},{5,6},{6,5},{7,8},{8,7},{9,10},{10,9},{11,... | collective-permute-start | bytes 1572872 | tf_op jit(solution)/shard_map/ppermute | solution.py:523
  86.0 13.8 %all-to-all-start = ((bf16[8,16,2048]{2,1,0:T(8,128)(2,1)}), bf16[8,16,2048]{2,1,0:T(8,128)(2,1)S(1)}, u32[]{:S(2)}, u32[]{:S(2)}) async-start(bf16[8,16,2048]{2,1,0:T(8,128)(2,1)} %collective-permute-done.16), calls=%async_computation | async-start | bytes 1048576 | tf_op jit(solution)/shard_map/all_to_all | solution.py:557
  89.5 1.0 copy-start.1
